TPU v7x, 32 devices: a whole 2x2x4 slice. The times are simulated.
32 devices in a mesh: row: 4 (over x, core), col: 8 (over z, y).
Axes of the slice: x: 2, y: 2, z: 4, core: 2. Of those that a mesh axis runs over, the one named last changes fastest.
Arguments:
- block_input: bfloat16 [8, 1024, 1024], P('col', 'row'), may hold values from -6 to 6
- state_start: bfloat16 [8, 512, 1024], P('col'), may hold values from -6 to 6
- teacher: bfloat16 [8, 1024, 1024], P('col', 'row'), may hold values from -6 to 6
- valid_mask: int32 [8, 1024], replicated, may hold values 0 or 1
- segment: int32 [8, 1024], P('col'), may hold values from 0 to 3, never falling along the last dimension, each value on 1 to 512 neighbouring positions
- image_offset: int32 [8, 2], P('col'), may hold values from 0 to 256
- retain: float32 [1024], replicated, may hold values from 0.55 to 0.995
- to_query: bfloat16 [1024, 1024], P('col', 'row'), may hold values from -0.1875 to 0.1875
- to_key: bfloat16 [1024, 1024], P('col', 'row'), may hold values from -0.1875 to 0.1875
- to_value: bfloat16 [1024, 1024], P('col', 'row'), may hold values from -0.1875 to 0.1875
- to_output: bfloat16 [1024, 1024], P('row', 'col'), may hold values from -4 to 4
- to_hidden: bfloat16 [1024, 4096], P('col'), may hold values from -0.1875 to 0.1875
- to_model: bfloat16 [4096, 1024], P(None, 'col'), may hold values from -0.09375 to 0.09375
- state_query: bfloat16 [1024, 1024], P('col', 'row'), may hold values from -0.1875 to 0.1875
- state_key: bfloat16 [1024, 1024], P('col', 'row'), may hold values from -0.1875 to 0.1875
- state_value: bfloat16 [1024, 1024], P('col', 'row'), may hold values from -0.1875 to 0.1875
- state_write: bfloat16 [1024, 1024], P(None, 'col'), may hold values from -4 to 4
- first_gain: float32 [1024], replicated, may hold values from 0.5 to 1.5
- second_gain: float32 [1024], replicated, may hold values from 0.5 to 1.5
- state_gain: float32 [1024], replicated, may hold values from 0.5 to 1.5
Outputs:
- total_loss: float32 [], replicated
- final_state: float32 [8, 512, 1024], P('col')
- input_grad: float32 [8, 1024, 1024], P('col', 'row')
- state_grad: float32 [8, 512, 1024], P('col')
- query_grad: float32 [1024, 1024], P('col', 'row')
- key_grad: float32 [1024, 1024], P('col', 'row')
- value_grad: float32 [1024, 1024], P('col', 'row')
- output_grad: float32 [1024, 1024], P('row', 'col')
- hidden_grad: float32 [1024, 4096], P('col', 'row')
- model_grad: float32 [4096, 1024], P('row', 'col')
- state_query_grad: float32 [1024, 1024], P('col', 'row')
- state_key_grad: float32 [1024, 1024], P('col', 'row')
- state_value_grad: float32 [1024, 1024], P('col', 'row')
- state_write_grad: float32 [1024, 1024], P('row', 'col')
- first_gain_grad: float32 [1024], replicated
- second_gain_grad: float32 [1024], replicated
- state_gain_grad: float32 [1024], replicated
Inputs may be any that keep to these rules, and one draw needn't show every extreme that they name: `image_offset`: each block's image piece starts at this offset from the block's first token and ends inside the block. `segment`: document numbers never fall along a sequence; every one of the 4 numbers appears in each sequence.
All inputs are finite; a program needn't handle non-finite values.
Results may differ from a plain program's by a relative error of at most 0.02.
Values may be sent and summed in bfloat16 or wider, within the bound.
No kernel may reach another device: no remote copies, remote signals or barrier semaphores. Data moves between devices by JAX's collectives and lax.ppermute only.
A program may use at most 192 MiB of HBM per device.

v0:
```python
import functools

import jax
import jax.numpy as jnp
from jax import lax
from jax.experimental import pallas as pl
from jax.experimental.pallas import tpu as pltpu
from jax.sharding import PartitionSpec as P

HEAD = 128
BLOCK = 512
HALF = 256
NS = 512
PIECE = 256
COST = 8
TILE = 256

epsilon = 1e-06
masked_value = -1e30
score_scale = HEAD ** (-0.5)
log2_scale = score_scale * 1.4426950408889634
f32 = jnp.float32
bf16 = jnp.bfloat16


def dot_nn(a, b):
    return lax.dot_general(a, b, (((1,), (0,)), ((), ())), preferred_element_type=f32)


def dot_nt(a, b):
    return lax.dot_general(a, b, (((1,), (1,)), ((), ())), preferred_element_type=f32)


def dot_tn(a, b):
    return lax.dot_general(a, b, (((0,), (0,)), ((), ())), preferred_element_type=f32)


def cost(flops, arrays):
    return pl.CostEstimate(flops=flops // COST, bytes_accessed=1024, transcendentals=0)


def after(x, *earlier):
    return lax.optimization_barrier((x,) + earlier)[0]


def shaped(shape, dtype):
    return jax.ShapeDtypeStruct(shape, dtype)


def launch(body, idx, inputs, outputs, scratch=(), flops=0, vmem=12, name=None):
    return pl.pallas_call(
        body,
        in_specs=[pl.BlockSpec(memory_space=pltpu.SMEM)]
        + [pl.BlockSpec(memory_space=pltpu.VMEM)] * len(inputs),
        out_specs=[pl.BlockSpec(memory_space=pltpu.VMEM)] * len(outputs),
        out_shape=list(outputs),
        scratch_shapes=list(scratch),
        compiler_params=pltpu.CompilerParams(vmem_limit_bytes=vmem << 20),
        cost_estimate=cost(flops, inputs),
        name=name,
    )(idx, *inputs)


def rows_of(i, base=0, size=HALF):
    return pl.ds(pl.multiple_of(base + i * size, size), size)


def tile_start(i, s):
    steps = HALF // TILE
    return lax.rem(i // steps + s[1], 2) * HALF + lax.rem(i, steps) * TILE


def span(start, base=0):
    return pl.ds(pl.multiple_of(base + start, TILE), TILE)


def unit_rows(x):
    inverse = lax.rsqrt(jnp.mean(x * x, axis=-1, keepdims=True) + epsilon)
    return x * inverse, inverse


def unit_back(up, unit, inverse, gain):
    scaled = up * gain
    inner = jnp.mean(scaled * unit, axis=-1, keepdims=True)
    return inverse * (scaled - unit * inner)


def norm_project(idx, values, gain, weights, column, width, name):
    rows, features = values.shape

    def body(s, x_ref, g_ref, w_ref, n_ref, p_ref):
        @pl.loop(0, rows // TILE)
        def _(i):
            at = span(i * TILE)
            unit, unused = unit_rows(x_ref[at, :].astype(f32))
            normed = (unit * g_ref[...]).astype(bf16)
            n_ref[at, :] = normed
            p_ref[at, :] = dot_nn(normed, w_ref[:, column : column + width]).astype(bf16)

    return launch(
        body,
        idx,
        [values, gain, weights],
        [shaped((rows, features), bf16), shaped((rows, width), bf16)],
        flops=2 * rows * features * width,
        name=name,
    )


def masked_scores(kind, keys, queries, katt, qatt):
    scores = dot_nt(keys, queries)
    if kind == "free":
        return scores
    if kind == "valid":
        return jnp.where(katt[:, 2:3] > 0.0, scores, masked_value)
    places = lax.broadcasted_iota(jnp.int32, scores.shape, 0)
    asking = lax.broadcasted_iota(jnp.int32, scores.shape, 1)
    same = katt[:, 0:1] == qatt[0:1, :]
    if kind == "prev":
        allowed = same & (places > asking)
    else:
        allowed = same & ((places <= asking) | (katt[:, 1:2] == qatt[1:2, :]))
    return jnp.where(allowed, scores, masked_value)


def attention_inputs(queries, segments, katt, qatt):
    arrays = []

    def place(array):
        for k, known in enumerate(arrays):
            if known is array:
                return k
        arrays.append(array)
        return len(arrays) - 1

    use_q = place(queries[0])
    use_k = [place(segment[1]) for segment in segments]
    use_att = place(katt)
    use_qatt = place(qatt) if qatt is not None else None
    return arrays, use_q, use_k, use_att, use_qatt


def read_attention(refs, uses, queries, segments, head):
    use_q, use_k, use_att, use_qatt = uses
    unused, q_row, q_col = queries

    def take(ref, row, col):
        lanes = pl.ds(pl.multiple_of(col + head * HEAD, HEAD), HEAD)
        return ref[row * BLOCK : (row + 1) * BLOCK, lanes]

    q = take(refs[use_q], q_row, q_col)
    parts = []
    for (kind, unused, row, k_col, v_col, att), k in zip(segments, use_k):
        rows = None if att is None else refs[use_att][att * BLOCK : (att + 1) * BLOCK, :]
        parts.append((kind, take(refs[k], row, k_col), take(refs[k], row, v_col), rows))
    qa = None if use_qatt is None else refs[use_qatt][:, q_row * BLOCK : (q_row + 1) * BLOCK]
    return q, parts, qa


def attend(idx, queries, segments, katt, qatt, heads, name):
    arrays, *uses = attention_inputs(queries, segments, katt, qatt)
    count = len(arrays)

    def body(s, *refs):
        o_ref, l_ref = refs[count:]

        @pl.loop(0, heads)
        def _(head):
            q, parts, qa = read_attention(refs, uses, queries, segments, head)
            scores = [masked_scores(kind, k, q, ka, qa) for kind, k, v, ka in parts]
            largest = functools.reduce(
                jnp.maximum, [jnp.max(x, axis=0, keepdims=True) for x in scores]
            )
            total = jnp.zeros_like(largest)
            mixed = jnp.zeros((HEAD, BLOCK), f32)
            for x, (kind, k, v, ka) in zip(scores, parts):
                raised = jnp.exp2((x - largest) * log2_scale)
                total = total + jnp.sum(raised, axis=0, keepdims=True)
                mixed = mixed + dot_tn(v, raised.astype(bf16))
            lanes = pl.ds(pl.multiple_of(head * HEAD, HEAD), HEAD)
            o_ref[:, lanes] = jnp.transpose(mixed * (1.0 / total)).astype(bf16)
            l_ref[head] = largest * log2_scale + jnp.log2(total)

    keys = BLOCK * len(segments)
    return launch(
        body,
        idx,
        arrays,
        [shaped((BLOCK, heads * HEAD), bf16), shaped((heads, 1, BLOCK), f32)],
        flops=4 * heads * BLOCK * keys * HEAD * 2,
        name=name,
    )


def attend_back(idx, queries, segments, katt, qatt, heads, logs, upstream, added, dtypes, name):
    arrays, *uses = attention_inputs(queries, segments, katt, qatt)
    count = len(arrays)
    inputs = arrays + [logs, upstream]
    for pairs in added:
        for pair in pairs:
            inputs.extend(pair)
    wide = (BLOCK, heads * HEAD)
    outputs = [shaped(wide, bf16)]
    for dtype in dtypes:
        outputs.extend([shaped(wide, dtype)] * 2)

    def body(s, *refs):
        rest = list(refs[count:])
        l_ref, go_ref = rest.pop(0), rest.pop(0)
        sums = []
        for pairs in added:
            sums.append([(rest.pop(0), rest.pop(0)) for unused in pairs])
        gq_ref = rest.pop(0)
        outs = list(zip(rest[0::2], rest[1::2]))

        @pl.loop(0, heads)
        def _(head):
            q, parts, qa = read_attention(refs, uses, queries, segments, head)
            lanes = pl.ds(pl.multiple_of(head * HEAD, HEAD), HEAD)
            log_total = l_ref[head]
            go = go_ref[:, lanes]
            chances, grads = [], []
            inner = jnp.zeros((1, BLOCK), f32)
            for kind, k, v, ka in parts:
                x = masked_scores(kind, k, q, ka, qa)
                chance = jnp.exp2(x * log2_scale - log_total)
                grad = dot_nt(v, go)
                inner = inner + jnp.sum(chance * grad, axis=0, keepdims=True)
                chances.append(chance)
                grads.append(grad)
            gq = jnp.zeros((HEAD, BLOCK), f32)
            for (kind, k, v, ka), chance, grad, pairs, out in zip(
                parts, chances, grads, sums, outs
            ):
                gl = (chance * (grad - inner)).astype(bf16)
                gk = dot_nn(gl, q) * score_scale
                gv = dot_nn(chance.astype(bf16), go)
                gq = gq + dot_tn(k, gl)
                for more_k, more_v in pairs:
                    gk = gk + more_k[:, lanes]
                    gv = gv + more_v[:, lanes]
                out[0][:, lanes] = gk.astype(out[0].dtype)
                out[1][:, lanes] = gv.astype(out[1].dtype)
            gq_ref[:, lanes] = jnp.transpose(gq * score_scale).astype(bf16)

    keys = BLOCK * len(segments)
    return launch(
        body,
        idx,
        inputs,
        outputs,
        flops=10 * heads * BLOCK * keys * HEAD * 2,
        vmem=20,
        name=name,
    )


def state_update(idx, pieces, write_pieces, state, retain, gain, weights, width, name):
    rows, features = state.shape
    count = len(pieces)
    project = weights is not None

    def body(s, *refs):
        refs = list(refs)
        piece_refs = [refs.pop(0) for unused in range(count)]
        w_refs = [refs.pop(0) for unused in range(count)]
        s_ref, r_ref = refs[:2]
        refs = refs[2:]
        if project:
            g_ref, p_ref, out_ref, n_ref, t_ref = refs
        else:
            (out_ref,) = refs

        @pl.loop(0, rows // TILE)
        def _(i):
            at = span(i * TILE)
            terms = [
                dot_nn(o_ref[at, :], w_ref[: o_ref.shape[1], :])
                for o_ref, w_ref in zip(piece_refs, w_refs)
            ]
            while len(terms) > 1:
                terms = [a + b for a, b in zip(terms[0::2], terms[1::2])]
            update = terms[0]
            keep = r_ref[...]
            following = keep * s_ref[at, :].astype(f32) + (1.0 - keep) * update
            out_ref[at, :] = following
            if project:
                normed = (unit_rows(following)[0] * g_ref[...]).astype(bf16)
                n_ref[at, :] = normed
                t_ref[at, :] = dot_nn(normed, p_ref[:, :width]).astype(bf16)

    inputs = list(pieces) + list(write_pieces) + [state, retain]
    outputs = [shaped((rows, features), f32)]
    if project:
        inputs += [gain, weights]
        outputs += [shaped((rows, features), bf16), shaped((rows, width), bf16)]
    return launch(
        body,
        idx,
        inputs,
        outputs,
        flops=2 * rows * features * (features + (width if project else 0)),
        name=name,
    )


def take_sum(i, s, refs, total):
    chip_ref, mine_ref, theirs_ref = refs
    steps = HALF // TILE
    at, inner = span(tile_start(i, s)), span(lax.rem(i, steps) * TILE)

    @pl.when(i < steps)
    def _():
        total[...] = chip_ref[at, :].astype(f32) + mine_ref[inner, :].astype(f32)

    @pl.when(i >= steps)
    def _():
        total[...] = chip_ref[at, :].astype(f32) + theirs_ref[inner, :].astype(f32)

    return total[...]


def chip_sum(idx, partial, other, name):
    rows, features = partial.shape
    tall = 32

    def body(s, a_ref, b_ref, sum_ref, own_ref):
        @pl.loop(0, rows // tall)
        def _(i):
            at = rows_of(i, 0, tall)
            sum_ref[at, :] = (a_ref[at, :].astype(f32) + b_ref[at, :].astype(f32)).astype(bf16)

        @pl.loop(0, HALF // tall)
        def _(i):
            own_ref[rows_of(i, 0, tall), :] = sum_ref[pl.ds(pl.multiple_of(s[1] * HALF + i * tall, tall), tall), :]

    return launch(
        body,
        idx,
        [partial, other],
        [shaped((rows, features), bf16), shaped((HALF, features), bf16)],
        name=name,
    )


def add_rows(i, ref, value):
    value = jnp.sum(value, axis=0, keepdims=True)

    @pl.when(i == 0)
    def _():
        ref[...] = value

    @pl.when(i != 0)
    def _():
        ref[...] = ref[...] + value


def project_back(idx, grads, weights, column, name):
    rows, width = grads[0].shape
    features = weights.shape[1]

    def body(s, *refs):
        *g_refs, w_ref, out_ref = refs

        @pl.loop(0, rows // TILE)
        def _(i):
            at = span(i * TILE)
            out = jnp.zeros((TILE, features), f32)
            for k, ref in enumerate(g_refs):
                first = column + k * width
                out = out + dot_nn(ref[at, :], w_ref[first : first + width, :])
            out_ref[at, :] = out.astype(bf16)

    return launch(
        body,
        idx,
        list(grads) + [weights],
        [shaped((rows, features), bf16)],
        flops=2 * rows * features * width * len(grads),
        name=name,
    )[0]


def state_back(idx, sums, state, following, retain, gain, write_own, name):
    rows, features = state.shape
    before = write_own is not None
    width = write_own.shape[1] // 2 if before else 10

    def body(s, *refs):
        refs = list(refs)
        total = refs.pop()
        sum_refs = [refs.pop(0) for unused in range(len(sums))]
        s_ref, r_ref, g_ref = refs[:3]
        refs = refs[3:]
        following_ref = refs.pop(0) if following is not None else None
        if before:
            w_ref, gs_ref, gain_ref, gu_ref, gos_ref = refs
        else:
            gs_ref, gain_ref = refs

        @pl.loop(0, rows // TILE)
        def _(i):
            at = span(tile_start(i, s))
            up = take_sum(i, s, sum_refs, total)
            unit, inverse = unit_rows(s_ref[at, :].astype(f32))
            out = unit_back(up, unit, inverse, g_ref[...])
            if following is not None:
                out = r_ref[...] * following_ref[at, :] + out
            gs_ref[at, :] = out
            add_rows(i, gain_ref, up * unit)
            if before:
                gu = ((1.0 - r_ref[...]) * out).astype(bf16)
                gu_ref[at, :] = gu
                gos_ref[at, :] = dot_nn(gu, w_ref[:, :width]).astype(bf16)

    inputs = list(sums) + [state, retain, gain]
    outputs = [shaped((rows, features), f32), shaped((1, features), f32)]
    if following is not None:
        inputs.append(following)
    if before:
        inputs.append(write_own)
        outputs += [shaped((rows, features), bf16), shaped((rows, width), bf16)]
    return launch(
        body,
        idx,
        inputs,
        outputs,
        scratch=[pltpu.VMEM((TILE, features), f32)],
        flops=2 * rows * features * width,
        name=name,
    )


def last_update_back(idx, retain, write_own, rows, name):
    features, width = write_own.shape[0], write_own.shape[1] // 2

    def body(s, r_ref, w_ref, gu_ref, gos_ref):
        gu = ((1.0 - r_ref[...]) * jnp.zeros((rows, features), f32)).astype(bf16)
        gu_ref[...] = gu
        gos_ref[...] = dot_nn(gu, w_ref[:, :width]).astype(bf16)

    return launch(
        body,
        idx,
        [retain, write_own],
        [shaped((rows, features), bf16), shaped((rows, width), bf16)],
        name=name,
    )


def gelu_both(a):
    root, cubic = 0.7978845608028654, 0.044715
    squared = a * a
    bent = jnp.tanh(root * (a + cubic * (squared * a)))
    rising = 0.5 * (1.0 + bent)
    slope = rising + (0.5 * root) * a * (1.0 - bent * bent) * (1.0 + (3.0 * cubic) * squared)
    return a * rising, slope


def output_forward(idx, number, pieces, out_pieces, tokens, gain, name):
    features = tokens.shape[1]
    count = len(pieces)

    def body(s, *refs):
        o_refs, w_refs = refs[:count], refs[count : 2 * count]
        t_ref, g_ref, x1_ref, xn_ref = refs[2 * count :]

        @pl.loop(0, BLOCK // TILE)
        def _(i):
            at = span(i * TILE)
            x1 = t_ref[span(i * TILE, number * BLOCK), :].astype(f32)
            for o_ref, w_ref in zip(o_refs, w_refs):
                x1 = x1 + dot_nn(o_ref[at, :], w_ref[o_ref.shape[1] :, :])
            x1_ref[at, :] = x1
            xn_ref[at, :] = (unit_rows(x1)[0] * g_ref[...]).astype(bf16)

    return launch(
        body,
        idx,
        list(pieces) + list(out_pieces) + [tokens, gain],
        [shaped((BLOCK, features), f32), shaped((BLOCK, features), bf16)],
        flops=2 * BLOCK * features * features,
        name=name,
    )


def dense_forward(idx, normed, dense, name):
    features = normed.shape[1]
    hidden = dense[1].shape[0]

    def body(s, n_ref, up_ref, down_ref, h_ref, slope_ref, part_ref):
        @pl.loop(0, BLOCK // TILE)
        def _(i):
            at = span(i * TILE)
            h, slope = gelu_both(dot_nn(n_ref[at, :], up_ref[:, :hidden]))
            h = h.astype(bf16)
            h_ref[at, :] = h
            slope_ref[at, :] = slope.astype(bf16)
            part_ref[at, :] = dot_nn(h, down_ref[...]).astype(bf16)

    return launch(
        body,
        idx,
        [normed, *dense],
        [
            shaped((BLOCK, hidden), bf16),
            shaped((BLOCK, hidden), bf16),
            shaped((BLOCK, features), bf16),
        ],
        flops=4 * BLOCK * features * hidden,
        name=name,
    )


def dense_backward(idx, number, sums, x1, teacher, katt, slope, dense, name):
    features = x1.shape[1]
    up_t, both = dense
    hidden = up_t.shape[0]

    def body(s, *refs):
        refs = list(refs)
        total = refs.pop()
        sum_refs = [refs.pop(0) for unused in range(len(sums))]
        x_ref, t_ref, v_ref, slope_ref, up_ref, d_ref = refs[:6]
        gm_ref, ga_ref, loss_ref, part_ref = refs[6:]

        @pl.loop(0, BLOCK // TILE)
        def _(i):
            start = tile_start(i, s)
            at, far = span(start), span(start, number * BLOCK)
            errors = x_ref[at, :] + take_sum(i, s, sum_refs, total) - t_ref[far, :].astype(f32)
            gy = v_ref[far, 2:3] * errors
            add_rows(i, loss_ref, gy * errors)
            gm = gy.astype(bf16)
            gm_ref[at, :] = gm
            ga = (dot_nn(gm, d_ref[:, hidden:]) * slope_ref[at, :].astype(f32)).astype(bf16)
            ga_ref[at, :] = ga
            part_ref[at, :] = dot_nn(ga, up_ref[...]).astype(bf16)

    return launch(
        body,
        idx,
        list(sums) + [x1, teacher, katt, slope, up_t, both],
        [
            shaped((BLOCK, features), bf16),
            shaped((BLOCK, hidden), bf16),
            shaped((1, features), f32),
            shaped((BLOCK, features), bf16),
        ],
        scratch=[pltpu.VMEM((TILE, features), f32)],
        flops=4 * BLOCK * features * hidden,
        name=name,
    )


def output_backward(idx, sums, gy, x1, gain, out_own, name):
    features = x1.shape[1]
    width = out_own.shape[1] // 2

    def body(s, *refs):
        refs = list(refs)
        total = refs.pop()
        sum_refs = [refs.pop(0) for unused in range(len(sums))]
        gy_ref, x_ref, g_ref, w_ref, gp_ref, go_ref, gain_ref = refs

        @pl.loop(0, BLOCK // TILE)
        def _(i):
            at = span(tile_start(i, s))
            up = take_sum(i, s, sum_refs, total)
            unit, inverse = unit_rows(x_ref[at, :])
            gx = gy_ref[at, :].astype(f32) + unit_back(up, unit, inverse, g_ref[...])
            gp = gx.astype(bf16)
            gp_ref[at, :] = gp
            go_ref[at, :] = dot_nn(gp, w_ref[:, width:]).astype(bf16)
            add_rows(i, gain_ref, up * unit)

    return launch(
        body,
        idx,
        list(sums) + [gy, x1, gain, out_own],
        [
            shaped((BLOCK, features), bf16),
            shaped((BLOCK, width), bf16),
            shaped((1, features), f32),
        ],
        scratch=[pltpu.VMEM((TILE, features), f32)],
        flops=2 * BLOCK * features * width,
        name=name,
    )


def weight_grads(idx, groups, name):
    features = groups[0][0][0].shape[1]
    inputs, specs, total, flops = [], [], 0, 0
    for parts in groups:
        for left, block, right in parts:
            rows = right.shape[0]
            inputs += [left, right]
            specs.append(pl.BlockSpec((rows, HALF), lambda i, block=block: (block, i)))
            specs.append(
                pl.BlockSpec(right.shape, lambda i: (0, 0), pipeline_mode=pl.Buffered(1))
            )
            flops += 2 * rows * features * right.shape[1]
        total += parts[0][2].shape[1]

    def body(s, *refs):
        refs = list(refs)
        out_ref = refs.pop()
        at = 0
        for parts in groups:
            size = parts[0][2].shape[1]
            out = jnp.zeros((HALF, size), f32)
            for unused in parts:
                left, right = refs.pop(0), refs.pop(0)
                out = out + dot_tn(left[...], right[...])
            out_ref[:, at : at + size] = out.astype(bf16)
            at += size

    return pl.pallas_call(
        body,
        grid=(features // HALF,),
        in_specs=[pl.BlockSpec(memory_space=pltpu.SMEM)] + specs,
        out_specs=pl.BlockSpec((HALF, total), lambda i: (i, 0)),
        out_shape=pltpu.HBM((features, total), bf16),
        compiler_params=pltpu.CompilerParams(
            dimension_semantics=("arbitrary",), vmem_limit_bytes=20 << 20
        ),
        cost_estimate=cost(flops, inputs),
        name=name,
    )(idx, *inputs)


def unpack_grads(packed, widths, flipped, name):
    rows = packed.shape[0]

    def body(p_ref, *out_refs):
        at = 0
        for size, flip, out_ref in zip(widths, flipped, out_refs):
            values = p_ref[:, at : at + size].astype(f32)
            out_ref[...] = jnp.transpose(values) if flip else values
            at += size

    return pl.pallas_call(
        body,
        in_specs=[pl.BlockSpec(memory_space=pltpu.VMEM)],
        out_specs=[pl.BlockSpec(memory_space=pltpu.VMEM)] * len(widths),
        out_shape=[
            shaped((size, rows) if flip else (rows, size), f32)
            for size, flip in zip(widths, flipped)
        ],
        compiler_params=pltpu.CompilerParams(vmem_limit_bytes=8 << 20),
        cost_estimate=cost(0, [packed]),
        name=name,
    )(packed)


def arrange_rows(idx, pieces, count, name):
    rows, features = pieces[0].shape
    rows = rows // count

    def body(s, *refs):
        ins, outs = refs[: len(pieces)], refs[len(pieces) :]
        for k, ref in enumerate(ins):
            for j, out_ref in enumerate(outs):
                out_ref[rows_of(s[0] ^ k, 0, rows), :] = ref[j * rows : (j + 1) * rows, :]

    return launch(
        body,
        idx,
        pieces,
        [shaped((rows * len(pieces), features), pieces[0].dtype)] * count,
        name=name,
    )


def turn(idx, values, first, count, name):
    rows = values.shape[0]
    wide = 256

    def body(s, v_ref, out_ref):
        @pl.loop(0, count // wide)
        def _(i):
            lanes = pl.ds(pl.multiple_of(first + i * wide, HEAD), wide)
            out_ref[rows_of(i, 0, wide), :] = jnp.transpose(v_ref[:, lanes])

    return launch(body, idx, [values], [shaped((count, rows), values.dtype)], name=name)[0]


def arrange_columns(idx, blocks, across, name):
    rows, width = blocks[0].shape
    depth = len(blocks)

    def body(s, *refs):
        out_ref = refs[-1]
        for k in range(depth):
            level = lax.rem(s[3] + depth - k, depth)
            out_ref[rows_of(2 * level + s[4], 0, rows), :] = refs[k][...]
            out_ref[rows_of(2 * level + 1 - s[4], 0, rows), :] = refs[depth + k][...]

    return launch(
        body,
        idx,
        list(blocks) + list(across),
        [shaped((2 * depth * rows, width), blocks[0].dtype)],
        name=name,
    )[0]


def split_grads(idx, groups, depth, name):
    features = groups[0][0][0].shape[1]
    rows = features // (2 * depth)
    total = sum(parts[0][2].shape[1] for parts in groups)
    inputs = []

    def place(array):
        for k, known in enumerate(inputs):
            if known is array:
                return k
        inputs.append(array)
        return len(inputs) - 1

    uses = [[(place(a), block, place(c)) for a, block, c in parts] for parts in groups]

    def body(s, *refs):
        *ins, theirs_ref, mine_ref, held = refs

        @pl.loop(0, depth)
        def _(i):
            lanes = pl.ds(pl.multiple_of(i * 2 * rows, 2 * rows), 2 * rows)
            at = 0
            for parts in uses:
                size = ins[parts[0][2]].shape[1]
                out = jnp.zeros((2 * rows, size), f32)
                for left, block, right in parts:
                    count = ins[right].shape[0]
                    tall = slice(block * count, (block + 1) * count)
                    out = out + dot_tn(ins[left][tall, lanes], ins[right][...])
                held[:, at : at + size] = out.astype(bf16)
                at += size
            mine_ref[rows_of(i, 0, rows), :] = held[rows_of(s[4], 0, rows), :]
            theirs_ref[rows_of(i, 0, rows), :] = held[rows_of(1 - s[4], 0, rows), :]

    return launch(
        body,
        idx,
        inputs,
        [shaped((depth * rows, total), bf16)] * 2,
        scratch=[pltpu.VMEM((2 * rows, total), bf16)],
        name=name,
    )


def pair_blocks(idx, mine, got, depth, name):
    rows, width = mine.shape[0] // depth, mine.shape[1]

    def body(s, mine_ref, got_ref, *out_refs):
        for k, ref in enumerate(out_refs):
            at = rows_of(lax.rem(s[3] + k, depth), 0, rows)
            ref[...] = (mine_ref[at, :].astype(f32) + got_ref[at, :].astype(f32)).astype(ref.dtype)

    return launch(
        body,
        idx,
        [mine, got],
        [shaped((rows, width), f32)] + [shaped((rows, width), bf16)] * (depth - 1),
        name=name,
    )


def line_sum(idx, own, others, widths, flipped, name):
    rows = own.shape[0]

    def body(s, own_ref, *refs):
        ins, outs = refs[: len(others)], refs[len(others) :]
        total = own_ref[...]
        for ref in ins:
            total = total + ref[...].astype(f32)
        at = 0
        for size, flip, out_ref in zip(widths, flipped, outs):
            values = total[:, at : at + size]
            out_ref[...] = jnp.transpose(values) if flip else values
            at += size

    return launch(
        body,
        idx,
        [own] + list(others),
        [
            shaped((size, rows) if flip else (rows, size), f32)
            for size, flip in zip(widths, flipped)
        ],
        name=name,
    )


def pack(idx, arrays, takes, shapes, name):
    flipped = [take for take in takes if take[-1]]

    def body(s, *refs):
        ins, outs = refs[: len(arrays)], refs[len(arrays) : len(arrays) + len(shapes)]
        *held, sems = refs[len(arrays) + len(shapes) :]
        copies, spare = [], list(held)
        for j, (k, row, col, rows, cols, out, place, flip) in enumerate(takes):
            at = pl.ds(0, rows) if row is None else rows_of(s[row], 0, rows)
            to = pl.ds(0, cols) if col is None else rows_of(s[col], 0, cols)
            if flip:
                target = spare.pop(0)
            else:
                target = outs[out].at[pl.ds(place[0], rows), pl.ds(place[1], cols)]
            copies.append(pltpu.make_async_copy(ins[k].at[at, to], target, sems.at[j]))
            copies[-1].start()
        spare = list(held)
        for copy, (k, row, col, rows, cols, out, place, flip) in zip(copies, takes):
            copy.wait()
            if flip:
                to = slice(place[1], place[1] + rows)
                outs[out][place[0] : place[0] + cols, to] = jnp.transpose(spare.pop(0)[...])

    return pl.pallas_call(
        body,
        in_specs=[pl.BlockSpec(memory_space=pltpu.SMEM)]
        + [pl.BlockSpec(memory_space=pl.ANY)] * len(arrays),
        out_specs=[pl.BlockSpec(memory_space=pltpu.VMEM)] * len(shapes),
        out_shape=[shaped(a, bf16) for a in shapes],
        scratch_shapes=[pltpu.VMEM((take[3], take[4]), bf16) for take in flipped]
        + [pltpu.SemaphoreType.DMA((len(takes),))],
        compiler_params=pltpu.CompilerParams(vmem_limit_bytes=8 << 20),
        cost_estimate=cost(0, arrays),
        name=name,
    )(idx, *[pltpu.with_memory_space_constraint(a, pltpu.HBM) for a in arrays])


def input_rows(idx, own, arrived, gps, tokens, gain, name):
    rows, features = tokens.shape
    count = len(gps)

    def body(s, *refs):
        own_refs, far_refs, gp_refs = refs[:count], refs[count : 2 * count], refs[2 * count : 3 * count]
        t_ref, g_ref, out_ref, gain_ref = refs[3 * count :]
        unit, inverse = unit_rows(t_ref[...].astype(f32))
        for b in range(count):

            @pl.when(s[2] // 2 == b)
            def _():
                at = rows_of(s[1])
                up = own_refs[b][at, :].astype(f32) + far_refs[b][...].astype(f32)
                base = gp_refs[b][rows_of(s[1]), :].astype(f32)
                out_ref[...] = base + unit_back(up, unit, inverse, g_ref[...])
                gain_ref[...] = jnp.sum(up * unit, axis=0, keepdims=True)

    return launch(
        body,
        idx,
        list(own) + list(arrived) + list(gps) + [tokens, gain],
        [shaped((rows, features), f32), shaped((1, features), f32)],
        name=name,
    )


def per_device(
    block_input,
    state_start,
    teacher,
    valid_mask,
    segment,
    image_offset,
    retain,
    to_query,
    to_key,
    to_value,
    to_output,
    to_hidden,
    to_model,
    state_query,
    state_key,
    state_value,
    state_write,
    first_gain,
    second_gain,
    state_gain,
):
    row_devices = lax.axis_size("row")
    col_devices = lax.axis_size("col")
    row_index = lax.axis_index("row")
    col_index = lax.axis_index("col")
    local_rows, features = block_input.shape[1:]
    length = local_rows * row_devices
    width = to_query.shape[1]
    heads = width // HEAD
    hidden = to_hidden.shape[1] // row_devices
    nblocks = length // BLOCK
    pairs = row_devices == 4 and 2 * local_rows == BLOCK
    lines = pairs and col_devices == 8
    core_pairs = [(k, k ^ 1) for k in range(row_devices)]
    chip_pairs = [(k, k ^ 2) for k in range(row_devices)] if pairs else None
    if pairs:
        idx = jnp.stack([row_index, row_index % 2, row_index, col_index // 2, col_index % 2])
    else:
        idx = jnp.stack([0, 1, row_index, 0, 0])
    idx = idx.astype(jnp.int32)

    def to_core(x):
        return lax.ppermute(x, "row", core_pairs)

    def to_chip(x):
        return lax.ppermute(x, "row", chip_pairs)

    def row_moves(x):
        if not pairs:
            stacked = lax.all_gather(x, "row", axis=0, tiled=False)
            return [stacked[k] for k in range(row_devices)]
        return [x, to_core(x), to_chip(x)]

    def row_pieces(moved, *ties):
        if not pairs:
            return moved
        x, near, far = moved
        return [x, near, far, to_core(after(far, *ties))]

    depth_z = col_devices // 2

    def along(v, step):
        levels = range(depth_z)
        moves = [(2 * z + y, 2 * ((z + step) % depth_z) + y) for z in levels for y in range(2)]
        return lax.ppermute(v, "col", moves)

    def across(v):
        return lax.ppermute(v, "col", [(k, k ^ 1) for k in range(col_devices)])

    class Columns:
        def __init__(self, x, name):
            self.name = name
            if lines:
                self.blocks = [x] + [along(x, k) for k in range(1, depth_z)]
                self.crossed = [across(x)]
            else:
                self.whole = lax.all_gather(x, "col", axis=0, tiled=True)

        def cross(self, k, *ties):
            if lines:
                self.crossed.append(across(after(self.blocks[k], *ties)))

        def landed(self, k):
            return [self.blocks[k], self.crossed[k - 1]] if lines else []

        def result(self, *ties):
            if lines:
                order = after(idx, *ties)
                return arrange_columns(order, self.blocks, self.crossed, self.name)
            return self.whole

    class Scattered:
        def __init__(self, groups, name, *ties):
            self.name, self.widths = name, [parts[0][2].shape[1] for parts in groups]
            if lines:
                order = after(idx, *ties) if ties else idx
                theirs, self.mine = split_grads(order, groups, depth_z, name)
                self.got = across(theirs)
            else:
                packed = weight_grads(idx, groups, name)
                self.whole = lax.psum_scatter(packed, "col", scatter_dimension=0, tiled=True)

        def send(self, *ties):
            if lines:
                mine = after(self.mine, *ties) if ties else self.mine
                self.own, *blocks = pair_blocks(idx, mine, self.got, depth_z, f"{self.name}_y")
                self.far = [along(block, k + 1) for k, block in enumerate(blocks)]

        def result(self, flipped):
            if lines:
                return line_sum(idx, self.own, self.far, self.widths, flipped, f"{self.name}_z")
            return unpack_grads(self.whole, self.widths, flipped, f"{self.name}_z")

    class RowSum:
        def __init__(self, partial, name, receiver=None, ties=()):
            if pairs:
                order = after(idx, *ties) if ties else idx
                self.chip, own = chip_sum(order, partial, to_core(partial), name)
                moves = [m for m in chip_pairs if receiver is None or m[1] // 2 == receiver]
                self.far = lax.ppermute(own, "row", moves)
            else:
                self.chip = lax.psum(partial, "row")

        def result(self, *ties):
            if pairs:
                return [self.chip, self.far, to_core(after(self.far, *ties))]
            none = jnp.zeros((HALF, features), bf16)
            return [self.chip, none, none]

    def all_sum(x):
        for axis, size in (("row", row_devices), ("col", col_devices)):
            step = 1
            while step < size:
                x = x + lax.ppermute(x, axis, [(k, k ^ step) for k in range(size)])
                step *= 2
        return x

    depth = to_query.shape[0]
    (near,) = pack(
        idx,
        [state_query, state_key, state_value, to_query, to_key, to_value],
        [(k, None, None, depth, width, 0, (0, k * width), False) for k in range(6)],
        [(depth, 6 * width)],
        "pack_near",
    )
    near = lax.all_gather(near, "col", axis=0, tiled=True)
    rows_in, mid, far_weights = pack(
        idx,
        [state_write, to_output, to_hidden, to_model, block_input[0], teacher[0]],
        [
            (4, None, None, local_rows, features, 0, (0, 0), False),
            (5, None, None, local_rows, features, 0, (local_rows, 0), False),
            (0, 2, None, width, depth, 1, (0, 0), True),
            (1, None, None, width, depth, 1, (0, width), True),
            (2, None, 2, depth, hidden, 2, (0, 0), False),
            (3, 2, None, hidden, depth, 2, (0, hidden), True),
        ],
        [(2 * local_rows, features), (depth, 2 * width), (depth, 2 * hidden)],
        "pack_rest",
    )
    rows_moved = row_moves(rows_in) if pairs else None
    mid = Columns(mid, "mid")
    for k in range(1, depth_z):
        mid.cross(k)
    mid = mid.result()
    mid_n = turn(idx, mid, 0, 2 * width, "mid_turn")
    held = [mid_n] + (rows_moved[2:] if pairs else [])
    dense = lax.all_gather(after(far_weights, *held), "col", axis=0, tiled=True)
    mid_moved = row_moves(mid_n)
    if pairs:
        tokens, teacher_all = arrange_rows(idx, row_pieces(rows_moved), 2, "tokens")
    else:
        tokens, teacher_all = [
            lax.all_gather(x[0], "row", axis=0, tiled=True) for x in (block_input, teacher)
        ]

    valid_row = lax.dynamic_index_in_dim(valid_mask, col_index, 0, keepdims=False)
    segment_row = segment[0]
    numbers = jnp.arange(nblocks, dtype=jnp.int32)
    places = jnp.arange(length, dtype=jnp.int32)
    starts = numbers * BLOCK + image_offset[0]
    inside = (places[:, None] >= starts[None, :]) & (places[:, None] < starts[None, :] + PIECE)
    piece = jnp.sum(jnp.where(inside, numbers[None, :] + 1, 0), axis=1) - 1
    valid_count = jnp.sum(valid_mask.astype(f32))
    total_tokens = f32(length * col_devices)
    weight_of_row = total_tokens / valid_count * valid_row.astype(f32)
    document = segment_row.astype(f32)
    nothing = jnp.zeros_like(document)
    katt = jnp.stack(
        [jnp.where(valid_row > 0, document, -1.0), piece.astype(f32), weight_of_row, nothing],
        axis=1,
    )
    qatt = jnp.stack(
        [document, jnp.where(piece >= 0, piece, -2).astype(f32), nothing, nothing], axis=0
    )
    retain2 = retain[None]
    first_gain2, second_gain2, state_gain2 = first_gain[None], second_gain[None], state_gain[None]

    def token_segments(number, trio):
        found = []
        if number > 0:
            found.append(("prev", token_heads, number - 1, width, 2 * width, number - 1))
        found.append(("own", token_heads, number, width, 2 * width, number))
        found.append(("free", trio, 0, width, 2 * width, None))
        return found

    def state_segments(number, trio):
        return [
            ("valid", token_heads, number, width, 2 * width, number),
            ("free", trio, 0, width, 2 * width, None),
        ]

    current = state_start[0]
    near_t = turn(idx, near, 0, 6 * width, "near_turn")
    state_low, trio = norm_project(after(idx, near_t), current, state_gain2, near, 0, 3 * width, "state_proj")
    first_low, token_heads = norm_project(
        idx, tokens, first_gain2, near, 3 * width, 3 * width, "token_proj"
    )
    states, lows, trios = [], [], []
    state_out, state_logs, token_out, token_logs = [], [], [], []
    x1s, second_lows, hiddens, slopes, dense_sums = [], [], [], [], []
    state_pieces, token_pieces = [], []
    end = nblocks - 1

    def state_part(b):
        mixed, logs = attend(
            idx,
            (trios[b], 0, 0),
            state_segments(b, trios[b]),
            katt,
            None,
            heads,
            f"state_attend{b}",
        )
        state_out.append(mixed)
        state_logs.append(logs)
        state_pieces.append(row_moves(mixed) if b < nblocks - 1 else None)

    for b in range(nblocks):
        states.append(current)
        lows.append(state_low)
        trios.append(trio)
        last = b + 1 == nblocks
        if not last:
            state_part(b)
        mixed, logs = attend(
            idx, (token_heads, b, 0), token_segments(b, trio), katt, qatt, heads, f"token_attend{b}"
        )
        if b == 0:
            mid_pieces = row_pieces(mid_moved, mixed)
        token_out.append(mixed)
        token_logs.append(logs)
        token_pieces.append(row_moves(mixed))
        if not last:
            current, state_low, trio = state_update(
                idx,
                row_pieces(state_pieces[b], mixed),
                mid_pieces,
                current,
                retain2,
                state_gain2,
                near,
                3 * width,
                f"update{b}",
            )
            token_pieces[b] = row_pieces(token_pieces[b], trio)
    state_part(nblocks - 1)
    token_pieces[-1] = row_pieces(token_pieces[-1], state_out[-1])

    gus = [None] * nblocks
    gms, gas, losses, gps, gos, second_sums = [], [], [], [], [], []
    second_back = []
    for b in range(nblocks):
        x1, low = output_forward(
            idx, b, token_pieces[b], mid_pieces, tokens, second_gain2, f"out{b}"
        )
        x1s.append(x1)
        second_lows.append(low)
    down = turn(after(idx, state_out[-1], *second_lows), dense, hidden, hidden, "down_turn")
    order = idx
    for b in range(nblocks):
        h, slope, partial = dense_forward(order, second_lows[b], (dense, down), f"dense{b}")
        hiddens.append(h)
        slopes.append(slope)
        ties = []
        if b == 0:
            up_t = turn(after(idx, h), dense, 0, hidden, "up_turn")
            ties.append(up_t)
        dense_sums.append(RowSum(partial, f"dense_sum{b}", ties=ties))
        order = after(idx, dense_sums[b].chip)

    def state_back_part(b, gos_state, own, free, dtype):
        return attend_back(
            idx,
            (trios[b], 0, 0),
            state_segments(b, trios[b]),
            katt,
            None,
            heads,
            state_logs[b],
            gos_state,
            [own, free],
            [dtype, dtype],
            f"state_back{b}",
        )

    def token_back_part(b, own, free, dtype, upstream):
        segments = token_segments(b, trios[b])
        added = ([[]] if b > 0 else []) + [own, free]
        dtypes = ([f32] if b > 0 else []) + [dtype, dtype]
        found = attend_back(
            idx,
            (token_heads, b, 0),
            segments,
            katt,
            qatt,
            heads,
            token_logs[b],
            upstream,
            added,
            dtypes,
            f"token_back{b}",
        )
        return found[0], found[-4:], (found[1], found[2]) if b > 0 else None

    late_mid = after(mid, dense_sums[end].chip)
    gus[end], gos_state = last_update_back(idx, retain2, late_mid, NS, "last_back")
    state_found = state_back_part(end, gos_state, [], [], f32)
    ready = teacher_all
    for b in range(nblocks):
        hides = [hiddens[end]] if b == 0 else [gms[b - 1], state_found[0]]
        gm, ga, loss, partial = dense_backward(
            idx, b, dense_sums[b].result(*hides), x1s[b], ready, katt, slopes[b], (up_t, dense), f"back{b}"
        )
        gms.append(gm)
        gas.append(ga)
        losses.append(loss)
        if b < end:
            second_back.append(RowSum(partial, f"back_sum{b}"))
            ready = after(teacher_all, second_back[b].chip)
    dense_grads = weight_grads(
        idx,
        [
            [(low, 0, ga) for low, ga in zip(second_lows, gas)],
            [(gm, 0, h) for gm, h in zip(gms, hiddens)],
        ],
        "dense_grads",
    )
    filled = [dense_grads]
    ties = [dense_grads] + [back.far for back in second_back] if pairs else []
    second_back.append(RowSum(partial, f"back_sum{end}", ties=ties))
    dense_grads = lax.psum_scatter(dense_grads, "col", scatter_dimension=0, tiled=True)

    token_found = [None] * nblocks
    for b in range(nblocks):
        gp, go, gain_sum = output_backward(
            idx,
            second_back[b].result(*(filled if b == end else [gms[end]])),
            gms[b],
            x1s[b],
            second_gain2,
            mid,
            f"out_back{b}",
        )
        gps.append(gp)
        gos.append(go)
        second_sums.append(gain_sum)
        if b < end:
            token_found[b] = token_back_part(b, [], [], f32, go)
            filled.append(token_found[b][0])
    trio_grads = [None] * nblocks
    token_grads = [None] * nblocks
    first_sums = [None] * nblocks
    gain_sums = []
    grad_next = None
    gqs, gk, gv, gks, gvs = state_found
    gq, (gk, gv, gks, gvs), key_part = token_back_part(
        end, [(gk, gv)], [(gks, gvs)], bf16, gos[end]
    )
    state_pieces[-1] = row_moves(after(state_out[-1], gos[end]))
    gqs = after(gqs, state_pieces[-1][2])
    trio_grads[end] = (gqs, gks, gvs)
    token_grads[end] = (gq, gk, gv)
    for b in reversed(range(nblocks)):
        order = idx
        if b == 0:

            def state_group(k):
                return [(lows[c], 0, trio_grads[c][k]) for c in range(nblocks)]

            def token_group(k):
                return [(first_low, c, token_grads[c][k]) for c in range(nblocks)]

            write_group = [(gu, 0, out) for gu, out in zip(gus, state_out)]
            late_grads = weight_grads(
                idx,
                [state_group(k) for k in range(3)] + [token_group(1), token_group(2)],
                "late_grads",
            )
            order = after(idx, late_grads)
            rest_grads = Scattered(
                [token_group(0), [(gp, 0, out) for gp, out in zip(gps, token_out)], write_group],
                "rest_grads",
                late_grads,
            )
            rest_grads.send()
            late_grads = lax.psum_scatter(late_grads, "col", scatter_dimension=0, tiled=True)
        trio_sum = RowSum(
            project_back(order, trio_grads[b], near_t, 0, f"trio_back{b}"),
            f"trio_sum{b}",
        )
        hides = []
        if b == end:
            (final_state,) = state_update(
                idx,
                row_pieces(state_pieces[-1], gq),
                mid_pieces,
                current,
                retain2,
                None,
                None,
                0,
                "update_last",
            )
            hides.append(final_state)
        first_sums[b] = project_back(idx, token_grads[b], near_t, 3 * width, f"first_back{b}")
        hides.append(first_sums[b])
        first_sums[b] = RowSum(first_sums[b], f"first_sum{b}", b) if pairs else first_sums[b]
        if b > 0:
            grad_next, gain_sum, gus[b - 1], gos_state = state_back(
                idx,
                trio_sum.result(*hides),
                states[b],
                grad_next,
                retain2,
                state_gain2,
                mid,
                f"chain_back{b}",
            )
            gq, (gk, gv, gks, gvs), next_part = token_found[b - 1]
            gqs, gk, gv, gks, gvs = state_back_part(
                b - 1, gos_state, [(gk, gv), key_part], [(gks, gvs)], bf16
            )
            key_part = next_part
            trio_grads[b - 1] = (gqs, gks, gvs)
            token_grads[b - 1] = (gq, gk, gv)
        else:
            grad_next, gain_sum = state_back(
                after(idx, rest_grads.own) if lines else idx,
                trio_sum.result(*hides),
                states[b],
                grad_next,
                retain2,
                state_gain2,
                None,
                "chain_back0",
            )
        gain_sums.append(gain_sum)

    if pairs:
        own_rows = [first.chip for first in first_sums]
        arrived = [first.far for first in first_sums]
        input_grad, first_sum = input_rows(
            idx, own_rows, arrived, gps, block_input[0], first_gain2, "input_rows"
        )
        first_sum = first_sum[0]
    else:
        both = jnp.concatenate(first_sums)
        grad_first = lax.psum_scatter(both, "row", scatter_dimension=0, tiled=True).astype(f32)
        own_gx1 = lax.dynamic_slice_in_dim(
            jnp.concatenate(gps), row_index * local_rows, local_rows
        ).astype(f32)
        unit, inverse = unit_rows(block_input[0].astype(f32))
        input_grad = own_gx1 + unit_back(grad_first, unit, inverse, first_gain2)
        first_sum = jnp.sum(grad_first * unit, axis=0)

    share = 1.0 / row_devices
    sums = jnp.stack(
        [
            sum(losses)[0] * share,
            first_sum,
            sum(second_sums)[0] * share,
            sum(gain_sums)[0] * share,
        ]
    )
    if lines:
        sums = after(sums, *rest_grads.far)
    summed = all_sum(sums)
    total_loss = jnp.sum(summed[0]) / (2.0 * total_tokens)

    upper_grad, lower_grad = unpack_grads(
        dense_grads, [hidden, hidden], [False, True], "unpack_dense"
    )
    late = unpack_grads(late_grads, [width] * 5, [False] * 5, "unpack_late")
    rest = rest_grads.result([False, True, True])

    return (
        total_loss,
        final_state[None],
        input_grad[None],
        grad_next[None],
        rest[0],
        late[3],
        late[4],
        rest[1],
        upper_grad,
        lower_grad,
        late[0],
        late[1],
        late[2],
        rest[2],
        summed[1],
        summed[2],
        summed[3],
    )


def solution(mesh):
    in_specs = (
        P("col", "row", None),
        P("col", None, None),
        P("col", "row", None),
        P(),
        P("col", None),
        P("col", None),
        P(),
        P("col", "row"),
        P("col", "row"),
        P("col", "row"),
        P("row", "col"),
        P("col", None),
        P(None, "col"),
        P("col", "row"),
        P("col", "row"),
        P("col", "row"),
        P(None, "col"),
        P(),
        P(),
        P(),
    )
    out_specs = (
        P(),
        P("col", None, None),
        P("col", "row", None),
        P("col", None, None),
        P("col", "row"),
        P("col", "row"),
        P("col", "row"),
        P("row", "col"),
        P("col", "row"),
        P("row", "col"),
        P("col", "row"),
        P("col", "row"),
        P("col", "row"),
        P("row", "col"),
        P(),
        P(),
        P(),
    )
    return jax.shard_map(
        per_device, mesh=mesh, in_specs=in_specs, out_specs=out_specs, check_vma=False
    )
```

profile of v0, /device:TPU:0, one launch (start us, length us, event | category | flops | bytes accessed | tf_op | source)
XLA Modules:
  0.0 386.8 jit_solution(17738179336661656416)
XLA Ops:
  7.3 2.3 pack_near.1
  9.8 2.9 pack_rest.1
  12.7 3.0 collective-permute-start.1
  15.7 3.6 collective-permute-start.10
  25.4 11.6 %collective-permute-done.9.refs_2_ = bf16[128,512]{1,0:T(8,128)(2,1)S(1)} collective-permute-done((bf16[128,512]{1,0:T(8,128)(2,1)S(1)}, bf16[128,512]{1,0:T(8,128)(2,1)S(1)}, u32[]{:S(2)}, u32[]{:S(2)}) %collective-permute-start.9) | collective-permute-done | bytes 131104 | tf_op jit(solution)/shard_map/ppermute | solution.py:925
  39.0 2.9 collective-permute-done.13.refs_6_
  55.5 24.3 %all-gather.3.cloned.1.call-done.w_ref.v_ref.refs_11_ = bf16[1024,1536]{1,0:T(8,128)(2,1)} async-done(((bf16[128,1536]{1,0:T(8,128)(2,1)}), bf16[1024,1536]{1,0:T(8,128)(2,1)}) %all-gather.3.cloned.1.call-update) | async-done | bytes 3145744 | tf_op jit(solution)/shard_map/all_gather | solution.py:1006
  87.7 3.4 token_proj.1
  91.1 3.0 token_attend0.1
  94.1 2.9 state_attend0.1
  98.8 7.0 %collective-permute-done.6.refs_2_ = bf16[512,256]{1,0:T(8,128)(2,1)S(1)} collective-permute-done((bf16[512,256]{1,0:T(8,128)(2,1)S(1)}, bf16[512,256]{1,0:T(8,128)(2,1)S(1)}, u32[]{:S(2)}, u32[]{:S(2)}) %collective-permute-start.6) | collective-permute-done | bytes 262176 | tf_op jit(solution)/shard_map/ppermute | solution.py:906
  107.4 5.5 %update0.1 = (f32[512,1024]{1,0:T(8,128)S(1)}, bf16[512,1024]{1,0:T(8,128)(2,1)S(1)}, bf16[512,768]{1,0:T(8,128)(2,1)S(1)}) custom-call(s32[5]{0:T(128)S(1)} %stack.40.s, bf16[512,256]{1,0:T(8,128)(2,1)S(1)} %get-tuple-element.156.refs_0_.refs_8_, bf16[512,256]{1,0:T(8,128)(2,1)S(1)} %collective-permute-done.5.refs_1_, ...), custom_call_target="tpu_custom_call" | custom-call | flops 234881024 | bytes 1024 | tf_op jit(solution)/shard_map/update0/pallas_call | solution.py:51
  112.9 3.7 token_attend1.1
  118.7 2.9 state_attend1.1
  121.6 3.5 collective-permute-done.20.refs_2_
  125.1 3.6 out0.1
  130.0 3.9 %out1.1 = (f32[512,1024]{1,0:T(8,128)S(1)}, bf16[512,1024]{1,0:T(8,128)(2,1)S(1)}) custom-call(s32[5]{0:T(128)S(1)} %stack.40.s, bf16[512,256]{1,0:T(8,128)(2,1)S(1)} %get-tuple-element.166.refs_0_.refs_6_, bf16[512,256]{1,0:T(8,128)(2,1)S(1)} %collective-permute-done.19.refs_1_, bf16[512,256]{1,0:T(8,128)(2,1)S(1)} %collective-permute-done.20.refs_2_, ...), custom_call_target="tpu_custom_call" | custom-call | flops 134217728 | bytes 1024 | tf_op jit(solution)/shard_map/out1/pallas_call | solution.py:51
  136.3 18.2 %all-gather.5.cloned.1.call-done.v_ref.up_ref.refs_8_ = bf16[1024,2048]{1,0:T(8,128)(2,1)} async-done(((bf16[128,2048]{1,0:T(8,128)(2,1)}), bf16[1024,2048]{1,0:T(8,128)(2,1)}) %all-gather.5.cloned.1.call-update) | async-done | bytes 4194320 | tf_op jit(solution)/shard_map/all_gather | solution.py:1028
  158.0 4.2 %dense0.1 = (bf16[512,1024]{1,0:T(8,128)(2,1)S(1)}, bf16[512,1024]{1,0:T(8,128)(2,1)S(1)}, bf16[512,1024]{1,0:T(8,128)(2,1)S(1)}) custom-call(s32[5]{0:T(128)S(1)} %stack.40.s, bf16[512,1024]{1,0:T(8,128)(2,1)S(1)} %copy-done.46, bf16[1024,2048]{1,0:T(8,128)(2,1)S(1)} %copy-done, bf16[1024,1024]{1,0:T(8,128)(2,1)S(1)} %down_turn.1.down_ref), custom_call_target="tpu_custom_call" | custom-call | flops 268435456 | bytes 1024 | tf_op jit(solution)/shard_map/dense0/pallas_call | solution.py:51
  167.4 4.4 %dense1.1 = (bf16[512,1024]{1,0:T(8,128)(2,1)S(1)}, bf16[512,1024]{1,0:T(8,128)(2,1)S(1)}, bf16[512,1024]{1,0:T(8,128)(2,1)S(1)}) custom-call(s32[5]{0:T(128)S(1)} %stack.40.s, bf16[512,1024]{1,0:T(8,128)(2,1)S(1)} %copy-done.48, bf16[1024,2048]{1,0:T(8,128)(2,1)S(1)} %copy-done.1, bf16[1024,1024]{1,0:T(8,128)(2,1)S(1)} %down_turn.1.down_ref), custom_call_target="tpu_custom_call" | custom-call | flops 268435456 | bytes 1024 | tf_op jit(solution)/shard_map/dense1/pallas_call | solution.py:51
  171.9 8.0 %collective-permute-done.23.refs_1_ = bf16[256,1024]{1,0:T(8,128)(2,1)S(1)} collective-permute-done((bf16[256,1024]{1,0:T(8,128)(2,1)S(1)}, bf16[256,1024]{1,0:T(8,128)(2,1)S(1)}, u32[]{:S(2)}, u32[]{:S(2)}) %collective-permute-start.23) | collective-permute-done | bytes 524320 | tf_op jit(solution)/shard_map/ppermute | solution.py:980
  182.5 4.2 %back0.1 = (bf16[512,1024]{1,0:T(8,128)(2,1)S(1)}, bf16[512,1024]{1,0:T(8,128)(2,1)S(1)}, f32[1,1024]{1,0:T(1,128)S(1)}, bf16[512,1024]{1,0:T(8,128)(2,1)S(1)}) custom-call(s32[5]{0:T(128)S(1)} %stack.40.s, bf16[512,1024]{1,0:T(8,128)(2,1)S(1)} %get-tuple-element.174.refs_0_, bf16[256,1024]{1,0:T(8,128)(2,1)S(1)} %collective-permute-done.23.refs_1_, ...), custom_call_target="tpu_custom_call" | custom-call | flops 268435456 | bytes 1024 | tf_op jit(solution)/shard_map/back0/pallas_call | solution.py:51
  189.0 4.4 %state_back1.1 = (bf16[512,256]{1,0:T(8,128)(2,1)S(1)}, f32[512,256]{1,0:T(8,128)S(1)}, f32[512,256]{1,0:T(8,128)S(1)}, f32[512,256]{1,0:T(8,128)S(1)}, f32[512,256]{1,0:T(8,128)S(1)}) custom-call(s32[5]{0:T(128)S(1)} %stack.40.s, bf16[512,768]{1,0:T(8,128)(2,1)S(1)} %copy-done.15, bf16[1024,768]{1,0:T(8,128)(2,1)S(1)} %get-tuple-element.152.refs_0_.refs_1_, ...), custom_call_target="tpu_custom_call" | custom-call | flops 335544320 | bytes 1024 | tf_op jit(solution)/shard_map/state_back1/pallas_call | solution.py:51
  197.3 4.2 %back1.1 = (bf16[512,1024]{1,0:T(8,128)(2,1)S(1)}, bf16[512,1024]{1,0:T(8,128)(2,1)S(1)}, f32[1,1024]{1,0:T(1,128)S(1)}, bf16[512,1024]{1,0:T(8,128)(2,1)S(1)}) custom-call(s32[5]{0:T(128)S(1)} %stack.40.s, bf16[512,1024]{1,0:T(8,128)(2,1)S(1)} %get-tuple-element.184.refs_0_, bf16[256,1024]{1,0:T(8,128)(2,1)S(1)} %collective-permute-done.26.refs_1_, ...), custom_call_target="tpu_custom_call" | custom-call | flops 268435456 | bytes 1024 | tf_op jit(solution)/shard_map/back1/pallas_call | solution.py:51
  202.5 7.2 %dense_grads.1 = bf16[1024,2048]{1,0:T(8,128)(2,1)} custom-call(s32[5]{0:T(128)S(1)} %stack.40.s, bf16[512,1024]{1,0:T(8,128)(2,1)S(1)} %copy-done.46, bf16[512,1024]{1,0:T(8,128)(2,1)S(1)} %get-tuple-element.205.refs_1_, bf16[512,1024]{1,0:T(8,128)(2,1)S(1)} %copy-done.48, bf16[512,1024]{1,0:T(8,128)(2,1)S(1)} %get-tuple-element.206.refs_3_, ...), custom_call_target="tpu_custom_call" | custom-call | flops 536870912 | bytes 1024 | tf_op jit(solution)/shard_map/dense_grads/pallas_call | solution.py:619
  213.0 12.6 %collective-permute-done.29.refs_1_ = bf16[256,1024]{1,0:T(8,128)(2,1)S(1)} collective-permute-done((bf16[256,1024]{1,0:T(8,128)(2,1)}, bf16[256,1024]{1,0:T(8,128)(2,1)S(1)}, u32[]{:S(2)}, u32[]{:S(2)}) %collective-permute-start.29) | collective-permute-done | bytes 524320 | tf_op jit(solution)/shard_map/ppermute | solution.py:980
  235.3 4.5 %token_back0.1 = (bf16[512,256]{1,0:T(8,128)(2,1)S(1)}, f32[512,256]{1,0:T(8,128)S(1)}, f32[512,256]{1,0:T(8,128)S(1)}, f32[512,256]{1,0:T(8,128)S(1)}, f32[512,256]{1,0:T(8,128)S(1)}) custom-call(s32[5]{0:T(128)S(1)} %stack.40.s, bf16[1024,768]{1,0:T(8,128)(2,1)S(1)} %get-tuple-element.152.refs_0_.refs_1_, bf16[512,768]{1,0:T(8,128)(2,1)S(1)} %copy-done.18, ...), custom_call_target="tpu_custom_call" | custom-call | flops 335544320 | bytes 1024 | tf_op jit(solution)/shard_map/token_back0/pallas_call | solution.py:51
  239.9 2.5 collective-permute-done.32.refs_1_
  244.4 2.3 out_back1.1
  249.3 5.6 %token_back1.1 = (bf16[512,256]{1,0:T(8,128)(2,1)S(1)}, f32[512,256]{1,0:T(8,128)S(1)}, f32[512,256]{1,0:T(8,128)S(1)}, bf16[512,256]{1,0:T(8,128)(2,1)S(1)}, bf...) custom-call(s32[5]{0:T(128)S(1)} %stack.40.s, ...), custom_call_target="tpu_custom_call" | custom-call | flops 503316480 | bytes 1024 | tf_op jit(solution)/shard_map/token_back1/pallas_call | solution.py:51
  257.8 2.6 collective-permute-done.35.b_ref
  265.5 4.8 %update_last.1 = f32[512,1024]{1,0:T(8,128)} custom-call(s32[5]{0:T(128)S(1)} %stack.40.s, bf16[512,256]{1,0:T(8,128)(2,1)S(1)} %copy-done.73, bf16[512,256]{1,0:T(8,128)(2,1)S(1)} %collective-permute-done.37.refs_1_, bf16[512,256]{1,0:T(8,128)(2,1)S(1)} %collective-permute-done.34.refs_2_, bf16[512,256]{1,0:T(8,128)(2,1)S(1)} %collective-permute-done.38.refs_3_, ...), custom_call_target="tpu_custom_call" | custom-call | flops 134217728 | bytes 1024 | tf_op jit(solution)/shard_map/update_last/pallas_call | solution.py:51
  270.3 5.2 %collective-permute-done.36.refs_1_ = bf16[256,1024]{1,0:T(8,128)(2,1)S(1)} collective-permute-done((bf16[256,1024]{1,0:T(8,128)(2,1)S(1)}, bf16[256,1024]{1,0:T(8,128)(2,1)S(1)}, u32[]{:S(2)}, u32[]{:S(2)}) %collective-permute-start.36) | collective-permute-done | bytes 524320 | tf_op jit(solution)/shard_map/ppermute | solution.py:980
  277.4 2.4 chain_back1.1
  282.1 4.4 %state_back0.1 = (bf16[512,256]{1,0:T(8,128)(2,1)S(1)}, bf16[512,256]{1,0:T(8,128)(2,1)S(1)}, bf16[512,256]{1,0:T(8,128)(2,1)S(1)}, bf16[512,256]{1,0:T(8,128)(2,1)S(1)}, bf16[512,256]{1,0:T(8,128)(2,1)S(1)}) custom-call(s32[5]{0:T(128)S(1)} %stack.40.s, bf16[512,768]{1,0:T(8,128)(2,1)S(1)} %copy-done.18, ...), custom_call_target="tpu_custom_call" | custom-call | flops 335544320 | bytes 1024 | tf_op jit(solution)/shard_map/state_back0/pallas_call | solution.py:51
  286.5 6.6 %late_grads.1 = bf16[1024,1280]{1,0:T(8,128)(2,1)} custom-call(s32[5]{0:T(128)S(1)} %stack.40.s, bf16[512,1024]{1,0:T(8,128)(2,1)S(1)} %copy-done.20, bf16[512,256]{1,0:T(8,128)(2,1)S(1)} %get-tuple-element.250.refs_1_.refs_0_, bf16[512,1024]{1,0:T(8,128)(2,1)S(1)} %copy-done.22, bf16[512,256]{1,0:T(8,128)(2,1)S(1)} %get-tuple-element.214.refs_0_.refs_3_, ...), custom_call_target="tpu_custom_call" | custom-call | flops 335544320 | bytes 1024 | tf_op jit(solution)/shard_map/late_grads/pallas_call | solution.py:619
  306.6 3.5 rest_grads.1
  311.7 2.7 collective-permute-start.43
  316.7 2.3 collective-permute-done.46.refs_1_
  319.1 15.0 %collective-permute-done.44.got_ref = bf16[512,768]{1,0:T(8,128)(2,1)S(1)} collective-permute-done((bf16[512,768]{1,0:T(8,128)(2,1)S(1)}, bf16[512,768]{1,0:T(8,128)(2,1)S(1)}, u32[]{:S(2)}, u32[]{:S(2)}) %collective-permute-start.44) | collective-permute-done | bytes 786464 | tf_op jit(solution)/shard_map/ppermute | solution.py:928
  336.3 2.4 collective-permute-start.49
  340.2 2.4 input_rows.1
  342.6 3.2 chain_back0.1
  345.9 6.3 %collective-permute-done.49.refs_1_ = bf16[128,768]{1,0:T(8,128)(2,1)S(1)} collective-permute-done((bf16[128,768]{1,0:T(8,128)(2,1)S(1)}, bf16[128,768]{1,0:T(8,128)(2,1)S(1)}, u32[]{:S(2)}, u32[]{:S(2)}) %collective-permute-start.49) | collective-permute-done | bytes 196640 | tf_op jit(solution)/shard_map/ppermute | solution.py:925
  354.5 2.6 collective-permute-done.52
  357.5 3.3 collective-permute-done.53
  360.9 4.7 %collective-permute-start.54 = (f32[4,1024]{1,0:T(4,128)S(1)}, f32[4,1024]{1,0:T(4,128)S(1)}, u32[]{:S(2)}, u32[]{:S(2)}) collective-permute-start(f32[4,1024]{1,0:T(4,128)S(1)} %add.86), channel_id=1, source_target_pairs={{0,2},{1,3},{2,0},{3,1},{4,6},{5,7},{6,4},{7,5},{8,10},{9,11},{10,... | collective-permute-start | bytes 49160 | tf_op jit(solution)/shard_map/ppermute | solution.py:994
  370.3 2.6 collective-permute-done.55
  (354 shorter events, 119.3 us)
Async XLA Ops:
  7.2 72.6 %all-gather.3.cloned.1.call-start = ((), (), s32[]{:S(2)}) async-start(), calls=%async_computation.2 | async-start | bytes 3538944 | tf_op jit(solution)/shard_map/all_gather | solution.py:1006
  9.7 144.7 %all-gather.5.cloned.1.call-start = ((), (), s32[]{:S(2)}) async-start(), calls=%async_computation.3 | async-start | bytes 4718592 | tf_op jit(solution)/shard_map/all_gather | solution.py:1028
  12.7 33.4 %collective-permute-start.1 = (bf16[512,1024]{1,0:T(8,128)(2,1)S(1)}, bf16[512,1024]{1,0:T(8,128)(2,1)}, u32[]{:S(2)}, u32[]{:S(2)}) collective-permute-start(bf16[512,1024]{1,0:T(8,128)(2,1)S(1)} %get-tuple-element.150.refs_0_), channel_id=1, source_target_pairs={{0,16},{8,24},{16,0},{24,8},{1,17},{9,25},{17,1},{25,9},{2,18},{10... | collective-permute-start | bytes 3145736 | tf_op jit(solution)/shard_map/ppermute | solution.py:906
  15.7 8.4 %collective-permute-start.10 = (bf16[128,512]{1,0:T(8,128)(2,1)S(1)}, bf16[128,512]{1,0:T(8,128)(2,1)S(1)}, u32[]{:S(2)}, u32[]{:S(2)}) collective-permute-start(bf16[128,512]{1,0:T(8,128)(2,1)S(1)} %get-tuple-element.158.refs_0_), channel_id=1, source_target_pairs={{0,6},{1,7},{2,0},{3,1},{4,2},{5,3},{6,4},{7,5},{8,14},{9,15},{10,... | collective-permute-start | bytes 393224 | tf_op jit(solution)/shard_map/ppermute | solution.py:925
  19.3 17.7 %collective-permute-start.9 = (bf16[128,512]{1,0:T(8,128)(2,1)S(1)}, bf16[128,512]{1,0:T(8,128)(2,1)S(1)}, u32[]{:S(2)}, u32[]{:S(2)}) collective-permute-start(bf16[128,512]{1,0:T(8,128)(2,1)S(1)} %get-tuple-element.158.refs_0_), channel_id=1, source_target_pairs={{0,4},{1,5},{2,6},{3,7},{4,0},{5,1},{6,2},{7,3},{8,12},{9,13},{10,... | collective-permute-start | bytes 393224 | tf_op jit(solution)/shard_map/ppermute | solution.py:925
  19.3 19.3 %collective-permute-start.8 = (bf16[128,512]{1,0:T(8,128)(2,1)S(1)}, bf16[128,512]{1,0:T(8,128)(2,1)S(1)}, u32[]{:S(2)}, u32[]{:S(2)}) collective-permute-start(bf16[128,512]{1,0:T(8,128)(2,1)S(1)} %get-tuple-element.158.refs_0_), channel_id=1, source_target_pairs={{0,2},{1,3},{2,4},{3,5},{4,6},{5,7},{6,0},{7,1},{8,10},{9,11},{10,... | collective-permute-start | bytes 393224 | tf_op jit(solution)/shard_map/ppermute | solution.py:925
  20.3 18.7 %collective-permute-start.11 = (bf16[128,512]{1,0:T(8,128)(2,1)S(1)}, bf16[128,512]{1,0:T(8,128)(2,1)S(1)}, u32[]{:S(2)}, u32[]{:S(2)}) collective-permute-start(bf16[128,512]{1,0:T(8,128)(2,1)S(1)} %get-tuple-element.158.refs_0_), channel_id=1, source_target_pairs={{0,1},{1,0},{2,3},{3,2},{4,5},{5,4},{6,7},{7,6},{8,9},{9,8},{10,11... | collective-permute-start | bytes 393224 | tf_op jit(solution)/shard_map/ppermute | solution.py:928
  24.0 15.0 %collective-permute-start.14 = (bf16[128,512]{1,0:T(8,128)(2,1)S(1)}, bf16[128,512]{1,0:T(8,128)(2,1)S(1)}, u32[]{:S(2)}, u32[]{:S(2)}) collective-permute-start(bf16[128,512]{1,0:T(8,128)(2,1)S(1)} %collective-permute-done.10.refs_3_), channel_id=1, source_target_pairs={{0,1},{1,0},{2,3},{3,2},{4,5},{5,4},{6,7},{7,6},{8,9},{9,8},{10,11... | collective-permute-start | bytes 393224 | tf_op jit(solution)/shard_map/ppermute | solution.py:928
  37.0 5.0 %collective-permute-start.13 = (bf16[128,512]{1,0:T(8,128)(2,1)S(1)}, bf16[128,512]{1,0:T(8,128)(2,1)S(1)}, u32[]{:S(2)}, u32[]{:S(2)}) collective-permute-start(bf16[128,512]{1,0:T(8,128)(2,1)S(1)} %collective-permute-done.9.refs_2_), channel_id=1, source_target_pairs={{0,1},{1,0},{2,3},{3,2},{4,5},{5,4},{6,7},{7,6},{8,9},{9,8},{10,11... | collective-permute-start | bytes 393224 | tf_op jit(solution)/shard_map/ppermute | solution.py:928
  38.5 5.0 %collective-permute-start.12 = (bf16[128,512]{1,0:T(8,128)(2,1)S(1)}, bf16[128,512]{1,0:T(8,128)(2,1)S(1)}, u32[]{:S(2)}, u32[]{:S(2)}) collective-permute-start(bf16[128,512]{1,0:T(8,128)(2,1)S(1)} %collective-permute-done.8.refs_1_), channel_id=1, source_target_pairs={{0,1},{1,0},{2,3},{3,2},{4,5},{5,4},{6,7},{7,6},{8,9},{9,8},{10,11... | collective-permute-start | bytes 393224 | tf_op jit(solution)/shard_map/ppermute | solution.py:928
  46.1 328.8 %reduce-scatter.5.cloned.1.call-start = ((), (), s32[]{:S(2)}) async-start(), calls=%async_computation.5 | async-start | bytes 4718592 | tf_op jit(solution)/shard_map/reduce_scatter | solution.py:1212
  46.3 4.4 %collective-permute-start.2 = (bf16[512,1024]{1,0:T(8,128)(2,1)}, bf16[512,1024]{1,0:T(8,128)(2,1)}, u32[]{:S(2)}, u32[]{:S(2)}) collective-permute-start(bf16[512,1024]{1,0:T(8,128)(2,1)} %collective-permute-done.1.refs_2_), channel_id=1, source_target_pairs={{0,8},{8,0},{16,24},{24,16},{1,9},{9,1},{17,25},{25,17},{2,10},{10... | collective-permute-start | bytes 3145736 | tf_op jit(solution)/shard_map/ppermute | solution.py:903
  47.0 47.0 %collective-permute-start.16 = (bf16[512,1024]{1,0:T(8,128)(2,1)}, bf16[512,1024]{1,0:T(8,128)(2,1)}, u32[]{:S(2)}, u32[]{:S(2)}) collective-permute-start(bf16[512,1024]{1,0:T(8,128)(2,1)} %mid_turn.1.refs_4_), channel_id=1, source_target_pairs={{0,16},{8,24},{16,0},{24,8},{1,17},{9,25},{17,1},{25,9},{2,18},{10... | collective-permute-start | bytes 3145736 | tf_op jit(solution)/shard_map/ppermute | solution.py:906
  49.0 58.3 %collective-permute-start.15 = (bf16[512,1024]{1,0:T(8,128)(2,1)}, bf16[512,1024]{1,0:T(8,128)(2,1)}, u32[]{:S(2)}, u32[]{:S(2)}) collective-permute-start(bf16[512,1024]{1,0:T(8,128)(2,1)} %mid_turn.1.refs_4_), channel_id=1, source_target_pairs={{0,8},{8,0},{16,24},{24,16},{1,9},{9,1},{17,25},{25,17},{2,10},{10... | collective-permute-start | bytes 3145736 | tf_op jit(solution)/shard_map/ppermute | solution.py:903
  94.1 13.3 %collective-permute-start.17 = (bf16[512,1024]{1,0:T(8,128)(2,1)}, bf16[512,1024]{1,0:T(8,128)(2,1)S(1)}, u32[]{:S(2)}, u32[]{:S(2)}) collective-permute-start(bf16[512,1024]{1,0:T(8,128)(2,1)} %collective-permute-done.16.refs_6_), channel_id=1, source_target_pairs={{0,8},{8,0},{16,24},{24,16},{1,9},{9,1},{17,25},{25,17},{2,10},{10... | collective-permute-start | bytes 3145736 | tf_op jit(solution)/shard_map/ppermute | solution.py:903
  97.0 8.8 %collective-permute-start.6 = (bf16[512,256]{1,0:T(8,128)(2,1)S(1)}, bf16[512,256]{1,0:T(8,128)(2,1)S(1)}, u32[]{:S(2)}, u32[]{:S(2)}) collective-permute-start(bf16[512,256]{1,0:T(8,128)(2,1)S(1)} %get-tuple-element.156.refs_0_.refs_8_), channel_id=1, source_target_pairs={{0,16},{8,24},{16,0},{24,8},{1,17},{9,25},{17,1},{25,9},{2,18},{10... | collective-permute-start | bytes 786440 | tf_op jit(solution)/shard_map/ppermute | solution.py:906
  98.6 8.7 %collective-permute-start.5 = (bf16[512,256]{1,0:T(8,128)(2,1)S(1)}, bf16[512,256]{1,0:T(8,128)(2,1)S(1)}, u32[]{:S(2)}, u32[]{:S(2)}) collective-permute-start(bf16[512,256]{1,0:T(8,128)(2,1)S(1)} %get-tuple-element.156.refs_0_.refs_8_), channel_id=1, source_target_pairs={{0,8},{8,0},{16,24},{24,16},{1,9},{9,1},{17,25},{25,17},{2,10},{10... | collective-permute-start | bytes 786440 | tf_op jit(solution)/shard_map/ppermute | solution.py:903
  105.8 12.8 %collective-permute-start.4 = (bf16[512,256]{1,0:T(8,128)(2,1)S(1)}, bf16[512,256]{1,0:T(8,128)(2,1)S(1)}, u32[]{:S(2)}, u32[]{:S(2)}) collective-permute-start(bf16[512,256]{1,0:T(8,128)(2,1)S(1)} %get-tuple-element.155.refs_0_.refs_4_), channel_id=1, source_target_pairs={{0,16},{8,24},{16,0},{24,8},{1,17},{9,25},{17,1},{25,9},{2,18},{10... | collective-permute-start | bytes 786440 | tf_op jit(solution)/shard_map/ppermute | solution.py:906
  116.6 8.4 %collective-permute-start.20 = (bf16[512,256]{1,0:T(8,128)(2,1)S(1)}, bf16[512,256]{1,0:T(8,128)(2,1)S(1)}, u32[]{:S(2)}, u32[]{:S(2)}) collective-permute-start(bf16[512,256]{1,0:T(8,128)(2,1)S(1)} %get-tuple-element.166.refs_0_.refs_6_), channel_id=1, source_target_pairs={{0,16},{8,24},{16,0},{24,8},{1,17},{9,25},{17,1},{25,9},{2,18},{10... | collective-permute-start | bytes 786440 | tf_op jit(solution)/shard_map/ppermute | solution.py:906
  118.1 6.9 %collective-permute-start.3 = (bf16[512,256]{1,0:T(8,128)(2,1)S(1)}, bf16[512,256]{1,0:T(8,128)(2,1)S(1)}, u32[]{:S(2)}, u32[]{:S(2)}) collective-permute-start(bf16[512,256]{1,0:T(8,128)(2,1)S(1)} %get-tuple-element.155.refs_0_.refs_4_), channel_id=1, source_target_pairs={{0,8},{8,0},{16,24},{24,16},{1,9},{9,1},{17,25},{25,17},{2,10},{10... | collective-permute-start | bytes 786440 | tf_op jit(solution)/shard_map/ppermute | solution.py:903
  118.1 11.9 %collective-permute-start.19 = (bf16[512,256]{1,0:T(8,128)(2,1)S(1)}, bf16[512,256]{1,0:T(8,128)(2,1)S(1)}, u32[]{:S(2)}, u32[]{:S(2)}) collective-permute-start(bf16[512,256]{1,0:T(8,128)(2,1)S(1)} %get-tuple-element.166.refs_0_.refs_6_), channel_id=1, source_target_pairs={{0,8},{8,0},{16,24},{24,16},{1,9},{9,1},{17,25},{25,17},{2,10},{10... | collective-permute-start | bytes 786440 | tf_op jit(solution)/shard_map/ppermute | solution.py:903
  118.7 6.4 %collective-permute-start.18 = (bf16[512,256]{1,0:T(8,128)(2,1)S(1)}, bf16[512,256]{1,0:T(8,128)(2,1)S(1)}, u32[]{:S(2)}, u32[]{:S(2)}) collective-permute-start(bf16[512,256]{1,0:T(8,128)(2,1)S(1)} %collective-permute-done.4.refs_2_), channel_id=1, source_target_pairs={{0,8},{8,0},{16,24},{24,16},{1,9},{9,1},{17,25},{25,17},{2,10},{10... | collective-permute-start | bytes 786440 | tf_op jit(solution)/shard_map/ppermute | solution.py:903
  125.1 4.9 %collective-permute-start.21 = (bf16[512,256]{1,0:T(8,128)(2,1)S(1)}, bf16[512,256]{1,0:T(8,128)(2,1)S(1)}, u32[]{:S(2)}, u32[]{:S(2)}) collective-permute-start(bf16[512,256]{1,0:T(8,128)(2,1)S(1)} %collective-permute-done.20.refs_2_), channel_id=1, source_target_pairs={{0,8},{8,0},{16,24},{24,16},{1,9},{9,1},{17,25},{25,17},{2,10},{10... | collective-permute-start | bytes 786440 | tf_op jit(solution)/shard_map/ppermute | solution.py:903
  165.9 14.0 %collective-permute-start.23 = (bf16[256,1024]{1,0:T(8,128)(2,1)S(1)}, bf16[256,1024]{1,0:T(8,128)(2,1)S(1)}, u32[]{:S(2)}, u32[]{:S(2)}) collective-permute-start(bf16[256,1024]{1,0:T(8,128)(2,1)S(1)} %get-tuple-element.175), channel_id=1, source_target_pairs={{0,16},{8,24},{16,0},{24,8},{1,17},{9,25},{17,1},{25,9},{2,18},{10... | collective-permute-start | bytes 1572872 | tf_op jit(solution)/shard_map/ppermute | solution.py:980
  171.8 8.1 %collective-permute-start.25 = (bf16[512,1024]{1,0:T(8,128)(2,1)S(1)}, bf16[512,1024]{1,0:T(8,128)(2,1)S(1)}, u32[]{:S(2)}, u32[]{:S(2)}) collective-permute-start(bf16[512,1024]{1,0:T(8,128)(2,1)S(1)} %get-tuple-element.183.a_ref), channel_id=1, source_target_pairs={{0,8},{8,0},{16,24},{24,16},{1,9},{9,1},{17,25},{25,17},{2,10},{10... | collective-permute-start | bytes 3145736 | tf_op jit(solution)/shard_map/ppermute | solution.py:903
  180.9 14.4 %collective-permute-start.26 = (bf16[256,1024]{1,0:T(8,128)(2,1)S(1)}, bf16[256,1024]{1,0:T(8,128)(2,1)S(1)}, u32[]{:S(2)}, u32[]{:S(2)}) collective-permute-start(bf16[256,1024]{1,0:T(8,128)(2,1)S(1)} %get-tuple-element.185), channel_id=1, source_target_pairs={{0,16},{8,24},{16,0},{24,8},{1,17},{9,25},{17,1},{25,9},{2,18},{10... | collective-permute-start | bytes 1572872 | tf_op jit(solution)/shard_map/ppermute | solution.py:980
  186.7 8.6 %collective-permute-start.28 = (bf16[512,1024]{1,0:T(8,128)(2,1)S(1)}, bf16[512,1024]{1,0:T(8,128)(2,1)S(1)}, u32[]{:S(2)}, u32[]{:S(2)}) collective-permute-start(bf16[512,1024]{1,0:T(8,128)(2,1)S(1)} %get-tuple-element.193.a_ref), channel_id=1, source_target_pairs={{0,8},{8,0},{16,24},{24,16},{1,9},{9,1},{17,25},{25,17},{2,10},{10... | collective-permute-start | bytes 3145736 | tf_op jit(solution)/shard_map/ppermute | solution.py:903
  210.8 166.2 %reduce-scatter.3.cloned.1.call-start = ((), (), s32[]{:S(2)}) async-start(), calls=%async_computation.4 | async-start | bytes 2949120 | tf_op jit(solution)/shard_map/reduce_scatter | solution.py:1267
  210.9 14.7 %collective-permute-start.31 = (bf16[512,1024]{1,0:T(8,128)(2,1)}, bf16[512,1024]{1,0:T(8,128)(2,1)S(1)}, u32[]{:S(2)}, u32[]{:S(2)}) collective-permute-start(bf16[512,1024]{1,0:T(8,128)(2,1)} %copy-done.79), channel_id=1, source_target_pairs={{0,8},{8,0},{16,24},{24,16},{1,9},{9,1},{17,25},{25,17},{2,10},{10... | collective-permute-start | bytes 3145736 | tf_op jit(solution)/shard_map/ppermute | solution.py:903
  211.5 14.1 %collective-permute-start.29 = (bf16[256,1024]{1,0:T(8,128)(2,1)}, bf16[256,1024]{1,0:T(8,128)(2,1)S(1)}, u32[]{:S(2)}, u32[]{:S(2)}) collective-permute-start(bf16[256,1024]{1,0:T(8,128)(2,1)} %copy-done.97), channel_id=1, source_target_pairs={{0,16},{8,24},{16,0},{24,8},{1,17},{9,25},{17,1},{25,9},{2,18},{10... | collective-permute-start | bytes 1572872 | tf_op jit(solution)/shard_map/ppermute | solution.py:980
  225.6 4.0 %collective-permute-start.30 = (bf16[256,1024]{1,0:T(8,128)(2,1)S(1)}, bf16[256,1024]{1,0:T(8,128)(2,1)S(1)}, u32[]{:S(2)}, u32[]{:S(2)}) collective-permute-start(bf16[256,1024]{1,0:T(8,128)(2,1)S(1)} %collective-permute-done.29.refs_1_), channel_id=1, source_target_pairs={{0,8},{8,0},{16,24},{24,16},{1,9},{9,1},{17,25},{25,17},{2,10},{10... | collective-permute-start | bytes 1572872 | tf_op jit(solution)/shard_map/ppermute | solution.py:903
  228.0 14.4 %collective-permute-start.32 = (bf16[256,1024]{1,0:T(8,128)(2,1)S(1)}, bf16[256,1024]{1,0:T(8,128)(2,1)S(1)}, u32[]{:S(2)}, u32[]{:S(2)}) collective-permute-start(bf16[256,1024]{1,0:T(8,128)(2,1)S(1)} %get-tuple-element.210), channel_id=1, source_target_pairs={{0,16},{8,24},{16,0},{24,8},{1,17},{9,25},{17,1},{25,9},{2,18},{10... | collective-permute-start | bytes 1572872 | tf_op jit(solution)/shard_map/ppermute | solution.py:980
  247.7 8.3 %collective-permute-start.34 = (bf16[512,256]{1,0:T(8,128)(2,1)S(1)}, bf16[512,256]{1,0:T(8,128)(2,1)S(1)}, u32[]{:S(2)}, u32[]{:S(2)}) collective-permute-start(bf16[512,256]{1,0:T(8,128)(2,1)S(1)} %copy-done.73), channel_id=1, source_target_pairs={{0,16},{8,24},{16,0},{24,8},{1,17},{9,25},{17,1},{25,9},{2,18},{10... | collective-permute-start | bytes 786440 | tf_op jit(solution)/shard_map/ppermute | solution.py:906
  261.4 14.0 %collective-permute-start.36 = (bf16[256,1024]{1,0:T(8,128)(2,1)S(1)}, bf16[256,1024]{1,0:T(8,128)(2,1)S(1)}, u32[]{:S(2)}, u32[]{:S(2)}) collective-permute-start(bf16[256,1024]{1,0:T(8,128)(2,1)S(1)} %get-tuple-element.223), channel_id=1, source_target_pairs={{0,16},{8,24},{16,0},{24,8},{1,17},{9,25},{17,1},{25,9},{2,18},{10... | collective-permute-start | bytes 1572872 | tf_op jit(solution)/shard_map/ppermute | solution.py:980
  301.4 9.3 %collective-permute-start.41 = (bf16[512,1024]{1,0:T(8,128)(2,1)S(1)}, bf16[512,1024]{1,0:T(8,128)(2,1)S(1)}, u32[]{:S(2)}, u32[]{:S(2)}) collective-permute-start(bf16[512,1024]{1,0:T(8,128)(2,1)S(1)} %copy-done.36), channel_id=1, source_target_pairs={{0,8},{8,0},{16,24},{24,16},{1,9},{9,1},{17,25},{25,17},{2,10},{10... | collective-permute-start | bytes 3145736 | tf_op jit(solution)/shard_map/ppermute | solution.py:903
  303.6 10.8 %collective-permute-start.40 = (bf16[512,1024]{1,0:T(8,128)(2,1)S(1)}, bf16[512,1024]{1,0:T(8,128)(2,1)S(1)}, u32[]{:S(2)}, u32[]{:S(2)}) collective-permute-start(bf16[512,1024]{1,0:T(8,128)(2,1)S(1)} %first_back0.1.a_ref), channel_id=1, source_target_pairs={{0,8},{8,0},{16,24},{24,16},{1,9},{9,1},{17,25},{25,17},{2,10},{10... | collective-permute-start | bytes 3145736 | tf_op jit(solution)/shard_map/ppermute | solution.py:903
  304.9 14.1 %collective-permute-start.46 = (bf16[256,1024]{1,0:T(8,128)(2,1)S(1)}, bf16[256,1024]{1,0:T(8,128)(2,1)S(1)}, u32[]{:S(2)}, u32[]{:S(2)}) collective-permute-start(bf16[256,1024]{1,0:T(8,128)(2,1)S(1)} %get-tuple-element.263), channel_id=1, source_target_pairs={{0,16},{8,24},{16,0},{24,8},{1,17},{9,25},{17,1},{25,9},{2,18},{10... | collective-permute-start | bytes 1572872 | tf_op jit(solution)/shard_map/ppermute | solution.py:980
  310.1 23.9 %collective-permute-start.44 = (bf16[512,768]{1,0:T(8,128)(2,1)S(1)}, bf16[512,768]{1,0:T(8,128)(2,1)S(1)}, u32[]{:S(2)}, u32[]{:S(2)}) collective-permute-start(bf16[512,768]{1,0:T(8,128)(2,1)S(1)} %get-tuple-element.259), channel_id=1, source_target_pairs={{0,1},{1,0},{2,3},{3,2},{4,5},{5,4},{6,7},{7,6},{8,9},{9,8},{10,11... | collective-permute-start | bytes 2359304 | tf_op jit(solution)/shard_map/ppermute | solution.py:928
  311.7 27.0 %collective-permute-start.43 = (bf16[256,1024]{1,0:T(8,128)(2,1)S(1)}, bf16[256,1024]{1,0:T(8,128)(2,1)S(1)}, u32[]{:S(2)}, u32[]{:S(2)}) collective-permute-start(bf16[256,1024]{1,0:T(8,128)(2,1)S(1)} %get-tuple-element.242), channel_id=1, source_target_pairs={{0,16},{8,24},{1,17},{9,25},{2,18},{10,26},{3,19},{11,27},{4,20},{... | collective-permute-start | bytes 1572872 | tf_op jit(solution)/shard_map/ppermute | solution.py:980
  315.4 24.7 %collective-permute-start.42 = (bf16[256,1024]{1,0:T(8,128)(2,1)S(1)}, bf16[256,1024]{1,0:T(8,128)(2,1)S(1)}, u32[]{:S(2)}, u32[]{:S(2)}) collective-permute-start(bf16[256,1024]{1,0:T(8,128)(2,1)S(1)} %get-tuple-element.241), channel_id=1, source_target_pairs={{16,0},{24,8},{17,1},{25,9},{18,2},{26,10},{19,3},{27,11},{20,4},{... | collective-permute-start | bytes 1572872 | tf_op jit(solution)/shard_map/ppermute | solution.py:980
  319.0 23.6 %collective-permute-start.47 = (bf16[256,1024]{1,0:T(8,128)(2,1)S(1)}, bf16[256,1024]{1,0:T(8,128)(2,1)S(1)}, u32[]{:S(2)}, u32[]{:S(2)}) collective-permute-start(bf16[256,1024]{1,0:T(8,128)(2,1)S(1)} %collective-permute-done.46.refs_1_), channel_id=1, source_target_pairs={{0,8},{8,0},{16,24},{24,16},{1,9},{9,1},{17,25},{25,17},{2,10},{10... | collective-permute-start | bytes 1572872 | tf_op jit(solution)/shard_map/ppermute | solution.py:903
  334.8 11.1 %collective-permute-start.48 = (bf16[128,768]{1,0:T(8,128)(2,1)S(1)}, bf16[128,768]{1,0:T(8,128)(2,1)S(1)}, u32[]{:S(2)}, u32[]{:S(2)}) collective-permute-start(bf16[128,768]{1,0:T(8,128)(2,1)S(1)} %get-tuple-element.267), channel_id=1, source_target_pairs={{0,2},{1,3},{2,4},{3,5},{4,6},{5,7},{6,0},{7,1},{8,10},{9,11},{10,... | collective-permute-start | bytes 589832 | tf_op jit(solution)/shard_map/ppermute | solution.py:925
  336.3 15.9 %collective-permute-start.49 = (bf16[128,768]{1,0:T(8,128)(2,1)S(1)}, bf16[128,768]{1,0:T(8,128)(2,1)S(1)}, u32[]{:S(2)}, u32[]{:S(2)}) collective-permute-start(bf16[128,768]{1,0:T(8,128)(2,1)S(1)} %get-tuple-element.268), channel_id=1, source_target_pairs={{0,4},{1,5},{2,6},{3,7},{4,0},{5,1},{6,2},{7,3},{8,12},{9,13},{10,... | collective-permute-start | bytes 589832 | tf_op jit(solution)/shard_map/ppermute | solution.py:925
  338.7 13.5 %collective-permute-start.50 = (bf16[128,768]{1,0:T(8,128)(2,1)S(1)}, bf16[128,768]{1,0:T(8,128)(2,1)S(1)}, u32[]{:S(2)}, u32[]{:S(2)}) collective-permute-start(bf16[128,768]{1,0:T(8,128)(2,1)S(1)} %get-tuple-element.269), channel_id=1, source_target_pairs={{0,6},{1,7},{2,0},{3,1},{4,2},{5,3},{6,4},{7,5},{8,14},{9,15},{10,... | collective-permute-start | bytes 589832 | tf_op jit(solution)/shard_map/ppermute | solution.py:925
  353.4 3.7 collective-permute-start.52
  357.1 3.7 collective-permute-start.53
  360.9 6.6 %collective-permute-start.54 = (f32[4,1024]{1,0:T(4,128)S(1)}, f32[4,1024]{1,0:T(4,128)S(1)}, u32[]{:S(2)}, u32[]{:S(2)}) collective-permute-start(f32[4,1024]{1,0:T(4,128)S(1)} %add.86), channel_id=1, source_target_pairs={{0,2},{1,3},{2,0},{3,1},{4,6},{5,7},{6,4},{7,5},{8,10},{9,11},{10,... | collective-permute-start | bytes 49160 | tf_op jit(solution)/shard_map/ppermute | solution.py:994
  367.4 5.5 %collective-permute-start.55 = (f32[4,1024]{1,0:T(4,128)S(1)}, f32[4,1024]{1,0:T(4,128)S(1)}, u32[]{:S(2)}, u32[]{:S(2)}) collective-permute-start(f32[4,1024]{1,0:T(4,128)S(1)} %add.87), channel_id=1, source_target_pairs={{0,4},{1,5},{2,6},{3,7},{4,0},{5,1},{6,2},{7,3},{8,12},{9,13},{10,... | collective-permute-start | bytes 49160 | tf_op jit(solution)/shard_map/ppermute | solution.py:994
  (113 other events, 639.3 us)
Sparse Core Ops, SparseCore 0:
  10.8 68.9 all-gather.2
  82.5 71.8 all-gather.4
  211.0 86.4 reduce-scatter.4
  301.2 75.8 reduce-scatter.2
where the time goes:
time: 393 us; the launch traced here: 387 us
  waiting for transfers between devices  148 us (38%)
  Pallas kernels  136 us (35%)
  starting transfers between devices  49.9 us (13%)
  local copies, waits for them, and re-layouts  33.2 us (8%)
  between operations  17.9 us (5%)
    pallas_call x45, Pallas kernels, launch(): pl.pallas_call(body, in_specs=[pl.BlockSpec(memory_space=pltpu.SMEM)] + [...  115 us
    unnamed x202, local copies, waits for them, and re-layouts  32.7 us
    ppermute x8, waiting for transfers between devices, __init__(): self.far = lax.ppermute(own, 'row', moves)  32.5 us
    all_gather x1, waiting for transfers between devices, per_device(): near = lax.all_gather(near, 'col', axis=0, tiled=True)  24.3 us
    ppermute x6, waiting for transfers between devices, along(): return lax.ppermute(v, 'col', moves)  20.2 us
    ppermute x5, waiting for transfers between devices, across(): return lax.ppermute(v, 'col', [(k, k ^ 1) for k in range(col_devices)])  19.4 us
    all_gather x1, waiting for transfers between devices, per_device(): dense = lax.all_gather(after(far_weights, *held), 'col', axis=0, tiled=True)  18.2 us
    pallas_call x2, Pallas kernels, weight_grads(): pl.pallas_call(body, grid=(features // HALF,), in_specs=[pl.BlockSpec(mem...  13.9 us
  transfers between devices with their start and end apart: 60, of which 30 were waited for; matrix products, arithmetic and copies ran while one was open for 1% of the time, Pallas kernels for 30%

commit v1 on v0

--- a/solution.py
+++ b/solution.py
@@ -589,7 +589,7 @@
     )
 
 
-def weight_grads(idx, groups, name):
+def weight_grads(idx, groups, name, before=None, weight=40):
     features = groups[0][0][0].shape[1]
     inputs, specs, total, flops = [], [], 0, 0
     for parts in groups:
@@ -602,14 +602,21 @@
             )
             flops += 2 * rows * features * right.shape[1]
         total += parts[0][2].shape[1]
+    if before is not None:
+        inputs.append(before)
+        specs.append(pl.BlockSpec((HALF, total), lambda i: (i, 0)))
 
     def body(s, *refs):
         refs = list(refs)
         out_ref = refs.pop()
+        before_ref = refs.pop() if before is not None else None
         at = 0
         for parts in groups:
             size = parts[0][2].shape[1]
-            out = jnp.zeros((HALF, size), f32)
+            if before is None:
+                out = jnp.zeros((HALF, size), f32)
+            else:
+                out = before_ref[:, at : at + size].astype(f32)
             for unused in parts:
                 left, right = refs.pop(0), refs.pop(0)
                 out = out + dot_tn(left[...], right[...])
@@ -625,7 +632,7 @@
         compiler_params=pltpu.CompilerParams(
             dimension_semantics=("arbitrary",), vmem_limit_bytes=20 << 20
         ),
-        cost_estimate=cost(flops, inputs),
+        cost_estimate=cost(weight * flops, inputs),
         name=name,
     )(idx, *inputs)
 
@@ -1127,6 +1134,40 @@
     state_part(nblocks - 1)
     token_pieces[-1] = row_pieces(token_pieces[-1], state_out[-1])
 
+    def state_back_part(b, gos_state, own, free, dtype):
+        return attend_back(
+            idx,
+            (trios[b], 0, 0),
+            state_segments(b, trios[b]),
+            katt,
+            None,
+            heads,
+            state_logs[b],
+            gos_state,
+            [own, free],
+            [dtype, dtype],
+            f"state_back{b}",
+        )
+
+    def token_back_part(b, own, free, dtype, upstream):
+        segments = token_segments(b, trios[b])
+        added = ([[]] if b > 0 else []) + [own, free]
+        dtypes = ([f32] if b > 0 else []) + [dtype, dtype]
+        found = attend_back(
+            idx,
+            (token_heads, b, 0),
+            segments,
+            katt,
+            qatt,
+            heads,
+            token_logs[b],
+            upstream,
+            added,
+            dtypes,
+            f"token_back{b}",
+        )
+        return found[0], found[-4:], (found[1], found[2]) if b > 0 else None
+
     gus = [None] * nblocks
     gms, gas, losses, gps, gos, second_sums = [], [], [], [], [], []
     second_back = []
@@ -1146,49 +1187,18 @@
         if b == 0:
             up_t = turn(after(idx, h), dense, 0, hidden, "up_turn")
             ties.append(up_t)
+        if b == end:
+            late_mid = after(mid, h)
+            gus[end], gos_state = last_update_back(idx, retain2, late_mid, NS, "last_back")
+            state_found = state_back_part(end, gos_state, [], [], f32)
+            ties.append(state_found[0])
         dense_sums.append(RowSum(partial, f"dense_sum{b}", ties=ties))
         order = after(idx, dense_sums[b].chip)
 
-    def state_back_part(b, gos_state, own, free, dtype):
-        return attend_back(
-            idx,
-            (trios[b], 0, 0),
-            state_segments(b, trios[b]),
-            katt,
-            None,
-            heads,
-            state_logs[b],
-            gos_state,
-            [own, free],
-            [dtype, dtype],
-            f"state_back{b}",
-        )
-
-    def token_back_part(b, own, free, dtype, upstream):
-        segments = token_segments(b, trios[b])
-        added = ([[]] if b > 0 else []) + [own, free]
-        dtypes = ([f32] if b > 0 else []) + [dtype, dtype]
-        found = attend_back(
-            idx,
-            (token_heads, b, 0),
-            segments,
-            katt,
-            qatt,
-            heads,
-            token_logs[b],
-            upstream,
-            added,
-            dtypes,
-            f"token_back{b}",
-        )
-        return found[0], found[-4:], (found[1], found[2]) if b > 0 else None
-
-    late_mid = after(mid, dense_sums[end].chip)
-    gus[end], gos_state = last_update_back(idx, retain2, late_mid, NS, "last_back")
-    state_found = state_back_part(end, gos_state, [], [], f32)
+    early_grads, partials = [], []
     ready = teacher_all
     for b in range(nblocks):
-        hides = [hiddens[end]] if b == 0 else [gms[b - 1], state_found[0]]
+        hides = [hiddens[end], state_found[0]] if b == 0 else [gms[b - 1]] + early_grads
         gm, ga, loss, partial = dense_backward(
             idx, b, dense_sums[b].result(*hides), x1s[b], ready, katt, slopes[b], (up_t, dense), f"back{b}"
         )
@@ -1196,15 +1206,23 @@
         gas.append(ga)
         losses.append(loss)
         if b < end:
-            second_back.append(RowSum(partial, f"back_sum{b}"))
-            ready = after(teacher_all, second_back[b].chip)
+            early_grads = [
+                weight_grads(
+                    idx,
+                    [[(second_lows[b], 0, ga)], [(gm, 0, hiddens[b])]],
+                    f"dense_grads{b}",
+                    *early_grads,
+                )
+            ]
+        partials.append(partial)
+        if b > 0:
+            second_back.append(RowSum(partials[b - 1], f"back_sum{b - 1}", ties=[gm]))
+            ready = after(teacher_all, second_back[b - 1].chip)
     dense_grads = weight_grads(
         idx,
-        [
-            [(low, 0, ga) for low, ga in zip(second_lows, gas)],
-            [(gm, 0, h) for gm, h in zip(gms, hiddens)],
-        ],
+        [[(second_lows[end], 0, gas[end])], [(gms[end], 0, hiddens[end])]],
         "dense_grads",
+        *early_grads,
     )
     filled = [dense_grads]
     ties = [dense_grads] + [back.far for back in second_back] if pairs else []
@@ -1256,6 +1274,7 @@
                 idx,
                 [state_group(k) for k in range(3)] + [token_group(1), token_group(2)],
                 "late_grads",
+                weight=130,
             )
             order = after(idx, late_grads)
             rest_grads = Scattered(

time: 393 us -> 387 us (0.985)
  Pallas kernels: 136 us -> 143 us
  waiting for transfers between devices: 148 us -> 142 us
  local copies, waits for them, and re-layouts: 33.2 us -> 28.7 us
    ppermute x6, waiting for transfers between devices: 20.2 us -> 13.5 us  [along(): return lax.ppermute(v, 'col', moves)]
    pallas_call x45, Pallas kernels: 115 us -> 119 us  [launch(): pl.pallas_call(body, in_specs=[pl.BlockSpec(memory_space=pltpu.SMEM)] + [...]
    unnamed x202 -> x194, local copies, waits for them, and re-layouts: 32.7 us -> 28.2 us
    pallas_call x2 -> x3, Pallas kernels: 13.9 us -> 16.6 us  [weight_grads(): pl.pallas_call(body, grid=(features // HALF,), in_specs=[pl.BlockSpec(mem...]
  transfers between devices with their start and end apart: 60 -> 60, of which waited for: 30 -> 29; matrix products, arithmetic and copies ran while one was open for 1% -> 1% of each run, Pallas kernels for 30% -> 35%
where the time goes in v1:
time: 387 us; the launch traced here: 384 us
  Pallas kernels  143 us (37%)
  waiting for transfers between devices  142 us (37%)
  starting transfers between devices  50.1 us (13%)
  local copies, waits for them, and re-layouts  28.7 us (7%)
  between operations  17.9 us (5%)
    pallas_call x45, Pallas kernels, launch(): pl.pallas_call(body, in_specs=[pl.BlockSpec(memory_space=pltpu.SMEM)] + [...  119 us
    ppermute x8, waiting for transfers between devices, __init__(): self.far = lax.ppermute(own, 'row', moves)  29.7 us
    unnamed x194, local copies, waits for them, and re-layouts  28.2 us
    all_gather x1, waiting for transfers between devices, per_device(): near = lax.all_gather(near, 'col', axis=0, tiled=True)  26.4 us
    ppermute x5, waiting for transfers between devices, across(): return lax.ppermute(v, 'col', [(k, k ^ 1) for k in range(col_devices)])  19.4 us
    all_gather x1, waiting for transfers between devices, per_device(): dense = lax.all_gather(after(far_weights, *held), 'col', axis=0, tiled=True)  17.2 us
    pallas_call x3, Pallas kernels, weight_grads(): pl.pallas_call(body, grid=(features // HALF,), in_specs=[pl.BlockSpec(mem...  16.6 us
    ppermute x6, waiting for transfers between devices, along(): return lax.ppermute(v, 'col', moves)  13.5 us
  transfers between devices with their start and end apart: 60, of which 29 were waited for; matrix products, arithmetic and copies ran while one was open for 1% of the time, Pallas kernels for 35%

profile of v1, /device:TPU:0, one launch (start us, length us, event | category | flops | bytes accessed | tf_op | source)
XLA Modules:
  0.0 384.3 jit_solution(6233504300029726111)
XLA Ops:
  9.8 2.9 pack_rest.1
  12.7 3.0 collective-permute-start.1
  17.3 2.6 collective-permute-start.9
  25.5 6.8 %collective-permute-done.9.refs_2_ = bf16[128,512]{1,0:T(8,128)(2,1)S(1)} collective-permute-done((bf16[128,512]{1,0:T(8,128)(2,1)S(1)}, bf16[128,512]{1,0:T(8,128)(2,1)S(1)}, u32[]{:S(2)}, u32[]{:S(2)}) %collective-permute-start.9) | collective-permute-done | bytes 131104 | tf_op jit(solution)/shard_map/ppermute | solution.py:932
  34.3 4.0 %collective-permute-done.13.refs_6_ = bf16[128,512]{1,0:T(8,128)(2,1)S(1)} collective-permute-done((bf16[128,512]{1,0:T(8,128)(2,1)S(1)}, bf16[128,512]{1,0:T(8,128)(2,1)S(1)}, u32[]{:S(2)}, u32[]{:S(2)}) %collective-permute-start.13) | collective-permute-done | bytes 131104 | tf_op jit(solution)/shard_map/ppermute | solution.py:935
  47.0 2.5 tokens.1
  52.1 26.4 %all-gather.3.cloned.1.call-done.w_ref.v_ref.refs_11_ = bf16[1024,1536]{1,0:T(8,128)(2,1)} async-done(((bf16[128,1536]{1,0:T(8,128)(2,1)}), bf16[1024,1536]{1,0:T(8,128)(2,1)}) %all-gather.3.cloned.1.call-update) | async-done | bytes 3145744 | tf_op jit(solution)/shard_map/all_gather | solution.py:1013
  86.5 3.4 token_proj.1
  89.9 2.9 token_attend0.1
  92.9 2.9 state_attend0.1
  97.7 6.9 %collective-permute-done.6.refs_2_ = bf16[512,256]{1,0:T(8,128)(2,1)S(1)} collective-permute-done((bf16[512,256]{1,0:T(8,128)(2,1)S(1)}, bf16[512,256]{1,0:T(8,128)(2,1)S(1)}, u32[]{:S(2)}, u32[]{:S(2)}) %collective-permute-start.6) | collective-permute-done | bytes 262176 | tf_op jit(solution)/shard_map/ppermute | solution.py:913
  106.2 5.5 %update0.1 = (f32[512,1024]{1,0:T(8,128)S(1)}, bf16[512,1024]{1,0:T(8,128)(2,1)S(1)}, bf16[512,768]{1,0:T(8,128)(2,1)S(1)}) custom-call(s32[5]{0:T(128)S(1)} %stack.40.s, bf16[512,256]{1,0:T(8,128)(2,1)S(1)} %get-tuple-element.157.refs_0_.refs_8_, bf16[512,256]{1,0:T(8,128)(2,1)S(1)} %collective-permute-done.5.refs_1_, ...), custom_call_target="tpu_custom_call" | custom-call | flops 234881024 | bytes 1024 | tf_op jit(solution)/shard_map/update0/pallas_call | solution.py:51
  112.8 3.7 token_attend1.1
  118.6 2.9 state_attend1.1
  121.5 3.5 collective-permute-done.20.refs_2_
  125.0 3.6 out0.1
  129.9 3.9 %out1.1 = (f32[512,1024]{1,0:T(8,128)S(1)}, bf16[512,1024]{1,0:T(8,128)(2,1)S(1)}) custom-call(s32[5]{0:T(128)S(1)} %stack.40.s, bf16[512,256]{1,0:T(8,128)(2,1)S(1)} %get-tuple-element.167.refs_0_.refs_6_, bf16[512,256]{1,0:T(8,128)(2,1)S(1)} %collective-permute-done.19.refs_1_, bf16[512,256]{1,0:T(8,128)(2,1)S(1)} %collective-permute-done.20.refs_2_, ...), custom_call_target="tpu_custom_call" | custom-call | flops 134217728 | bytes 1024 | tf_op jit(solution)/shard_map/out1/pallas_call | solution.py:51
  136.2 17.2 %all-gather.5.cloned.1.call-done.v_ref.up_ref.refs_8_ = bf16[1024,2048]{1,0:T(8,128)(2,1)} async-done(((bf16[128,2048]{1,0:T(8,128)(2,1)}), bf16[1024,2048]{1,0:T(8,128)(2,1)}) %all-gather.5.cloned.1.call-update) | async-done | bytes 4194320 | tf_op jit(solution)/shard_map/all_gather | solution.py:1035
  157.0 4.2 %dense0.1 = (bf16[512,1024]{1,0:T(8,128)(2,1)S(1)}, bf16[512,1024]{1,0:T(8,128)(2,1)S(1)}, bf16[512,1024]{1,0:T(8,128)(2,1)S(1)}) custom-call(s32[5]{0:T(128)S(1)} %stack.40.s, bf16[512,1024]{1,0:T(8,128)(2,1)S(1)} %copy-done.62, bf16[1024,2048]{1,0:T(8,128)(2,1)S(1)} %copy-done, bf16[1024,1024]{1,0:T(8,128)(2,1)S(1)} %down_turn.1.down_ref), custom_call_target="tpu_custom_call" | custom-call | flops 268435456 | bytes 1024 | tf_op jit(solution)/shard_map/dense0/pallas_call | solution.py:51
  166.4 4.4 %dense1.1 = (bf16[512,1024]{1,0:T(8,128)(2,1)S(1)}, bf16[512,1024]{1,0:T(8,128)(2,1)S(1)}, bf16[512,1024]{1,0:T(8,128)(2,1)S(1)}) custom-call(s32[5]{0:T(128)S(1)} %stack.40.s, bf16[512,1024]{1,0:T(8,128)(2,1)S(1)} %copy-done.60, bf16[1024,2048]{1,0:T(8,128)(2,1)S(1)} %copy-done.1, bf16[1024,1024]{1,0:T(8,128)(2,1)S(1)} %down_turn.1.down_ref), custom_call_target="tpu_custom_call" | custom-call | flops 268435456 | bytes 1024 | tf_op jit(solution)/shard_map/dense1/pallas_call | solution.py:51
  172.9 4.4 %state_back1.1 = (bf16[512,256]{1,0:T(8,128)(2,1)S(1)}, f32[512,256]{1,0:T(8,128)S(1)}, f32[512,256]{1,0:T(8,128)S(1)}, f32[512,256]{1,0:T(8,128)S(1)}, f32[512,256]{1,0:T(8,128)S(1)}) custom-call(s32[5]{0:T(128)S(1)} %stack.40.s, bf16[512,768]{1,0:T(8,128)(2,1)S(1)} %copy-done.12, bf16[1024,768]{1,0:T(8,128)(2,1)S(1)} %get-tuple-element.153.refs_0_.refs_1_, ...), custom_call_target="tpu_custom_call" | custom-call | flops 335544320 | bytes 1024 | tf_op jit(solution)/shard_map/state_back1/pallas_call | solution.py:51
  181.4 5.2 %back0.1 = (bf16[512,1024]{1,0:T(8,128)(2,1)S(1)}, bf16[512,1024]{1,0:T(8,128)(2,1)S(1)}, f32[1,1024]{1,0:T(1,128)S(1)}, bf16[512,1024]{1,0:T(8,128)(2,1)}) custom-call(s32[5]{0:T(128)S(1)} %stack.40.s, bf16[512,1024]{1,0:T(8,128)(2,1)S(1)} %get-tuple-element.175.refs_0_, bf16[256,1024]{1,0:T(8,128)(2,1)S(1)} %collective-permute-done.23.refs_1_, ...), custom_call_target="tpu_custom_call" | custom-call | flops 268435456 | bytes 1024 | tf_op jit(solution)/shard_map/back0/pallas_call | solution.py:51
  186.7 5.0 %dense_grads0.1.refs_4_ = bf16[1024,2048]{1,0:T(8,128)(2,1)} custom-call(s32[5]{0:T(128)S(1)} %stack.40.s, bf16[512,1024]{1,0:T(8,128)(2,1)S(1)} %copy-done.62, bf16[512,1024]{1,0:T(8,128)(2,1)S(1)} %get-tuple-element.193.refs_1_, bf16[512,1024]{1,0:T(8,128)(2,1)S(1)} %get-tuple-element.192.refs_2_.refs_3_, bf16[512,1024]{1,0:T(8,128)(2,1)S(1)} %get-tuple-element.171.refs_3_), custom_call_target="tpu_custom_call" | custom-call | flops 10737418240 | bytes 1024 | tf_op jit(solution)/shard_map/dense_grads0/pallas_call | solution.py:626
  191.6 2.6 collective-permute-done.26.refs_1_
  196.9 5.2 %back1.1 = (bf16[512,1024]{1,0:T(8,128)(2,1)S(1)}, bf16[512,1024]{1,0:T(8,128)(2,1)S(1)}, f32[1,1024]{1,0:T(1,128)S(1)}, bf16[512,1024]{1,0:T(8,128)(2,1)}) custom-call(s32[5]{0:T(128)S(1)} %stack.40.s, bf16[512,1024]{1,0:T(8,128)(2,1)S(1)} %get-tuple-element.190.refs_0_, bf16[256,1024]{1,0:T(8,128)(2,1)S(1)} %collective-permute-done.26.refs_1_, ...), custom_call_target="tpu_custom_call" | custom-call | flops 268435456 | bytes 1024 | tf_op jit(solution)/shard_map/back1/pallas_call | solution.py:51
  202.3 5.0 %dense_grads.1 = bf16[1024,2048]{1,0:T(8,128)(2,1)} custom-call(s32[5]{0:T(128)S(1)} %stack.40.s, bf16[512,1024]{1,0:T(8,128)(2,1)S(1)} %copy-done.60, bf16[512,1024]{1,0:T(8,128)(2,1)S(1)} %get-tuple-element.208.refs_1_, bf16[512,1024]{1,0:T(8,128)(2,1)S(1)} %get-tuple-element.199.refs_2_.refs_3_, bf16[512,1024]{1,0:T(8,128)(2,1)S(1)} %get-tuple-element.178.refs_3_, ...), custom_call_target="tpu_custom_call" | custom-call | flops 10737418240 | bytes 1024 | tf_op jit(solution)/shard_map/dense_grads/pallas_call | solution.py:626
  212.3 12.7 %collective-permute-done.29.refs_1_ = bf16[256,1024]{1,0:T(8,128)(2,1)S(1)} collective-permute-done((bf16[256,1024]{1,0:T(8,128)(2,1)S(1)}, bf16[256,1024]{1,0:T(8,128)(2,1)S(1)}, u32[]{:S(2)}, u32[]{:S(2)}) %collective-permute-start.29) | collective-permute-done | bytes 524320 | tf_op jit(solution)/shard_map/ppermute | solution.py:987
  231.8 4.5 %token_back0.1 = (bf16[512,256]{1,0:T(8,128)(2,1)S(1)}, f32[512,256]{1,0:T(8,128)S(1)}, f32[512,256]{1,0:T(8,128)S(1)}, f32[512,256]{1,0:T(8,128)S(1)}, f32[512,256]{1,0:T(8,128)S(1)}) custom-call(s32[5]{0:T(128)S(1)} %stack.40.s, bf16[1024,768]{1,0:T(8,128)(2,1)S(1)} %get-tuple-element.153.refs_0_.refs_1_, bf16[512,768]{1,0:T(8,128)(2,1)S(1)} %copy-done.15, ...), custom_call_target="tpu_custom_call" | custom-call | flops 335544320 | bytes 1024 | tf_op jit(solution)/shard_map/token_back0/pallas_call | solution.py:51
  236.3 5.0 %collective-permute-done.32.refs_1_ = bf16[256,1024]{1,0:T(8,128)(2,1)S(1)} collective-permute-done((bf16[256,1024]{1,0:T(8,128)(2,1)S(1)}, bf16[256,1024]{1,0:T(8,128)(2,1)S(1)}, u32[]{:S(2)}, u32[]{:S(2)}) %collective-permute-start.32) | collective-permute-done | bytes 524320 | tf_op jit(solution)/shard_map/ppermute | solution.py:987
  248.1 5.6 %token_back1.1 = (bf16[512,256]{1,0:T(8,128)(2,1)S(1)}, f32[512,256]{1,0:T(8,128)S(1)}, f32[512,256]{1,0:T(8,128)S(1)}, bf16[512,256]{1,0:T(8,128)(2,1)S(1)}, bf...) custom-call(s32[5]{0:T(128)S(1)} %stack.40.s, ...), custom_call_target="tpu_custom_call" | custom-call | flops 503316480 | bytes 1024 | tf_op jit(solution)/shard_map/token_back1/pallas_call | solution.py:51
  256.8 2.6 collective-permute-done.35.b_ref
  264.3 4.8 %update_last.1 = f32[512,1024]{1,0:T(8,128)} custom-call(s32[5]{0:T(128)S(1)} %stack.40.s, bf16[512,256]{1,0:T(8,128)(2,1)S(1)} %copy-done.49, bf16[512,256]{1,0:T(8,128)(2,1)S(1)} %collective-permute-done.37.refs_1_, bf16[512,256]{1,0:T(8,128)(2,1)S(1)} %collective-permute-done.34.refs_2_, bf16[512,256]{1,0:T(8,128)(2,1)S(1)} %collective-permute-done.38.refs_3_, ...), custom_call_target="tpu_custom_call" | custom-call | flops 134217728 | bytes 1024 | tf_op jit(solution)/shard_map/update_last/pallas_call | solution.py:51
  269.2 5.2 %collective-permute-done.36.refs_1_ = bf16[256,1024]{1,0:T(8,128)(2,1)S(1)} collective-permute-done((bf16[256,1024]{1,0:T(8,128)(2,1)S(1)}, bf16[256,1024]{1,0:T(8,128)(2,1)S(1)}, u32[]{:S(2)}, u32[]{:S(2)}) %collective-permute-start.36) | collective-permute-done | bytes 524320 | tf_op jit(solution)/shard_map/ppermute | solution.py:987
  276.3 2.4 chain_back1.1
  281.0 4.4 %state_back0.1 = (bf16[512,256]{1,0:T(8,128)(2,1)S(1)}, bf16[512,256]{1,0:T(8,128)(2,1)S(1)}, bf16[512,256]{1,0:T(8,128)(2,1)S(1)}, bf16[512,256]{1,0:T(8,128)(2,1)S(1)}, bf16[512,256]{1,0:T(8,128)(2,1)S(1)}) custom-call(s32[5]{0:T(128)S(1)} %stack.40.s, bf16[512,768]{1,0:T(8,128)(2,1)S(1)} %copy-done.15, ...), custom_call_target="tpu_custom_call" | custom-call | flops 335544320 | bytes 1024 | tf_op jit(solution)/shard_map/state_back0/pallas_call | solution.py:51
  285.4 6.7 %late_grads.1 = bf16[1024,1280]{1,0:T(8,128)(2,1)} custom-call(s32[5]{0:T(128)S(1)} %stack.40.s, bf16[512,1024]{1,0:T(8,128)(2,1)S(1)} %copy-done.90, bf16[512,256]{1,0:T(8,128)(2,1)S(1)} %get-tuple-element.252.refs_1_.refs_0_, bf16[512,1024]{1,0:T(8,128)(2,1)S(1)} %copy-done.92, bf16[512,256]{1,0:T(8,128)(2,1)S(1)} %copy-done.74, ...), custom_call_target="tpu_custom_call" | custom-call | flops 43620761600 | bytes 1024 | tf_op jit(solution)/shard_map/late_grads/pallas_call | solution.py:626
  305.6 3.4 rest_grads.1
  310.6 2.6 collective-permute-start.43
  315.5 2.5 collective-permute-done.46.refs_1_
  318.1 13.9 %collective-permute-done.44.got_ref = bf16[512,768]{1,0:T(8,128)(2,1)S(1)} collective-permute-done((bf16[512,768]{1,0:T(8,128)(2,1)S(1)}, bf16[512,768]{1,0:T(8,128)(2,1)S(1)}, u32[]{:S(2)}, u32[]{:S(2)}) %collective-permute-start.44) | collective-permute-done | bytes 786464 | tf_op jit(solution)/shard_map/ppermute | solution.py:935
  333.9 2.7 collective-permute-start.49
  338.0 2.4 input_rows.1
  340.5 3.2 chain_back0.1
  343.7 5.4 %collective-permute-done.49.refs_1_ = bf16[128,768]{1,0:T(8,128)(2,1)S(1)} collective-permute-done((bf16[128,768]{1,0:T(8,128)(2,1)S(1)}, bf16[128,768]{1,0:T(8,128)(2,1)S(1)}, u32[]{:S(2)}, u32[]{:S(2)}) %collective-permute-start.49) | collective-permute-done | bytes 196640 | tf_op jit(solution)/shard_map/ppermute | solution.py:932
  351.4 2.7 collective-permute-done.52
  354.6 3.2 collective-permute-done.53
  357.8 5.0 %collective-permute-start.54 = (f32[4,1024]{1,0:T(4,128)S(1)}, f32[4,1024]{1,0:T(4,128)S(1)}, u32[]{:S(2)}, u32[]{:S(2)}) collective-permute-start(f32[4,1024]{1,0:T(4,128)S(1)} %add.86), channel_id=1, source_target_pairs={{0,2},{1,3},{2,0},{3,1},{4,6},{5,7},{6,4},{7,5},{8,10},{9,11},{10,... | collective-permute-start | bytes 49160 | tf_op jit(solution)/shard_map/ppermute | solution.py:1001
  366.9 3.6 collective-permute-done.55
  (347 shorter events, 121.0 us)
Async XLA Ops:
  7.2 71.4 %all-gather.3.cloned.1.call-start = ((), (), s32[]{:S(2)}) async-start(), calls=%async_computation.2 | async-start | bytes 3538944 | tf_op jit(solution)/shard_map/all_gather | solution.py:1013
  9.7 143.7 %all-gather.5.cloned.1.call-start = ((), (), s32[]{:S(2)}) async-start(), calls=%async_computation.3 | async-start | bytes 4718592 | tf_op jit(solution)/shard_map/all_gather | solution.py:1035
  12.7 29.7 %collective-permute-start.1 = (bf16[512,1024]{1,0:T(8,128)(2,1)S(1)}, bf16[512,1024]{1,0:T(8,128)(2,1)}, u32[]{:S(2)}, u32[]{:S(2)}) collective-permute-start(bf16[512,1024]{1,0:T(8,128)(2,1)S(1)} %get-tuple-element.151.refs_0_), channel_id=1, source_target_pairs={{0,16},{8,24},{16,0},{24,8},{1,17},{9,25},{17,1},{25,9},{2,18},{10... | collective-permute-start | bytes 3145736 | tf_op jit(solution)/shard_map/ppermute | solution.py:913
  15.7 8.3 %collective-permute-start.8 = (bf16[128,512]{1,0:T(8,128)(2,1)S(1)}, bf16[128,512]{1,0:T(8,128)(2,1)S(1)}, u32[]{:S(2)}, u32[]{:S(2)}) collective-permute-start(bf16[128,512]{1,0:T(8,128)(2,1)S(1)} %get-tuple-element.159.refs_0_), channel_id=1, source_target_pairs={{0,2},{1,3},{2,4},{3,5},{4,6},{5,7},{6,0},{7,1},{8,10},{9,11},{10,... | collective-permute-start | bytes 393224 | tf_op jit(solution)/shard_map/ppermute | solution.py:932
  17.3 15.1 %collective-permute-start.9 = (bf16[128,512]{1,0:T(8,128)(2,1)S(1)}, bf16[128,512]{1,0:T(8,128)(2,1)S(1)}, u32[]{:S(2)}, u32[]{:S(2)}) collective-permute-start(bf16[128,512]{1,0:T(8,128)(2,1)S(1)} %get-tuple-element.159.refs_0_), channel_id=1, source_target_pairs={{0,4},{1,5},{2,6},{3,7},{4,0},{5,1},{6,2},{7,3},{8,12},{9,13},{10,... | collective-permute-start | bytes 393224 | tf_op jit(solution)/shard_map/ppermute | solution.py:932
  19.8 14.0 %collective-permute-start.10 = (bf16[128,512]{1,0:T(8,128)(2,1)S(1)}, bf16[128,512]{1,0:T(8,128)(2,1)S(1)}, u32[]{:S(2)}, u32[]{:S(2)}) collective-permute-start(bf16[128,512]{1,0:T(8,128)(2,1)S(1)} %get-tuple-element.159.refs_0_), channel_id=1, source_target_pairs={{0,6},{1,7},{2,0},{3,1},{4,2},{5,3},{6,4},{7,5},{8,14},{9,15},{10,... | collective-permute-start | bytes 393224 | tf_op jit(solution)/shard_map/ppermute | solution.py:932
  21.2 13.2 %collective-permute-start.11 = (bf16[128,512]{1,0:T(8,128)(2,1)S(1)}, bf16[128,512]{1,0:T(8,128)(2,1)S(1)}, u32[]{:S(2)}, u32[]{:S(2)}) collective-permute-start(bf16[128,512]{1,0:T(8,128)(2,1)S(1)} %get-tuple-element.159.refs_0_), channel_id=1, source_target_pairs={{0,1},{1,0},{2,3},{3,2},{4,5},{5,4},{6,7},{7,6},{8,9},{9,8},{10,11... | collective-permute-start | bytes 393224 | tf_op jit(solution)/shard_map/ppermute | solution.py:935
  24.0 10.4 %collective-permute-start.12 = (bf16[128,512]{1,0:T(8,128)(2,1)S(1)}, bf16[128,512]{1,0:T(8,128)(2,1)S(1)}, u32[]{:S(2)}, u32[]{:S(2)}) collective-permute-start(bf16[128,512]{1,0:T(8,128)(2,1)S(1)} %collective-permute-done.8.refs_1_), channel_id=1, source_target_pairs={{0,1},{1,0},{2,3},{3,2},{4,5},{5,4},{6,7},{7,6},{8,9},{9,8},{10,11... | collective-permute-start | bytes 393224 | tf_op jit(solution)/shard_map/ppermute | solution.py:935
  32.3 6.1 %collective-permute-start.13 = (bf16[128,512]{1,0:T(8,128)(2,1)S(1)}, bf16[128,512]{1,0:T(8,128)(2,1)S(1)}, u32[]{:S(2)}, u32[]{:S(2)}) collective-permute-start(bf16[128,512]{1,0:T(8,128)(2,1)S(1)} %collective-permute-done.9.refs_2_), channel_id=1, source_target_pairs={{0,1},{1,0},{2,3},{3,2},{4,5},{5,4},{6,7},{7,6},{8,9},{9,8},{10,11... | collective-permute-start | bytes 393224 | tf_op jit(solution)/shard_map/ppermute | solution.py:935
  33.9 5.9 %collective-permute-start.14 = (bf16[128,512]{1,0:T(8,128)(2,1)S(1)}, bf16[128,512]{1,0:T(8,128)(2,1)S(1)}, u32[]{:S(2)}, u32[]{:S(2)}) collective-permute-start(bf16[128,512]{1,0:T(8,128)(2,1)S(1)} %collective-permute-done.10.refs_3_), channel_id=1, source_target_pairs={{0,1},{1,0},{2,3},{3,2},{4,5},{5,4},{6,7},{7,6},{8,9},{9,8},{10,11... | collective-permute-start | bytes 393224 | tf_op jit(solution)/shard_map/ppermute | solution.py:935
  42.4 330.0 %reduce-scatter.5.cloned.1.call-start = ((), (), s32[]{:S(2)}) async-start(), calls=%async_computation.5 | async-start | bytes 4718592 | tf_op jit(solution)/shard_map/reduce_scatter | solution.py:1230
  42.6 4.4 %collective-permute-start.2 = (bf16[512,1024]{1,0:T(8,128)(2,1)}, bf16[512,1024]{1,0:T(8,128)(2,1)}, u32[]{:S(2)}, u32[]{:S(2)}) collective-permute-start(bf16[512,1024]{1,0:T(8,128)(2,1)} %collective-permute-done.1.refs_2_), channel_id=1, source_target_pairs={{0,8},{8,0},{16,24},{24,16},{1,9},{9,1},{17,25},{25,17},{2,10},{10... | collective-permute-start | bytes 3145736 | tf_op jit(solution)/shard_map/ppermute | solution.py:910
  43.2 49.7 %collective-permute-start.16 = (bf16[512,1024]{1,0:T(8,128)(2,1)}, bf16[512,1024]{1,0:T(8,128)(2,1)}, u32[]{:S(2)}, u32[]{:S(2)}) collective-permute-start(bf16[512,1024]{1,0:T(8,128)(2,1)} %mid_turn.1.refs_4_), channel_id=1, source_target_pairs={{0,16},{8,24},{16,0},{24,8},{1,17},{9,25},{17,1},{25,9},{2,18},{10... | collective-permute-start | bytes 3145736 | tf_op jit(solution)/shard_map/ppermute | solution.py:913
  45.3 60.9 %collective-permute-start.15 = (bf16[512,1024]{1,0:T(8,128)(2,1)}, bf16[512,1024]{1,0:T(8,128)(2,1)}, u32[]{:S(2)}, u32[]{:S(2)}) collective-permute-start(bf16[512,1024]{1,0:T(8,128)(2,1)} %mid_turn.1.refs_4_), channel_id=1, source_target_pairs={{0,8},{8,0},{16,24},{24,16},{1,9},{9,1},{17,25},{25,17},{2,10},{10... | collective-permute-start | bytes 3145736 | tf_op jit(solution)/shard_map/ppermute | solution.py:910
  92.9 13.3 %collective-permute-start.17 = (bf16[512,1024]{1,0:T(8,128)(2,1)}, bf16[512,1024]{1,0:T(8,128)(2,1)S(1)}, u32[]{:S(2)}, u32[]{:S(2)}) collective-permute-start(bf16[512,1024]{1,0:T(8,128)(2,1)} %collective-permute-done.16.refs_6_), channel_id=1, source_target_pairs={{0,8},{8,0},{16,24},{24,16},{1,9},{9,1},{17,25},{25,17},{2,10},{10... | collective-permute-start | bytes 3145736 | tf_op jit(solution)/shard_map/ppermute | solution.py:910
  95.8 8.8 %collective-permute-start.6 = (bf16[512,256]{1,0:T(8,128)(2,1)S(1)}, bf16[512,256]{1,0:T(8,128)(2,1)S(1)}, u32[]{:S(2)}, u32[]{:S(2)}) collective-permute-start(bf16[512,256]{1,0:T(8,128)(2,1)S(1)} %get-tuple-element.157.refs_0_.refs_8_), channel_id=1, source_target_pairs={{0,16},{8,24},{16,0},{24,8},{1,17},{9,25},{17,1},{25,9},{2,18},{10... | collective-permute-start | bytes 786440 | tf_op jit(solution)/shard_map/ppermute | solution.py:913
  97.5 8.7 %collective-permute-start.5 = (bf16[512,256]{1,0:T(8,128)(2,1)S(1)}, bf16[512,256]{1,0:T(8,128)(2,1)S(1)}, u32[]{:S(2)}, u32[]{:S(2)}) collective-permute-start(bf16[512,256]{1,0:T(8,128)(2,1)S(1)} %get-tuple-element.157.refs_0_.refs_8_), channel_id=1, source_target_pairs={{0,8},{8,0},{16,24},{24,16},{1,9},{9,1},{17,25},{25,17},{2,10},{10... | collective-permute-start | bytes 786440 | tf_op jit(solution)/shard_map/ppermute | solution.py:910
  104.6 13.9 %collective-permute-start.4 = (bf16[512,256]{1,0:T(8,128)(2,1)S(1)}, bf16[512,256]{1,0:T(8,128)(2,1)S(1)}, u32[]{:S(2)}, u32[]{:S(2)}) collective-permute-start(bf16[512,256]{1,0:T(8,128)(2,1)S(1)} %get-tuple-element.156.refs_0_.refs_4_), channel_id=1, source_target_pairs={{0,16},{8,24},{16,0},{24,8},{1,17},{9,25},{17,1},{25,9},{2,18},{10... | collective-permute-start | bytes 786440 | tf_op jit(solution)/shard_map/ppermute | solution.py:913
  116.5 8.5 %collective-permute-start.20 = (bf16[512,256]{1,0:T(8,128)(2,1)S(1)}, bf16[512,256]{1,0:T(8,128)(2,1)S(1)}, u32[]{:S(2)}, u32[]{:S(2)}) collective-permute-start(bf16[512,256]{1,0:T(8,128)(2,1)S(1)} %get-tuple-element.167.refs_0_.refs_6_), channel_id=1, source_target_pairs={{0,16},{8,24},{16,0},{24,8},{1,17},{9,25},{17,1},{25,9},{2,18},{10... | collective-permute-start | bytes 786440 | tf_op jit(solution)/shard_map/ppermute | solution.py:913
  118.0 7.0 %collective-permute-start.3 = (bf16[512,256]{1,0:T(8,128)(2,1)S(1)}, bf16[512,256]{1,0:T(8,128)(2,1)S(1)}, u32[]{:S(2)}, u32[]{:S(2)}) collective-permute-start(bf16[512,256]{1,0:T(8,128)(2,1)S(1)} %get-tuple-element.156.refs_0_.refs_4_), channel_id=1, source_target_pairs={{0,8},{8,0},{16,24},{24,16},{1,9},{9,1},{17,25},{25,17},{2,10},{10... | collective-permute-start | bytes 786440 | tf_op jit(solution)/shard_map/ppermute | solution.py:910
  118.0 11.9 %collective-permute-start.19 = (bf16[512,256]{1,0:T(8,128)(2,1)S(1)}, bf16[512,256]{1,0:T(8,128)(2,1)S(1)}, u32[]{:S(2)}, u32[]{:S(2)}) collective-permute-start(bf16[512,256]{1,0:T(8,128)(2,1)S(1)} %get-tuple-element.167.refs_0_.refs_6_), channel_id=1, source_target_pairs={{0,8},{8,0},{16,24},{24,16},{1,9},{9,1},{17,25},{25,17},{2,10},{10... | collective-permute-start | bytes 786440 | tf_op jit(solution)/shard_map/ppermute | solution.py:910
  118.6 6.4 %collective-permute-start.18 = (bf16[512,256]{1,0:T(8,128)(2,1)S(1)}, bf16[512,256]{1,0:T(8,128)(2,1)S(1)}, u32[]{:S(2)}, u32[]{:S(2)}) collective-permute-start(bf16[512,256]{1,0:T(8,128)(2,1)S(1)} %collective-permute-done.4.refs_2_), channel_id=1, source_target_pairs={{0,8},{8,0},{16,24},{24,16},{1,9},{9,1},{17,25},{25,17},{2,10},{10... | collective-permute-start | bytes 786440 | tf_op jit(solution)/shard_map/ppermute | solution.py:910
  125.0 4.9 %collective-permute-start.21 = (bf16[512,256]{1,0:T(8,128)(2,1)S(1)}, bf16[512,256]{1,0:T(8,128)(2,1)S(1)}, u32[]{:S(2)}, u32[]{:S(2)}) collective-permute-start(bf16[512,256]{1,0:T(8,128)(2,1)S(1)} %collective-permute-done.20.refs_2_), channel_id=1, source_target_pairs={{0,8},{8,0},{16,24},{24,16},{1,9},{9,1},{17,25},{25,17},{2,10},{10... | collective-permute-start | bytes 786440 | tf_op jit(solution)/shard_map/ppermute | solution.py:910
  164.9 14.0 %collective-permute-start.23 = (bf16[256,1024]{1,0:T(8,128)(2,1)S(1)}, bf16[256,1024]{1,0:T(8,128)(2,1)S(1)}, u32[]{:S(2)}, u32[]{:S(2)}) collective-permute-start(bf16[256,1024]{1,0:T(8,128)(2,1)S(1)} %get-tuple-element.176), channel_id=1, source_target_pairs={{0,16},{8,24},{16,0},{24,8},{1,17},{9,25},{17,1},{25,9},{2,18},{10... | collective-permute-start | bytes 1572872 | tf_op jit(solution)/shard_map/ppermute | solution.py:987
  170.8 8.1 %collective-permute-start.25 = (bf16[512,1024]{1,0:T(8,128)(2,1)S(1)}, bf16[512,1024]{1,0:T(8,128)(2,1)S(1)}, u32[]{:S(2)}, u32[]{:S(2)}) collective-permute-start(bf16[512,1024]{1,0:T(8,128)(2,1)S(1)} %get-tuple-element.189.a_ref), channel_id=1, source_target_pairs={{0,8},{8,0},{16,24},{24,16},{1,9},{9,1},{17,25},{25,17},{2,10},{10... | collective-permute-start | bytes 3145736 | tf_op jit(solution)/shard_map/ppermute | solution.py:910
  179.9 14.4 %collective-permute-start.26 = (bf16[256,1024]{1,0:T(8,128)(2,1)S(1)}, bf16[256,1024]{1,0:T(8,128)(2,1)S(1)}, u32[]{:S(2)}, u32[]{:S(2)}) collective-permute-start(bf16[256,1024]{1,0:T(8,128)(2,1)S(1)} %get-tuple-element.191), channel_id=1, source_target_pairs={{0,16},{8,24},{16,0},{24,8},{1,17},{9,25},{17,1},{25,9},{2,18},{10... | collective-permute-start | bytes 1572872 | tf_op jit(solution)/shard_map/ppermute | solution.py:987
  194.3 14.1 %collective-permute-start.28 = (bf16[512,1024]{1,0:T(8,128)(2,1)}, bf16[512,1024]{1,0:T(8,128)(2,1)}, u32[]{:S(2)}, u32[]{:S(2)}) collective-permute-start(bf16[512,1024]{1,0:T(8,128)(2,1)} %get-tuple-element.201.a_ref), channel_id=1, source_target_pairs={{0,8},{8,0},{16,24},{24,16},{1,9},{9,1},{17,25},{25,17},{2,10},{10... | collective-permute-start | bytes 3145736 | tf_op jit(solution)/shard_map/ppermute | solution.py:910
  202.1 22.9 %collective-permute-start.31 = (bf16[512,1024]{1,0:T(8,128)(2,1)}, bf16[512,1024]{1,0:T(8,128)(2,1)}, u32[]{:S(2)}, u32[]{:S(2)}) collective-permute-start(bf16[512,1024]{1,0:T(8,128)(2,1)} %get-tuple-element.210.a_ref), channel_id=1, source_target_pairs={{0,8},{8,0},{16,24},{24,16},{1,9},{9,1},{17,25},{25,17},{2,10},{10... | collective-permute-start | bytes 3145736 | tf_op jit(solution)/shard_map/ppermute | solution.py:910
  208.3 166.2 %reduce-scatter.3.cloned.1.call-start = ((), (), s32[]{:S(2)}) async-start(), calls=%async_computation.4 | async-start | bytes 2949120 | tf_op jit(solution)/shard_map/reduce_scatter | solution.py:1286
  210.7 14.3 %collective-permute-start.29 = (bf16[256,1024]{1,0:T(8,128)(2,1)S(1)}, bf16[256,1024]{1,0:T(8,128)(2,1)S(1)}, u32[]{:S(2)}, u32[]{:S(2)}) collective-permute-start(bf16[256,1024]{1,0:T(8,128)(2,1)S(1)} %get-tuple-element.203), channel_id=1, source_target_pairs={{0,16},{8,24},{16,0},{24,8},{1,17},{9,25},{17,1},{25,9},{2,18},{10... | collective-permute-start | bytes 1572872 | tf_op jit(solution)/shard_map/ppermute | solution.py:987
  225.0 3.5 collective-permute-start.30
  227.0 14.4 %collective-permute-start.32 = (bf16[256,1024]{1,0:T(8,128)(2,1)S(1)}, bf16[256,1024]{1,0:T(8,128)(2,1)S(1)}, u32[]{:S(2)}, u32[]{:S(2)}) collective-permute-start(bf16[256,1024]{1,0:T(8,128)(2,1)S(1)} %get-tuple-element.212), channel_id=1, source_target_pairs={{0,16},{8,24},{16,0},{24,8},{1,17},{9,25},{17,1},{25,9},{2,18},{10... | collective-permute-start | bytes 1572872 | tf_op jit(solution)/shard_map/ppermute | solution.py:987
  246.6 8.3 %collective-permute-start.34 = (bf16[512,256]{1,0:T(8,128)(2,1)S(1)}, bf16[512,256]{1,0:T(8,128)(2,1)S(1)}, u32[]{:S(2)}, u32[]{:S(2)}) collective-permute-start(bf16[512,256]{1,0:T(8,128)(2,1)S(1)} %copy-done.49), channel_id=1, source_target_pairs={{0,16},{8,24},{16,0},{24,8},{1,17},{9,25},{17,1},{25,9},{2,18},{10... | collective-permute-start | bytes 786440 | tf_op jit(solution)/shard_map/ppermute | solution.py:913
  260.4 14.0 %collective-permute-start.36 = (bf16[256,1024]{1,0:T(8,128)(2,1)S(1)}, bf16[256,1024]{1,0:T(8,128)(2,1)S(1)}, u32[]{:S(2)}, u32[]{:S(2)}) collective-permute-start(bf16[256,1024]{1,0:T(8,128)(2,1)S(1)} %get-tuple-element.225), channel_id=1, source_target_pairs={{0,16},{8,24},{16,0},{24,8},{1,17},{9,25},{17,1},{25,9},{2,18},{10... | collective-permute-start | bytes 1572872 | tf_op jit(solution)/shard_map/ppermute | solution.py:987
  300.5 9.2 %collective-permute-start.41 = (bf16[512,1024]{1,0:T(8,128)(2,1)S(1)}, bf16[512,1024]{1,0:T(8,128)(2,1)S(1)}, u32[]{:S(2)}, u32[]{:S(2)}) collective-permute-start(bf16[512,1024]{1,0:T(8,128)(2,1)S(1)} %copy-done.29), channel_id=1, source_target_pairs={{0,8},{8,0},{16,24},{24,16},{1,9},{9,1},{17,25},{25,17},{2,10},{10... | collective-permute-start | bytes 3145736 | tf_op jit(solution)/shard_map/ppermute | solution.py:910
  302.6 10.6 %collective-permute-start.40 = (bf16[512,1024]{1,0:T(8,128)(2,1)S(1)}, bf16[512,1024]{1,0:T(8,128)(2,1)S(1)}, u32[]{:S(2)}, u32[]{:S(2)}) collective-permute-start(bf16[512,1024]{1,0:T(8,128)(2,1)S(1)} %first_back0.1.a_ref), channel_id=1, source_target_pairs={{0,8},{8,0},{16,24},{24,16},{1,9},{9,1},{17,25},{25,17},{2,10},{10... | collective-permute-start | bytes 3145736 | tf_op jit(solution)/shard_map/ppermute | solution.py:910
  304.0 14.1 %collective-permute-start.46 = (bf16[256,1024]{1,0:T(8,128)(2,1)S(1)}, bf16[256,1024]{1,0:T(8,128)(2,1)S(1)}, u32[]{:S(2)}, u32[]{:S(2)}) collective-permute-start(bf16[256,1024]{1,0:T(8,128)(2,1)S(1)} %get-tuple-element.265), channel_id=1, source_target_pairs={{0,16},{8,24},{16,0},{24,8},{1,17},{9,25},{17,1},{25,9},{2,18},{10... | collective-permute-start | bytes 1572872 | tf_op jit(solution)/shard_map/ppermute | solution.py:987
  309.0 23.0 %collective-permute-start.44 = (bf16[512,768]{1,0:T(8,128)(2,1)S(1)}, bf16[512,768]{1,0:T(8,128)(2,1)S(1)}, u32[]{:S(2)}, u32[]{:S(2)}) collective-permute-start(bf16[512,768]{1,0:T(8,128)(2,1)S(1)} %get-tuple-element.261), channel_id=1, source_target_pairs={{0,1},{1,0},{2,3},{3,2},{4,5},{5,4},{6,7},{7,6},{8,9},{9,8},{10,11... | collective-permute-start | bytes 2359304 | tf_op jit(solution)/shard_map/ppermute | solution.py:935
  310.6 25.9 %collective-permute-start.43 = (bf16[256,1024]{1,0:T(8,128)(2,1)S(1)}, bf16[256,1024]{1,0:T(8,128)(2,1)S(1)}, u32[]{:S(2)}, u32[]{:S(2)}) collective-permute-start(bf16[256,1024]{1,0:T(8,128)(2,1)S(1)} %get-tuple-element.244), channel_id=1, source_target_pairs={{0,16},{8,24},{1,17},{9,25},{2,18},{10,26},{3,19},{11,27},{4,20},{... | collective-permute-start | bytes 1572872 | tf_op jit(solution)/shard_map/ppermute | solution.py:987
  314.2 23.8 %collective-permute-start.42 = (bf16[256,1024]{1,0:T(8,128)(2,1)S(1)}, bf16[256,1024]{1,0:T(8,128)(2,1)S(1)}, u32[]{:S(2)}, u32[]{:S(2)}) collective-permute-start(bf16[256,1024]{1,0:T(8,128)(2,1)S(1)} %get-tuple-element.243), channel_id=1, source_target_pairs={{16,0},{24,8},{17,1},{25,9},{18,2},{26,10},{19,3},{27,11},{20,4},{... | collective-permute-start | bytes 1572872 | tf_op jit(solution)/shard_map/ppermute | solution.py:987
  318.1 22.4 %collective-permute-start.47 = (bf16[256,1024]{1,0:T(8,128)(2,1)S(1)}, bf16[256,1024]{1,0:T(8,128)(2,1)S(1)}, u32[]{:S(2)}, u32[]{:S(2)}) collective-permute-start(bf16[256,1024]{1,0:T(8,128)(2,1)S(1)} %collective-permute-done.46.refs_1_), channel_id=1, source_target_pairs={{0,8},{8,0},{16,24},{24,16},{1,9},{9,1},{17,25},{25,17},{2,10},{10... | collective-permute-start | bytes 1572872 | tf_op jit(solution)/shard_map/ppermute | solution.py:910
  332.8 10.9 %collective-permute-start.48 = (bf16[128,768]{1,0:T(8,128)(2,1)S(1)}, bf16[128,768]{1,0:T(8,128)(2,1)S(1)}, u32[]{:S(2)}, u32[]{:S(2)}) collective-permute-start(bf16[128,768]{1,0:T(8,128)(2,1)S(1)} %get-tuple-element.269), channel_id=1, source_target_pairs={{0,2},{1,3},{2,4},{3,5},{4,6},{5,7},{6,0},{7,1},{8,10},{9,11},{10,... | collective-permute-start | bytes 589832 | tf_op jit(solution)/shard_map/ppermute | solution.py:932
  333.9 15.2 %collective-permute-start.49 = (bf16[128,768]{1,0:T(8,128)(2,1)S(1)}, bf16[128,768]{1,0:T(8,128)(2,1)S(1)}, u32[]{:S(2)}, u32[]{:S(2)}) collective-permute-start(bf16[128,768]{1,0:T(8,128)(2,1)S(1)} %get-tuple-element.270), channel_id=1, source_target_pairs={{0,4},{1,5},{2,6},{3,7},{4,0},{5,1},{6,2},{7,3},{8,12},{9,13},{10,... | collective-permute-start | bytes 589832 | tf_op jit(solution)/shard_map/ppermute | solution.py:932
  336.6 12.6 %collective-permute-start.50 = (bf16[128,768]{1,0:T(8,128)(2,1)S(1)}, bf16[128,768]{1,0:T(8,128)(2,1)S(1)}, u32[]{:S(2)}, u32[]{:S(2)}) collective-permute-start(bf16[128,768]{1,0:T(8,128)(2,1)S(1)} %get-tuple-element.271), channel_id=1, source_target_pairs={{0,6},{1,7},{2,0},{3,1},{4,2},{5,3},{6,4},{7,5},{8,14},{9,15},{10,... | collective-permute-start | bytes 589832 | tf_op jit(solution)/shard_map/ppermute | solution.py:932
  350.3 3.7 collective-permute-start.52
  354.1 3.7 collective-permute-start.53
  357.8 7.0 %collective-permute-start.54 = (f32[4,1024]{1,0:T(4,128)S(1)}, f32[4,1024]{1,0:T(4,128)S(1)}, u32[]{:S(2)}, u32[]{:S(2)}) collective-permute-start(f32[4,1024]{1,0:T(4,128)S(1)} %add.86), channel_id=1, source_target_pairs={{0,2},{1,3},{2,0},{3,1},{4,6},{5,7},{6,4},{7,5},{8,10},{9,11},{10,... | collective-permute-start | bytes 49160 | tf_op jit(solution)/shard_map/ppermute | solution.py:1001
  364.8 5.7 %collective-permute-start.55 = (f32[4,1024]{1,0:T(4,128)S(1)}, f32[4,1024]{1,0:T(4,128)S(1)}, u32[]{:S(2)}, u32[]{:S(2)}) collective-permute-start(f32[4,1024]{1,0:T(4,128)S(1)} %add.87), channel_id=1, source_target_pairs={{0,4},{1,5},{2,6},{3,7},{4,0},{5,1},{6,2},{7,3},{8,12},{9,13},{10,... | collective-permute-start | bytes 49160 | tf_op jit(solution)/shard_map/ppermute | solution.py:1001
  (109 other events, 604.1 us)
Sparse Core Ops, SparseCore 0:
  10.8 67.7 all-gather.2
  81.3 72.0 all-gather.4
  208.4 86.2 reduce-scatter.4
  298.4 73.9 reduce-scatter.2

commit v2 on v1

--- a/solution.py
+++ b/solution.py
@@ -47,7 +47,7 @@
     return jax.ShapeDtypeStruct(shape, dtype)
 
 
-def launch(body, idx, inputs, outputs, scratch=(), flops=0, vmem=12, name=None):
+def launch(body, idx, inputs, outputs, scratch=(), flops=0, vmem=8, name=None):
     return pl.pallas_call(
         body,
         in_specs=[pl.BlockSpec(memory_space=pltpu.SMEM)]
@@ -250,7 +250,7 @@
         inputs,
         outputs,
         flops=10 * heads * BLOCK * keys * HEAD * 2,
-        vmem=20,
+        vmem=8,
         name=name,
     )
 
@@ -589,7 +589,7 @@
     )
 
 
-def weight_grads(idx, groups, name, before=None, weight=40):
+def weight_grads(idx, groups, name, before=None, weight=40, vmem=8):
     features = groups[0][0][0].shape[1]
     inputs, specs, total, flops = [], [], 0, 0
     for parts in groups:
@@ -630,7 +630,7 @@
         out_specs=pl.BlockSpec((HALF, total), lambda i: (i, 0)),
         out_shape=pltpu.HBM((features, total), bf16),
         compiler_params=pltpu.CompilerParams(
-            dimension_semantics=("arbitrary",), vmem_limit_bytes=20 << 20
+            dimension_semantics=("arbitrary",), vmem_limit_bytes=vmem << 20
         ),
         cost_estimate=cost(weight * flops, inputs),
         name=name,
@@ -979,10 +979,11 @@
             return unpack_grads(self.whole, self.widths, flipped, f"{self.name}_z")
 
     class RowSum:
-        def __init__(self, partial, name, receiver=None, ties=()):
+        def __init__(self, partial, name, receiver=None, ties=(), near=None):
             if pairs:
                 order = after(idx, *ties) if ties else idx
-                self.chip, own = chip_sum(order, partial, to_core(partial), name)
+                near = to_core(partial) if near is None else near
+                self.chip, own = chip_sum(order, partial, near, name)
                 moves = [m for m in chip_pairs if receiver is None or m[1] // 2 == receiver]
                 self.far = lax.ppermute(own, "row", moves)
             else:
@@ -994,12 +995,16 @@
             none = jnp.zeros((HALF, features), bf16)
             return [self.chip, none, none]
 
-    def all_sum(x):
+    def all_sum(x, *held):
+        hops = 0
         for axis, size in (("row", row_devices), ("col", col_devices)):
             step = 1
             while step < size:
+                if hops == 2 and held:
+                    x = after(x, *held)
                 x = x + lax.ppermute(x, axis, [(k, k ^ step) for k in range(size)])
                 step *= 2
+                hops += 1
         return x
 
     depth = to_query.shape[0]
@@ -1214,10 +1219,13 @@
                     *early_grads,
                 )
             ]
-        partials.append(partial)
+        partials.append((partial, to_core(partial) if pairs and b < end else None))
+        ready = after(teacher_all, partials[b][1]) if pairs and b < end else teacher_all
         if b > 0:
-            second_back.append(RowSum(partials[b - 1], f"back_sum{b - 1}", ties=[gm]))
-            ready = after(teacher_all, second_back[b - 1].chip)
+            part, near_part = partials[b - 1]
+            second_back.append(
+                RowSum(part, f"back_sum{b - 1}", ties=[gm], near=near_part)
+            )
     dense_grads = weight_grads(
         idx,
         [[(second_lows[end], 0, gas[end])], [(gms[end], 0, hiddens[end])]],
@@ -1275,6 +1283,7 @@
                 [state_group(k) for k in range(3)] + [token_group(1), token_group(2)],
                 "late_grads",
                 weight=130,
+                vmem=12,
             )
             order = after(idx, late_grads)
             rest_grads = Scattered(
@@ -1282,7 +1291,6 @@
                 "rest_grads",
                 late_grads,
             )
-            rest_grads.send()
             late_grads = lax.psum_scatter(late_grads, "col", scatter_dimension=0, tiled=True)
         trio_sum = RowSum(
             project_back(order, trio_grads[b], near_t, 0, f"trio_back{b}"),
@@ -1325,7 +1333,7 @@
             token_grads[b - 1] = (gq, gk, gv)
         else:
             grad_next, gain_sum = state_back(
-                after(idx, rest_grads.own) if lines else idx,
+                idx,
                 trio_sum.result(*hides),
                 states[b],
                 grad_next,
@@ -1335,6 +1343,8 @@
                 "chain_back0",
             )
         gain_sums.append(gain_sum)
+
+    rest_grads.send(grad_next)
 
     if pairs:
         own_rows = [first.chip for first in first_sums]
@@ -1363,8 +1373,8 @@
         ]
     )
     if lines:
-        sums = after(sums, *rest_grads.far)
-    summed = all_sum(sums)
+        sums = after(sums, rest_grads.own)
+    summed = all_sum(sums, *(rest_grads.far if lines else []))
     total_loss = jnp.sum(summed[0]) / (2.0 * total_tokens)
 
     upper_grad, lower_grad = unpack_grads(

time: 387 us -> 385 us (level)
    ppermute x5, waiting for transfers between devices: 19.4 us -> 4.48 us  [across(): return lax.ppermute(v, 'col', [(k, k ^ 1) for k in range(col_devices)])]
    ppermute x8, waiting for transfers between devices: 29.7 us -> 40.3 us  [__init__(): self.far = lax.ppermute(own, 'row', moves)]
    ppermute x6, waiting for transfers between devices: 13.5 us -> 20.4 us  [along(): return lax.ppermute(v, 'col', moves)]
    unnamed x194 -> x202, local copies, waits for them, and re-layouts: 28.2 us -> 31.5 us
  transfers between devices with their start and end apart: 60 -> 60, of which waited for: 29 -> 33; matrix products, arithmetic and copies ran while one was open for 1% -> 1% of each run, Pallas kernels for 35% -> 33%
where the time goes in v2:
time: 385 us; the launch traced here: 382 us
  waiting for transfers between devices  141 us (37%)
  Pallas kernels  140 us (36%)
  starting transfers between devices  48.1 us (12%)
  local copies, waits for them, and re-layouts  32 us (8%)
  between operations  17.9 us (5%)
    pallas_call x45, Pallas kernels, launch(): pl.pallas_call(body, in_specs=[pl.BlockSpec(memory_space=pltpu.SMEM)] + [...  117 us
    ppermute x8, waiting for transfers between devices, __init__(): self.far = lax.ppermute(own, 'row', moves)  40.3 us
    unnamed x202, local copies, waits for them, and re-layouts  31.5 us
    all_gather x1, waiting for transfers between devices, per_device(): near = lax.all_gather(near, 'col', axis=0, tiled=True)  24.3 us
    ppermute x6, waiting for transfers between devices, along(): return lax.ppermute(v, 'col', moves)  20.4 us
    all_gather x1, waiting for transfers between devices, per_device(): dense = lax.all_gather(after(far_weights, *held), 'col', axis=0, tiled=True)  17.2 us
    pallas_call x3, Pallas kernels, weight_grads(): pl.pallas_call(body, grid=(features // HALF,), in_specs=[pl.BlockSpec(mem...  16.5 us
    ppermute x8, starting transfers between devices, __init__(): self.far = lax.ppermute(own, 'row', moves)  12.5 us
  transfers between devices with their start and end apart: 60, of which 33 were waited for; matrix products, arithmetic and copies ran while one was open for 1% of the time, Pallas kernels for 33%

profile of v2, /device:TPU:0, one launch (start us, length us, event | category | flops | bytes accessed | tf_op | source)
XLA Modules:
  0.0 382.0 jit_solution(4379068907358130821)
XLA Ops:
  7.3 2.3 pack_near.1
  9.8 2.9 pack_rest.1
  12.7 3.0 collective-permute-start.1
  15.7 3.6 collective-permute-start.10
  25.4 11.6 %collective-permute-done.9.refs_2_ = bf16[128,512]{1,0:T(8,128)(2,1)S(1)} collective-permute-done((bf16[128,512]{1,0:T(8,128)(2,1)S(1)}, bf16[128,512]{1,0:T(8,128)(2,1)S(1)}, u32[]{:S(2)}, u32[]{:S(2)}) %collective-permute-start.9) | collective-permute-done | bytes 131104 | tf_op jit(solution)/shard_map/ppermute | solution.py:932
  39.0 2.9 collective-permute-done.13.refs_6_
  55.5 24.3 %all-gather.3.cloned.1.call-done.w_ref.v_ref.refs_11_ = bf16[1024,1536]{1,0:T(8,128)(2,1)} async-done(((bf16[128,1536]{1,0:T(8,128)(2,1)}), bf16[1024,1536]{1,0:T(8,128)(2,1)}) %all-gather.3.cloned.1.call-update) | async-done | bytes 3145744 | tf_op jit(solution)/shard_map/all_gather | solution.py:1018
  87.7 3.4 token_proj.1
  91.1 2.9 token_attend0.1
  94.1 2.9 state_attend0.1
  98.8 7.0 %collective-permute-done.6.refs_2_ = bf16[512,256]{1,0:T(8,128)(2,1)S(1)} collective-permute-done((bf16[512,256]{1,0:T(8,128)(2,1)S(1)}, bf16[512,256]{1,0:T(8,128)(2,1)S(1)}, u32[]{:S(2)}, u32[]{:S(2)}) %collective-permute-start.6) | collective-permute-done | bytes 262176 | tf_op jit(solution)/shard_map/ppermute | solution.py:913
  107.4 5.5 %update0.1 = (f32[512,1024]{1,0:T(8,128)S(1)}, bf16[512,1024]{1,0:T(8,128)(2,1)S(1)}, bf16[512,768]{1,0:T(8,128)(2,1)S(1)}) custom-call(s32[5]{0:T(128)S(1)} %stack.40.s, bf16[512,256]{1,0:T(8,128)(2,1)S(1)} %get-tuple-element.159.refs_0_.refs_8_, bf16[512,256]{1,0:T(8,128)(2,1)S(1)} %collective-permute-done.5.refs_1_, ...), custom_call_target="tpu_custom_call" | custom-call | flops 234881024 | bytes 1024 | tf_op jit(solution)/shard_map/update0/pallas_call | solution.py:51
  113.9 3.7 token_attend1.1
  119.7 2.9 state_attend1.1
  122.6 3.5 collective-permute-done.20.refs_2_
  126.1 3.6 out0.1
  131.1 3.9 %out1.1 = (f32[512,1024]{1,0:T(8,128)S(1)}, bf16[512,1024]{1,0:T(8,128)(2,1)S(1)}) custom-call(s32[5]{0:T(128)S(1)} %stack.40.s, bf16[512,256]{1,0:T(8,128)(2,1)S(1)} %get-tuple-element.169.refs_0_.refs_6_, bf16[512,256]{1,0:T(8,128)(2,1)S(1)} %collective-permute-done.19.refs_1_, bf16[512,256]{1,0:T(8,128)(2,1)S(1)} %collective-permute-done.20.refs_2_, ...), custom_call_target="tpu_custom_call" | custom-call | flops 134217728 | bytes 1024 | tf_op jit(solution)/shard_map/out1/pallas_call | solution.py:51
  137.3 17.2 %all-gather.5.cloned.1.call-done.v_ref.up_ref.refs_8_ = bf16[1024,2048]{1,0:T(8,128)(2,1)} async-done(((bf16[128,2048]{1,0:T(8,128)(2,1)}), bf16[1024,2048]{1,0:T(8,128)(2,1)}) %all-gather.5.cloned.1.call-update) | async-done | bytes 4194320 | tf_op jit(solution)/shard_map/all_gather | solution.py:1040
  158.1 4.2 %dense0.1 = (bf16[512,1024]{1,0:T(8,128)(2,1)S(1)}, bf16[512,1024]{1,0:T(8,128)(2,1)S(1)}, bf16[512,1024]{1,0:T(8,128)(2,1)S(1)}) custom-call(s32[5]{0:T(128)S(1)} %stack.40.s, bf16[512,1024]{1,0:T(8,128)(2,1)S(1)} %copy-done.66, bf16[1024,2048]{1,0:T(8,128)(2,1)S(1)} %copy-done, bf16[1024,1024]{1,0:T(8,128)(2,1)S(1)} %down_turn.1.down_ref), custom_call_target="tpu_custom_call" | custom-call | flops 268435456 | bytes 1024 | tf_op jit(solution)/shard_map/dense0/pallas_call | solution.py:51
  167.5 4.4 %dense1.1 = (bf16[512,1024]{1,0:T(8,128)(2,1)S(1)}, bf16[512,1024]{1,0:T(8,128)(2,1)S(1)}, bf16[512,1024]{1,0:T(8,128)(2,1)S(1)}) custom-call(s32[5]{0:T(128)S(1)} %stack.40.s, bf16[512,1024]{1,0:T(8,128)(2,1)S(1)} %copy-done.64, bf16[1024,2048]{1,0:T(8,128)(2,1)S(1)} %copy-done.1, bf16[1024,1024]{1,0:T(8,128)(2,1)S(1)} %down_turn.1.down_ref), custom_call_target="tpu_custom_call" | custom-call | flops 268435456 | bytes 1024 | tf_op jit(solution)/shard_map/dense1/pallas_call | solution.py:51
  173.1 4.4 %state_back1.1 = (bf16[512,256]{1,0:T(8,128)(2,1)S(1)}, f32[512,256]{1,0:T(8,128)S(1)}, f32[512,256]{1,0:T(8,128)S(1)}, f32[512,256]{1,0:T(8,128)S(1)}, f32[512,256]{1,0:T(8,128)S(1)}) custom-call(s32[5]{0:T(128)S(1)} %stack.40.s, bf16[512,768]{1,0:T(8,128)(2,1)S(1)} %copy-done.12, bf16[1024,768]{1,0:T(8,128)(2,1)S(1)} %get-tuple-element.155.refs_0_.refs_1_, ...), custom_call_target="tpu_custom_call" | custom-call | flops 335544320 | bytes 1024 | tf_op jit(solution)/shard_map/state_back1/pallas_call | solution.py:51
  182.5 4.2 %back0.1 = (bf16[512,1024]{1,0:T(8,128)(2,1)S(1)}, bf16[512,1024]{1,0:T(8,128)(2,1)S(1)}, f32[1,1024]{1,0:T(1,128)S(1)}, bf16[512,1024]{1,0:T(8,128)(2,1)S(1)}) custom-call(s32[5]{0:T(128)S(1)} %stack.40.s, bf16[512,1024]{1,0:T(8,128)(2,1)S(1)} %get-tuple-element.177.refs_0_, bf16[256,1024]{1,0:T(8,128)(2,1)S(1)} %collective-permute-done.23.refs_1_, ...), custom_call_target="tpu_custom_call" | custom-call | flops 268435456 | bytes 1024 | tf_op jit(solution)/shard_map/back0/pallas_call | solution.py:51
  187.0 4.9 %dense_grads0.1.refs_4_ = bf16[1024,2048]{1,0:T(8,128)(2,1)} custom-call(s32[5]{0:T(128)S(1)} %stack.40.s, bf16[512,1024]{1,0:T(8,128)(2,1)S(1)} %copy-done.66, bf16[512,1024]{1,0:T(8,128)(2,1)S(1)} %get-tuple-element.195.refs_1_, bf16[512,1024]{1,0:T(8,128)(2,1)S(1)} %get-tuple-element.194.refs_2_.refs_3_, bf16[512,1024]{1,0:T(8,128)(2,1)S(1)} %get-tuple-element.173.refs_3_), custom_call_target="tpu_custom_call" | custom-call | flops 10737418240 | bytes 1024 | tf_op jit(solution)/shard_map/dense_grads0/pallas_call | solution.py:626
  192.0 3.4 collective-permute-done.26.refs_1_
  197.3 5.2 %back1.1 = (bf16[512,1024]{1,0:T(8,128)(2,1)S(1)}, bf16[512,1024]{1,0:T(8,128)(2,1)S(1)}, f32[1,1024]{1,0:T(1,128)S(1)}, bf16[512,1024]{1,0:T(8,128)(2,1)}) custom-call(s32[5]{0:T(128)S(1)} %stack.40.s, bf16[512,1024]{1,0:T(8,128)(2,1)S(1)} %get-tuple-element.192.refs_0_, bf16[256,1024]{1,0:T(8,128)(2,1)S(1)} %collective-permute-done.26.refs_1_, ...), custom_call_target="tpu_custom_call" | custom-call | flops 268435456 | bytes 1024 | tf_op jit(solution)/shard_map/back1/pallas_call | solution.py:51
  202.6 4.9 %dense_grads.1 = bf16[1024,2048]{1,0:T(8,128)(2,1)} custom-call(s32[5]{0:T(128)S(1)} %stack.40.s, bf16[512,1024]{1,0:T(8,128)(2,1)S(1)} %copy-done.64, bf16[512,1024]{1,0:T(8,128)(2,1)S(1)} %get-tuple-element.211.refs_1_, bf16[512,1024]{1,0:T(8,128)(2,1)S(1)} %get-tuple-element.203.refs_2_.refs_3_, bf16[512,1024]{1,0:T(8,128)(2,1)S(1)} %get-tuple-element.180.refs_3_, ...), custom_call_target="tpu_custom_call" | custom-call | flops 10737418240 | bytes 1024 | tf_op jit(solution)/shard_map/dense_grads/pallas_call | solution.py:626
  213.9 12.8 %collective-permute-done.29.refs_1_ = bf16[256,1024]{1,0:T(8,128)(2,1)S(1)} collective-permute-done((bf16[256,1024]{1,0:T(8,128)(2,1)S(1)}, bf16[256,1024]{1,0:T(8,128)(2,1)S(1)}, u32[]{:S(2)}, u32[]{:S(2)}) %collective-permute-start.29) | collective-permute-done | bytes 524320 | tf_op jit(solution)/shard_map/ppermute | solution.py:988
  230.1 2.3 out_back0.1
  232.5 4.5 %token_back0.1 = (bf16[512,256]{1,0:T(8,128)(2,1)S(1)}, f32[512,256]{1,0:T(8,128)S(1)}, f32[512,256]{1,0:T(8,128)S(1)}, f32[512,256]{1,0:T(8,128)S(1)}, f32[512,256]{1,0:T(8,128)S(1)}) custom-call(s32[5]{0:T(128)S(1)} %stack.40.s, bf16[1024,768]{1,0:T(8,128)(2,1)S(1)} %get-tuple-element.155.refs_0_.refs_1_, bf16[512,768]{1,0:T(8,128)(2,1)S(1)} %copy-done.15, ...), custom_call_target="tpu_custom_call" | custom-call | flops 335544320 | bytes 1024 | tf_op jit(solution)/shard_map/token_back0/pallas_call | solution.py:51
  237.8 5.3 %collective-permute-done.32.refs_1_ = bf16[256,1024]{1,0:T(8,128)(2,1)S(1)} collective-permute-done((bf16[256,1024]{1,0:T(8,128)(2,1)S(1)}, bf16[256,1024]{1,0:T(8,128)(2,1)S(1)}, u32[]{:S(2)}, u32[]{:S(2)}) %collective-permute-start.32) | collective-permute-done | bytes 524320 | tf_op jit(solution)/shard_map/ppermute | solution.py:988
  249.7 5.6 %token_back1.1 = (bf16[512,256]{1,0:T(8,128)(2,1)S(1)}, f32[512,256]{1,0:T(8,128)S(1)}, f32[512,256]{1,0:T(8,128)S(1)}, bf16[512,256]{1,0:T(8,128)(2,1)S(1)}, bf...) custom-call(s32[5]{0:T(128)S(1)} %stack.40.s, ...), custom_call_target="tpu_custom_call" | custom-call | flops 503316480 | bytes 1024 | tf_op jit(solution)/shard_map/token_back1/pallas_call | solution.py:51
  258.4 2.6 collective-permute-done.35.b_ref
  266.7 4.7 %update_last.1 = f32[512,1024]{1,0:T(8,128)} custom-call(s32[5]{0:T(128)S(1)} %stack.40.s, bf16[512,256]{1,0:T(8,128)(2,1)S(1)} %copy-done.49, bf16[512,256]{1,0:T(8,128)(2,1)S(1)} %collective-permute-done.37.refs_1_, bf16[512,256]{1,0:T(8,128)(2,1)S(1)} %collective-permute-done.34.refs_2_, bf16[512,256]{1,0:T(8,128)(2,1)S(1)} %collective-permute-done.38.refs_3_, ...), custom_call_target="tpu_custom_call" | custom-call | flops 134217728 | bytes 1024 | tf_op jit(solution)/shard_map/update_last/pallas_call | solution.py:51
  271.4 4.7 %collective-permute-done.36.refs_1_ = bf16[256,1024]{1,0:T(8,128)(2,1)S(1)} collective-permute-done((bf16[256,1024]{1,0:T(8,128)(2,1)S(1)}, bf16[256,1024]{1,0:T(8,128)(2,1)S(1)}, u32[]{:S(2)}, u32[]{:S(2)}) %collective-permute-start.36) | collective-permute-done | bytes 524320 | tf_op jit(solution)/shard_map/ppermute | solution.py:988
  277.9 2.5 chain_back1.1
  281.8 4.4 %state_back0.1 = (bf16[512,256]{1,0:T(8,128)(2,1)S(1)}, bf16[512,256]{1,0:T(8,128)(2,1)S(1)}, bf16[512,256]{1,0:T(8,128)(2,1)S(1)}, bf16[512,256]{1,0:T(8,128)(2,1)S(1)}, bf16[512,256]{1,0:T(8,128)(2,1)S(1)}) custom-call(s32[5]{0:T(128)S(1)} %stack.40.s, bf16[512,768]{1,0:T(8,128)(2,1)S(1)} %copy-done.15, ...), custom_call_target="tpu_custom_call" | custom-call | flops 335544320 | bytes 1024 | tf_op jit(solution)/shard_map/state_back0/pallas_call | solution.py:51
  286.2 6.7 %late_grads.1 = bf16[1024,1280]{1,0:T(8,128)(2,1)} custom-call(s32[5]{0:T(128)S(1)} %stack.40.s, bf16[512,1024]{1,0:T(8,128)(2,1)S(1)} %copy-done.94, bf16[512,256]{1,0:T(8,128)(2,1)S(1)} %get-tuple-element.255.refs_1_.refs_0_, bf16[512,1024]{1,0:T(8,128)(2,1)S(1)} %copy-done.96, bf16[512,256]{1,0:T(8,128)(2,1)S(1)} %copy-done.78, ...), custom_call_target="tpu_custom_call" | custom-call | flops 43620761600 | bytes 1024 | tf_op jit(solution)/shard_map/late_grads/pallas_call | solution.py:626
  306.2 3.4 rest_grads.1
  311.3 2.5 collective-permute-start.43
  316.1 2.9 collective-permute-done.45.refs_1_
  319.0 10.0 %collective-permute-done.43.refs_3_ = bf16[256,1024]{1,0:T(8,128)(2,1)S(1)} collective-permute-done((bf16[256,1024]{1,0:T(8,128)(2,1)S(1)}, bf16[256,1024]{1,0:T(8,128)(2,1)S(1)}, u32[]{:S(2)}, u32[]{:S(2)}) %collective-permute-start.43) | collective-permute-done | bytes 524320 | tf_op jit(solution)/shard_map/ppermute | solution.py:988
  330.1 2.4 input_rows.1
  332.5 3.2 chain_back0.1
  338.6 2.4 collective-permute-start.52
  346.2 6.3 %collective-permute-done.51.refs_1_ = bf16[128,768]{1,0:T(8,128)(2,1)S(1)} collective-permute-done((bf16[128,768]{1,0:T(8,128)(2,1)S(1)}, bf16[128,768]{1,0:T(8,128)(2,1)S(1)}, u32[]{:S(2)}, u32[]{:S(2)}) %collective-permute-start.51) | collective-permute-done | bytes 196640 | tf_op jit(solution)/shard_map/ppermute | solution.py:932
  353.6 2.7 collective-permute-done.53
  356.3 4.1 %collective-permute-start.54 = (f32[4,1024]{1,0:T(4,128)S(1)}, f32[4,1024]{1,0:T(4,128)S(1)}, u32[]{:S(2)}, u32[]{:S(2)}) collective-permute-start(f32[4,1024]{1,0:T(4,128)S(1)} %add.86), channel_id=1, source_target_pairs={{0,2},{1,3},{2,0},{3,1},{4,6},{5,7},{6,4},{7,5},{8,10},{9,11},{10,... | collective-permute-start | bytes 49160 | tf_op jit(solution)/shard_map/ppermute | solution.py:1005
  364.8 3.0 collective-permute-done.55
  (354 shorter events, 122.3 us)
Async XLA Ops:
  7.2 72.6 %all-gather.3.cloned.1.call-start = ((), (), s32[]{:S(2)}) async-start(), calls=%async_computation.2 | async-start | bytes 3538944 | tf_op jit(solution)/shard_map/all_gather | solution.py:1018
  9.7 144.8 %all-gather.5.cloned.1.call-start = ((), (), s32[]{:S(2)}) async-start(), calls=%async_computation.3 | async-start | bytes 4718592 | tf_op jit(solution)/shard_map/all_gather | solution.py:1040
  12.7 33.4 %collective-permute-start.1 = (bf16[512,1024]{1,0:T(8,128)(2,1)S(1)}, bf16[512,1024]{1,0:T(8,128)(2,1)}, u32[]{:S(2)}, u32[]{:S(2)}) collective-permute-start(bf16[512,1024]{1,0:T(8,128)(2,1)S(1)} %get-tuple-element.153.refs_0_), channel_id=1, source_target_pairs={{0,16},{8,24},{16,0},{24,8},{1,17},{9,25},{17,1},{25,9},{2,18},{10... | collective-permute-start | bytes 3145736 | tf_op jit(solution)/shard_map/ppermute | solution.py:913
  15.7 8.4 %collective-permute-start.10 = (bf16[128,512]{1,0:T(8,128)(2,1)S(1)}, bf16[128,512]{1,0:T(8,128)(2,1)S(1)}, u32[]{:S(2)}, u32[]{:S(2)}) collective-permute-start(bf16[128,512]{1,0:T(8,128)(2,1)S(1)} %get-tuple-element.161.refs_0_), channel_id=1, source_target_pairs={{0,6},{1,7},{2,0},{3,1},{4,2},{5,3},{6,4},{7,5},{8,14},{9,15},{10,... | collective-permute-start | bytes 393224 | tf_op jit(solution)/shard_map/ppermute | solution.py:932
  19.3 17.7 %collective-permute-start.9 = (bf16[128,512]{1,0:T(8,128)(2,1)S(1)}, bf16[128,512]{1,0:T(8,128)(2,1)S(1)}, u32[]{:S(2)}, u32[]{:S(2)}) collective-permute-start(bf16[128,512]{1,0:T(8,128)(2,1)S(1)} %get-tuple-element.161.refs_0_), channel_id=1, source_target_pairs={{0,4},{1,5},{2,6},{3,7},{4,0},{5,1},{6,2},{7,3},{8,12},{9,13},{10,... | collective-permute-start | bytes 393224 | tf_op jit(solution)/shard_map/ppermute | solution.py:932
  19.3 19.3 %collective-permute-start.8 = (bf16[128,512]{1,0:T(8,128)(2,1)S(1)}, bf16[128,512]{1,0:T(8,128)(2,1)S(1)}, u32[]{:S(2)}, u32[]{:S(2)}) collective-permute-start(bf16[128,512]{1,0:T(8,128)(2,1)S(1)} %get-tuple-element.161.refs_0_), channel_id=1, source_target_pairs={{0,2},{1,3},{2,4},{3,5},{4,6},{5,7},{6,0},{7,1},{8,10},{9,11},{10,... | collective-permute-start | bytes 393224 | tf_op jit(solution)/shard_map/ppermute | solution.py:932
  20.3 18.7 %collective-permute-start.11 = (bf16[128,512]{1,0:T(8,128)(2,1)S(1)}, bf16[128,512]{1,0:T(8,128)(2,1)S(1)}, u32[]{:S(2)}, u32[]{:S(2)}) collective-permute-start(bf16[128,512]{1,0:T(8,128)(2,1)S(1)} %get-tuple-element.161.refs_0_), channel_id=1, source_target_pairs={{0,1},{1,0},{2,3},{3,2},{4,5},{5,4},{6,7},{7,6},{8,9},{9,8},{10,11... | collective-permute-start | bytes 393224 | tf_op jit(solution)/shard_map/ppermute | solution.py:935
  24.0 15.0 %collective-permute-start.14 = (bf16[128,512]{1,0:T(8,128)(2,1)S(1)}, bf16[128,512]{1,0:T(8,128)(2,1)S(1)}, u32[]{:S(2)}, u32[]{:S(2)}) collective-permute-start(bf16[128,512]{1,0:T(8,128)(2,1)S(1)} %collective-permute-done.10.refs_3_), channel_id=1, source_target_pairs={{0,1},{1,0},{2,3},{3,2},{4,5},{5,4},{6,7},{7,6},{8,9},{9,8},{10,11... | collective-permute-start | bytes 393224 | tf_op jit(solution)/shard_map/ppermute | solution.py:935
  37.0 5.0 %collective-permute-start.13 = (bf16[128,512]{1,0:T(8,128)(2,1)S(1)}, bf16[128,512]{1,0:T(8,128)(2,1)S(1)}, u32[]{:S(2)}, u32[]{:S(2)}) collective-permute-start(bf16[128,512]{1,0:T(8,128)(2,1)S(1)} %collective-permute-done.9.refs_2_), channel_id=1, source_target_pairs={{0,1},{1,0},{2,3},{3,2},{4,5},{5,4},{6,7},{7,6},{8,9},{9,8},{10,11... | collective-permute-start | bytes 393224 | tf_op jit(solution)/shard_map/ppermute | solution.py:935
  38.5 5.0 %collective-permute-start.12 = (bf16[128,512]{1,0:T(8,128)(2,1)S(1)}, bf16[128,512]{1,0:T(8,128)(2,1)S(1)}, u32[]{:S(2)}, u32[]{:S(2)}) collective-permute-start(bf16[128,512]{1,0:T(8,128)(2,1)S(1)} %collective-permute-done.8.refs_1_), channel_id=1, source_target_pairs={{0,1},{1,0},{2,3},{3,2},{4,5},{5,4},{6,7},{7,6},{8,9},{9,8},{10,11... | collective-permute-start | bytes 393224 | tf_op jit(solution)/shard_map/ppermute | solution.py:935
  46.1 323.7 %reduce-scatter.5.cloned.1.call-start = ((), (), s32[]{:S(2)}) async-start(), calls=%async_computation.5 | async-start | bytes 4718592 | tf_op jit(solution)/shard_map/reduce_scatter | solution.py:1238
  46.3 4.4 %collective-permute-start.2 = (bf16[512,1024]{1,0:T(8,128)(2,1)}, bf16[512,1024]{1,0:T(8,128)(2,1)}, u32[]{:S(2)}, u32[]{:S(2)}) collective-permute-start(bf16[512,1024]{1,0:T(8,128)(2,1)} %collective-permute-done.1.refs_2_), channel_id=1, source_target_pairs={{0,8},{8,0},{16,24},{24,16},{1,9},{9,1},{17,25},{25,17},{2,10},{10... | collective-permute-start | bytes 3145736 | tf_op jit(solution)/shard_map/ppermute | solution.py:910
  47.0 47.0 %collective-permute-start.16 = (bf16[512,1024]{1,0:T(8,128)(2,1)}, bf16[512,1024]{1,0:T(8,128)(2,1)}, u32[]{:S(2)}, u32[]{:S(2)}) collective-permute-start(bf16[512,1024]{1,0:T(8,128)(2,1)} %mid_turn.1.refs_4_), channel_id=1, source_target_pairs={{0,16},{8,24},{16,0},{24,8},{1,17},{9,25},{17,1},{25,9},{2,18},{10... | collective-permute-start | bytes 3145736 | tf_op jit(solution)/shard_map/ppermute | solution.py:913
  49.0 58.3 %collective-permute-start.15 = (bf16[512,1024]{1,0:T(8,128)(2,1)}, bf16[512,1024]{1,0:T(8,128)(2,1)}, u32[]{:S(2)}, u32[]{:S(2)}) collective-permute-start(bf16[512,1024]{1,0:T(8,128)(2,1)} %mid_turn.1.refs_4_), channel_id=1, source_target_pairs={{0,8},{8,0},{16,24},{24,16},{1,9},{9,1},{17,25},{25,17},{2,10},{10... | collective-permute-start | bytes 3145736 | tf_op jit(solution)/shard_map/ppermute | solution.py:910
  94.1 13.3 %collective-permute-start.17 = (bf16[512,1024]{1,0:T(8,128)(2,1)}, bf16[512,1024]{1,0:T(8,128)(2,1)S(1)}, u32[]{:S(2)}, u32[]{:S(2)}) collective-permute-start(bf16[512,1024]{1,0:T(8,128)(2,1)} %collective-permute-done.16.refs_6_), channel_id=1, source_target_pairs={{0,8},{8,0},{16,24},{24,16},{1,9},{9,1},{17,25},{25,17},{2,10},{10... | collective-permute-start | bytes 3145736 | tf_op jit(solution)/shard_map/ppermute | solution.py:910
  97.1 8.8 %collective-permute-start.6 = (bf16[512,256]{1,0:T(8,128)(2,1)S(1)}, bf16[512,256]{1,0:T(8,128)(2,1)S(1)}, u32[]{:S(2)}, u32[]{:S(2)}) collective-permute-start(bf16[512,256]{1,0:T(8,128)(2,1)S(1)} %get-tuple-element.159.refs_0_.refs_8_), channel_id=1, source_target_pairs={{0,16},{8,24},{16,0},{24,8},{1,17},{9,25},{17,1},{25,9},{2,18},{10... | collective-permute-start | bytes 786440 | tf_op jit(solution)/shard_map/ppermute | solution.py:913
  98.6 8.7 %collective-permute-start.5 = (bf16[512,256]{1,0:T(8,128)(2,1)S(1)}, bf16[512,256]{1,0:T(8,128)(2,1)S(1)}, u32[]{:S(2)}, u32[]{:S(2)}) collective-permute-start(bf16[512,256]{1,0:T(8,128)(2,1)S(1)} %get-tuple-element.159.refs_0_.refs_8_), channel_id=1, source_target_pairs={{0,8},{8,0},{16,24},{24,16},{1,9},{9,1},{17,25},{25,17},{2,10},{10... | collective-permute-start | bytes 786440 | tf_op jit(solution)/shard_map/ppermute | solution.py:910
  105.8 13.9 %collective-permute-start.4 = (bf16[512,256]{1,0:T(8,128)(2,1)S(1)}, bf16[512,256]{1,0:T(8,128)(2,1)S(1)}, u32[]{:S(2)}, u32[]{:S(2)}) collective-permute-start(bf16[512,256]{1,0:T(8,128)(2,1)S(1)} %get-tuple-element.158.refs_0_.refs_4_), channel_id=1, source_target_pairs={{0,16},{8,24},{16,0},{24,8},{1,17},{9,25},{17,1},{25,9},{2,18},{10... | collective-permute-start | bytes 786440 | tf_op jit(solution)/shard_map/ppermute | solution.py:913
  117.6 8.5 %collective-permute-start.20 = (bf16[512,256]{1,0:T(8,128)(2,1)S(1)}, bf16[512,256]{1,0:T(8,128)(2,1)S(1)}, u32[]{:S(2)}, u32[]{:S(2)}) collective-permute-start(bf16[512,256]{1,0:T(8,128)(2,1)S(1)} %get-tuple-element.169.refs_0_.refs_6_), channel_id=1, source_target_pairs={{0,16},{8,24},{16,0},{24,8},{1,17},{9,25},{17,1},{25,9},{2,18},{10... | collective-permute-start | bytes 786440 | tf_op jit(solution)/shard_map/ppermute | solution.py:913
  119.2 6.9 %collective-permute-start.3 = (bf16[512,256]{1,0:T(8,128)(2,1)S(1)}, bf16[512,256]{1,0:T(8,128)(2,1)S(1)}, u32[]{:S(2)}, u32[]{:S(2)}) collective-permute-start(bf16[512,256]{1,0:T(8,128)(2,1)S(1)} %get-tuple-element.158.refs_0_.refs_4_), channel_id=1, source_target_pairs={{0,8},{8,0},{16,24},{24,16},{1,9},{9,1},{17,25},{25,17},{2,10},{10... | collective-permute-start | bytes 786440 | tf_op jit(solution)/shard_map/ppermute | solution.py:910
  119.2 11.8 %collective-permute-start.19 = (bf16[512,256]{1,0:T(8,128)(2,1)S(1)}, bf16[512,256]{1,0:T(8,128)(2,1)S(1)}, u32[]{:S(2)}, u32[]{:S(2)}) collective-permute-start(bf16[512,256]{1,0:T(8,128)(2,1)S(1)} %get-tuple-element.169.refs_0_.refs_6_), channel_id=1, source_target_pairs={{0,8},{8,0},{16,24},{24,16},{1,9},{9,1},{17,25},{25,17},{2,10},{10... | collective-permute-start | bytes 786440 | tf_op jit(solution)/shard_map/ppermute | solution.py:910
  119.7 6.4 %collective-permute-start.18 = (bf16[512,256]{1,0:T(8,128)(2,1)S(1)}, bf16[512,256]{1,0:T(8,128)(2,1)S(1)}, u32[]{:S(2)}, u32[]{:S(2)}) collective-permute-start(bf16[512,256]{1,0:T(8,128)(2,1)S(1)} %collective-permute-done.4.refs_2_), channel_id=1, source_target_pairs={{0,8},{8,0},{16,24},{24,16},{1,9},{9,1},{17,25},{25,17},{2,10},{10... | collective-permute-start | bytes 786440 | tf_op jit(solution)/shard_map/ppermute | solution.py:910
  126.1 4.9 %collective-permute-start.21 = (bf16[512,256]{1,0:T(8,128)(2,1)S(1)}, bf16[512,256]{1,0:T(8,128)(2,1)S(1)}, u32[]{:S(2)}, u32[]{:S(2)}) collective-permute-start(bf16[512,256]{1,0:T(8,128)(2,1)S(1)} %collective-permute-done.20.refs_2_), channel_id=1, source_target_pairs={{0,8},{8,0},{16,24},{24,16},{1,9},{9,1},{17,25},{25,17},{2,10},{10... | collective-permute-start | bytes 786440 | tf_op jit(solution)/shard_map/ppermute | solution.py:910
  166.0 14.0 %collective-permute-start.23 = (bf16[256,1024]{1,0:T(8,128)(2,1)S(1)}, bf16[256,1024]{1,0:T(8,128)(2,1)S(1)}, u32[]{:S(2)}, u32[]{:S(2)}) collective-permute-start(bf16[256,1024]{1,0:T(8,128)(2,1)S(1)} %get-tuple-element.178), channel_id=1, source_target_pairs={{0,16},{8,24},{16,0},{24,8},{1,17},{9,25},{17,1},{25,9},{2,18},{10... | collective-permute-start | bytes 1572872 | tf_op jit(solution)/shard_map/ppermute | solution.py:988
  171.9 8.4 %collective-permute-start.25 = (bf16[512,1024]{1,0:T(8,128)(2,1)S(1)}, bf16[512,1024]{1,0:T(8,128)(2,1)S(1)}, u32[]{:S(2)}, u32[]{:S(2)}) collective-permute-start(bf16[512,1024]{1,0:T(8,128)(2,1)S(1)} %get-tuple-element.191.a_ref), channel_id=1, source_target_pairs={{0,8},{8,0},{16,24},{24,16},{1,9},{9,1},{17,25},{25,17},{2,10},{10... | collective-permute-start | bytes 3145736 | tf_op jit(solution)/shard_map/ppermute | solution.py:910
  181.3 14.1 %collective-permute-start.26 = (bf16[256,1024]{1,0:T(8,128)(2,1)S(1)}, bf16[256,1024]{1,0:T(8,128)(2,1)S(1)}, u32[]{:S(2)}, u32[]{:S(2)}) collective-permute-start(bf16[256,1024]{1,0:T(8,128)(2,1)S(1)} %get-tuple-element.193), channel_id=1, source_target_pairs={{0,16},{8,24},{16,0},{24,8},{1,17},{9,25},{17,1},{25,9},{2,18},{10... | collective-permute-start | bytes 1572872 | tf_op jit(solution)/shard_map/ppermute | solution.py:988
  186.7 8.6 %collective-permute-start.28 = (bf16[512,1024]{1,0:T(8,128)(2,1)S(1)}, bf16[512,1024]{1,0:T(8,128)(2,1)S(1)}, u32[]{:S(2)}, u32[]{:S(2)}) collective-permute-start(bf16[512,1024]{1,0:T(8,128)(2,1)S(1)} %get-tuple-element.198.a_ref), channel_id=1, source_target_pairs={{0,8},{8,0},{16,24},{24,16},{1,9},{9,1},{17,25},{25,17},{2,10},{10... | collective-permute-start | bytes 3145736 | tf_op jit(solution)/shard_map/ppermute | solution.py:910
  202.5 24.2 %collective-permute-start.31 = (bf16[512,1024]{1,0:T(8,128)(2,1)}, bf16[512,1024]{1,0:T(8,128)(2,1)}, u32[]{:S(2)}, u32[]{:S(2)}) collective-permute-start(bf16[512,1024]{1,0:T(8,128)(2,1)} %get-tuple-element.213.a_ref), channel_id=1, source_target_pairs={{0,8},{8,0},{16,24},{24,16},{1,9},{9,1},{17,25},{25,17},{2,10},{10... | collective-permute-start | bytes 3145736 | tf_op jit(solution)/shard_map/ppermute | solution.py:910
  208.6 163.6 %reduce-scatter.3.cloned.1.call-start = ((), (), s32[]{:S(2)}) async-start(), calls=%async_computation.4 | async-start | bytes 2949120 | tf_op jit(solution)/shard_map/reduce_scatter | solution.py:1294
  212.3 14.3 %collective-permute-start.29 = (bf16[256,1024]{1,0:T(8,128)(2,1)S(1)}, bf16[256,1024]{1,0:T(8,128)(2,1)S(1)}, u32[]{:S(2)}, u32[]{:S(2)}) collective-permute-start(bf16[256,1024]{1,0:T(8,128)(2,1)S(1)} %get-tuple-element.206), channel_id=1, source_target_pairs={{0,16},{8,24},{16,0},{24,8},{1,17},{9,25},{17,1},{25,9},{2,18},{10... | collective-permute-start | bytes 1572872 | tf_op jit(solution)/shard_map/ppermute | solution.py:988
  226.6 3.5 collective-permute-start.30
  228.6 14.4 %collective-permute-start.32 = (bf16[256,1024]{1,0:T(8,128)(2,1)S(1)}, bf16[256,1024]{1,0:T(8,128)(2,1)S(1)}, u32[]{:S(2)}, u32[]{:S(2)}) collective-permute-start(bf16[256,1024]{1,0:T(8,128)(2,1)S(1)} %get-tuple-element.215), channel_id=1, source_target_pairs={{0,16},{8,24},{16,0},{24,8},{1,17},{9,25},{17,1},{25,9},{2,18},{10... | collective-permute-start | bytes 1572872 | tf_op jit(solution)/shard_map/ppermute | solution.py:988
  248.3 8.3 %collective-permute-start.34 = (bf16[512,256]{1,0:T(8,128)(2,1)S(1)}, bf16[512,256]{1,0:T(8,128)(2,1)S(1)}, u32[]{:S(2)}, u32[]{:S(2)}) collective-permute-start(bf16[512,256]{1,0:T(8,128)(2,1)S(1)} %copy-done.49), channel_id=1, source_target_pairs={{0,16},{8,24},{16,0},{24,8},{1,17},{9,25},{17,1},{25,9},{2,18},{10... | collective-permute-start | bytes 786440 | tf_op jit(solution)/shard_map/ppermute | solution.py:913
  262.0 14.0 %collective-permute-start.36 = (bf16[256,1024]{1,0:T(8,128)(2,1)S(1)}, bf16[256,1024]{1,0:T(8,128)(2,1)S(1)}, u32[]{:S(2)}, u32[]{:S(2)}) collective-permute-start(bf16[256,1024]{1,0:T(8,128)(2,1)S(1)} %get-tuple-element.228), channel_id=1, source_target_pairs={{0,16},{8,24},{16,0},{24,8},{1,17},{9,25},{17,1},{25,9},{2,18},{10... | collective-permute-start | bytes 1572872 | tf_op jit(solution)/shard_map/ppermute | solution.py:988
  301.2 9.1 %collective-permute-start.41 = (bf16[512,1024]{1,0:T(8,128)(2,1)S(1)}, bf16[512,1024]{1,0:T(8,128)(2,1)S(1)}, u32[]{:S(2)}, u32[]{:S(2)}) collective-permute-start(bf16[512,1024]{1,0:T(8,128)(2,1)S(1)} %copy-done.29), channel_id=1, source_target_pairs={{0,8},{8,0},{16,24},{24,16},{1,9},{9,1},{17,25},{25,17},{2,10},{10... | collective-permute-start | bytes 3145736 | tf_op jit(solution)/shard_map/ppermute | solution.py:910
  303.4 10.4 %collective-permute-start.40 = (bf16[512,1024]{1,0:T(8,128)(2,1)S(1)}, bf16[512,1024]{1,0:T(8,128)(2,1)S(1)}, u32[]{:S(2)}, u32[]{:S(2)}) collective-permute-start(bf16[512,1024]{1,0:T(8,128)(2,1)S(1)} %first_back0.1.a_ref), channel_id=1, source_target_pairs={{0,8},{8,0},{16,24},{24,16},{1,9},{9,1},{17,25},{25,17},{2,10},{10... | collective-permute-start | bytes 3145736 | tf_op jit(solution)/shard_map/ppermute | solution.py:910
  304.7 14.3 %collective-permute-start.45 = (bf16[256,1024]{1,0:T(8,128)(2,1)S(1)}, bf16[256,1024]{1,0:T(8,128)(2,1)S(1)}, u32[]{:S(2)}, u32[]{:S(2)}) collective-permute-start(bf16[256,1024]{1,0:T(8,128)(2,1)S(1)} %get-tuple-element.262), channel_id=1, source_target_pairs={{0,16},{8,24},{16,0},{24,8},{1,17},{9,25},{17,1},{25,9},{2,18},{10... | collective-permute-start | bytes 1572872 | tf_op jit(solution)/shard_map/ppermute | solution.py:988
  309.7 26.0 %collective-permute-start.47 = (bf16[512,768]{1,0:T(8,128)(2,1)S(1)}, bf16[512,768]{1,0:T(8,128)(2,1)S(1)}, u32[]{:S(2)}, u32[]{:S(2)}) collective-permute-start(bf16[512,768]{1,0:T(8,128)(2,1)S(1)} %get-tuple-element.271), channel_id=1, source_target_pairs={{0,1},{1,0},{2,3},{3,2},{4,5},{5,4},{6,7},{7,6},{8,9},{9,8},{10,11... | collective-permute-start | bytes 2359304 | tf_op jit(solution)/shard_map/ppermute | solution.py:935
  311.3 17.7 %collective-permute-start.43 = (bf16[256,1024]{1,0:T(8,128)(2,1)S(1)}, bf16[256,1024]{1,0:T(8,128)(2,1)S(1)}, u32[]{:S(2)}, u32[]{:S(2)}) collective-permute-start(bf16[256,1024]{1,0:T(8,128)(2,1)S(1)} %get-tuple-element.247), channel_id=1, source_target_pairs={{0,16},{8,24},{1,17},{9,25},{2,18},{10,26},{3,19},{11,27},{4,20},{... | collective-permute-start | bytes 1572872 | tf_op jit(solution)/shard_map/ppermute | solution.py:988
  314.8 15.3 %collective-permute-start.42 = (bf16[256,1024]{1,0:T(8,128)(2,1)S(1)}, bf16[256,1024]{1,0:T(8,128)(2,1)S(1)}, u32[]{:S(2)}, u32[]{:S(2)}) collective-permute-start(bf16[256,1024]{1,0:T(8,128)(2,1)S(1)} %get-tuple-element.246), channel_id=1, source_target_pairs={{16,0},{24,8},{17,1},{25,9},{18,2},{26,10},{19,3},{27,11},{20,4},{... | collective-permute-start | bytes 1572872 | tf_op jit(solution)/shard_map/ppermute | solution.py:988
  319.0 13.5 %collective-permute-start.46 = (bf16[256,1024]{1,0:T(8,128)(2,1)S(1)}, bf16[256,1024]{1,0:T(8,128)(2,1)S(1)}, u32[]{:S(2)}, u32[]{:S(2)}) collective-permute-start(bf16[256,1024]{1,0:T(8,128)(2,1)S(1)} %collective-permute-done.45.refs_1_), channel_id=1, source_target_pairs={{0,8},{8,0},{16,24},{24,16},{1,9},{9,1},{17,25},{25,17},{2,10},{10... | collective-permute-start | bytes 1572872 | tf_op jit(solution)/shard_map/ppermute | solution.py:910
  336.5 9.8 %collective-permute-start.50 = (bf16[128,768]{1,0:T(8,128)(2,1)S(1)}, bf16[128,768]{1,0:T(8,128)(2,1)S(1)}, u32[]{:S(2)}, u32[]{:S(2)}) collective-permute-start(bf16[128,768]{1,0:T(8,128)(2,1)S(1)} %get-tuple-element.274), channel_id=1, source_target_pairs={{0,2},{1,3},{2,4},{3,5},{4,6},{5,7},{6,0},{7,1},{8,10},{9,11},{10,... | collective-permute-start | bytes 589832 | tf_op jit(solution)/shard_map/ppermute | solution.py:932
  337.3 15.2 %collective-permute-start.51 = (bf16[128,768]{1,0:T(8,128)(2,1)S(1)}, bf16[128,768]{1,0:T(8,128)(2,1)S(1)}, u32[]{:S(2)}, u32[]{:S(2)}) collective-permute-start(bf16[128,768]{1,0:T(8,128)(2,1)S(1)} %get-tuple-element.275), channel_id=1, source_target_pairs={{0,4},{1,5},{2,6},{3,7},{4,0},{5,1},{6,2},{7,3},{8,12},{9,13},{10,... | collective-permute-start | bytes 589832 | tf_op jit(solution)/shard_map/ppermute | solution.py:932
  338.6 13.9 %collective-permute-start.52 = (bf16[128,768]{1,0:T(8,128)(2,1)S(1)}, bf16[128,768]{1,0:T(8,128)(2,1)S(1)}, u32[]{:S(2)}, u32[]{:S(2)}) collective-permute-start(bf16[128,768]{1,0:T(8,128)(2,1)S(1)} %get-tuple-element.276), channel_id=1, source_target_pairs={{0,6},{1,7},{2,0},{3,1},{4,2},{5,3},{6,4},{7,5},{8,14},{9,15},{10,... | collective-permute-start | bytes 589832 | tf_op jit(solution)/shard_map/ppermute | solution.py:932
  342.3 3.7 collective-permute-start.49
  352.5 3.7 collective-permute-start.53
  356.3 5.9 %collective-permute-start.54 = (f32[4,1024]{1,0:T(4,128)S(1)}, f32[4,1024]{1,0:T(4,128)S(1)}, u32[]{:S(2)}, u32[]{:S(2)}) collective-permute-start(f32[4,1024]{1,0:T(4,128)S(1)} %add.86), channel_id=1, source_target_pairs={{0,2},{1,3},{2,0},{3,1},{4,6},{5,7},{6,4},{7,5},{8,10},{9,11},{10,... | collective-permute-start | bytes 49160 | tf_op jit(solution)/shard_map/ppermute | solution.py:1005
  362.2 5.6 %collective-permute-start.55 = (f32[4,1024]{1,0:T(4,128)S(1)}, f32[4,1024]{1,0:T(4,128)S(1)}, u32[]{:S(2)}, u32[]{:S(2)}) collective-permute-start(f32[4,1024]{1,0:T(4,128)S(1)} %add.87), channel_id=1, source_target_pairs={{0,4},{1,5},{2,6},{3,7},{4,0},{5,1},{6,2},{7,3},{8,12},{9,13},{10,... | collective-permute-start | bytes 49160 | tf_op jit(solution)/shard_map/ppermute | solution.py:1005
  (113 other events, 610.3 us)
Sparse Core Ops, SparseCore 0:
  10.8 68.9 all-gather.2
  82.5 72.0 all-gather.4
  208.8 86.3 reduce-scatter.4
  298.9 73.2 reduce-scatter.2

commit v3 on v2

--- a/solution.py
+++ b/solution.py
@@ -512,7 +512,19 @@
     )
 
 
-def dense_backward(idx, number, sums, x1, teacher, katt, slope, dense, name):
+def dense_part(idx, grads, up_t, name):
+    rows, features = grads.shape[0], up_t.shape[1]
+
+    def body(s, ga_ref, up_ref, part_ref):
+        @pl.loop(0, rows // TILE)
+        def _(i):
+            at = span(i * TILE)
+            part_ref[at, :] = dot_nn(ga_ref[at, :], up_ref[...]).astype(bf16)
+
+    return launch(body, idx, [grads, up_t], [shaped((rows, features), bf16)], name=name)[0]
+
+
+def dense_backward(idx, number, sums, x1, teacher, katt, slope, dense, name, with_part):
     features = x1.shape[1]
     up_t, both = dense
     hidden = up_t.shape[0]
@@ -522,7 +534,7 @@
         total = refs.pop()
         sum_refs = [refs.pop(0) for unused in range(len(sums))]
         x_ref, t_ref, v_ref, slope_ref, up_ref, d_ref = refs[:6]
-        gm_ref, ga_ref, loss_ref, part_ref = refs[6:]
+        gm_ref, ga_ref, loss_ref, *part_refs = refs[6:]
 
         @pl.loop(0, BLOCK // TILE)
         def _(i):
@@ -535,7 +547,8 @@
             gm_ref[at, :] = gm
             ga = (dot_nn(gm, d_ref[:, hidden:]) * slope_ref[at, :].astype(f32)).astype(bf16)
             ga_ref[at, :] = ga
-            part_ref[at, :] = dot_nn(ga, up_ref[...]).astype(bf16)
+            for part_ref in part_refs:
+                part_ref[at, :] = dot_nn(ga, up_ref[...]).astype(bf16)
 
     return launch(
         body,
@@ -545,8 +558,8 @@
             shaped((BLOCK, features), bf16),
             shaped((BLOCK, hidden), bf16),
             shaped((1, features), f32),
-            shaped((BLOCK, features), bf16),
-        ],
+        ]
+        + [shaped((BLOCK, features), bf16)] * with_part,
         scratch=[pltpu.VMEM((TILE, features), f32)],
         flops=4 * BLOCK * features * hidden,
         name=name,
@@ -1204,9 +1217,19 @@
     ready = teacher_all
     for b in range(nblocks):
         hides = [hiddens[end], state_found[0]] if b == 0 else [gms[b - 1]] + early_grads
-        gm, ga, loss, partial = dense_backward(
-            idx, b, dense_sums[b].result(*hides), x1s[b], ready, katt, slopes[b], (up_t, dense), f"back{b}"
+        gm, ga, loss, *partial = dense_backward(
+            idx,
+            b,
+            dense_sums[b].result(*hides),
+            x1s[b],
+            ready,
+            katt,
+            slopes[b],
+            (up_t, dense),
+            f"back{b}",
+            b < end,
         )
+        partial = partial[0] if b < end else None
         gms.append(gm)
         gas.append(ga)
         losses.append(loss)
@@ -1234,6 +1257,8 @@
     )
     filled = [dense_grads]
     ties = [dense_grads] + [back.far for back in second_back] if pairs else []
+    held = [back.chip for back in second_back] if pairs else []
+    partial = dense_part(after(idx, dense_grads, *held), gas[end], up_t, "back_part")
     second_back.append(RowSum(partial, f"back_sum{end}", ties=ties))
     dense_grads = lax.psum_scatter(dense_grads, "col", scatter_dimension=0, tiled=True)
 
@@ -1282,7 +1307,7 @@
                 idx,
                 [state_group(k) for k in range(3)] + [token_group(1), token_group(2)],
                 "late_grads",
-                weight=130,
+                weight=115,
                 vmem=12,
             )
             order = after(idx, late_grads)
@@ -1346,11 +1371,16 @@
 
     rest_grads.send(grad_next)
 
+    upper_grad, lower_grad = unpack_grads(
+        dense_grads, [hidden, hidden], [False, True], "unpack_dense"
+    )
+    order = after(idx, upper_grad)
+
     if pairs:
         own_rows = [first.chip for first in first_sums]
         arrived = [first.far for first in first_sums]
         input_grad, first_sum = input_rows(
-            idx, own_rows, arrived, gps, block_input[0], first_gain2, "input_rows"
+            order, own_rows, arrived, gps, block_input[0], first_gain2, "input_rows"
         )
         first_sum = first_sum[0]
     else:
@@ -1377,9 +1407,6 @@
     summed = all_sum(sums, *(rest_grads.far if lines else []))
     total_loss = jnp.sum(summed[0]) / (2.0 * total_tokens)
 
-    upper_grad, lower_grad = unpack_grads(
-        dense_grads, [hidden, hidden], [False, True], "unpack_dense"
-    )
     late = unpack_grads(late_grads, [width] * 5, [False] * 5, "unpack_late")
     rest = rest_grads.result([False, True, True])
 

time: 385 us -> 384 us (level)
  waiting for transfers between devices: 141 us -> 133 us
  local copies, waits for them, and re-layouts: 32 us -> 37 us
    ppermute x6, waiting for transfers between devices: 20.4 us -> 8.09 us  [along(): return lax.ppermute(v, 'col', moves)]
    ppermute x5, starting transfers between devices: 7.97 us -> 1.8 us  [all_sum(): x = x + lax.ppermute(x, axis, [(k, k ^ step) for k in range(size)])]
    ppermute x8, waiting for transfers between devices: 40.3 us -> 34.7 us  [__init__(): self.far = lax.ppermute(own, 'row', moves)]
    unnamed x202 -> x228, local copies, waits for them, and re-layouts: 31.5 us -> 36.5 us
    ppermute x5, waiting for transfers between devices: 4.48 us -> 9.01 us  [across(): return lax.ppermute(v, 'col', [(k, k ^ 1) for k in range(col_devices)])]
    pallas_call x45 -> x46, Pallas kernels: 117 us -> 119 us  [launch(): pl.pallas_call(body, in_specs=[pl.BlockSpec(memory_space=pltpu.SMEM)] + [...]
  transfers between devices with their start and end apart: 60 -> 60, of which waited for: 33 -> 28; matrix products, arithmetic and copies ran while one was open for 1% -> 1% of each run, Pallas kernels for 33% -> 33%
where the time goes in v3:
time: 384 us; the launch traced here: 380 us
  Pallas kernels  143 us (37%)
  waiting for transfers between devices  133 us (35%)
  starting transfers between devices  45.7 us (12%)
  local copies, waits for them, and re-layouts  37 us (10%)
  between operations  18 us (5%)
    pallas_call x46, Pallas kernels, launch(): pl.pallas_call(body, in_specs=[pl.BlockSpec(memory_space=pltpu.SMEM)] + [...  119 us
    unnamed x228, local copies, waits for them, and re-layouts  36.5 us
    ppermute x8, waiting for transfers between devices, __init__(): self.far = lax.ppermute(own, 'row', moves)  34.7 us
    all_gather x1, waiting for transfers between devices, per_device(): near = lax.all_gather(near, 'col', axis=0, tiled=True)  26.4 us
    all_gather x1, waiting for transfers between devices, per_device(): dense = lax.all_gather(after(far_weights, *held), 'col', axis=0, tiled=True)  17.3 us
    pallas_call x3, Pallas kernels, weight_grads(): pl.pallas_call(body, grid=(features // HALF,), in_specs=[pl.BlockSpec(mem...  16.6 us
    ppermute x5, waiting for transfers between devices, all_sum(): x = x + lax.ppermute(x, axis, [(k, k ^ step) for k in range(size)])  14.5 us
    ppermute x8, starting transfers between devices, __init__(): self.far = lax.ppermute(own, 'row', moves)  14.3 us
  transfers between devices with their start and end apart: 60, of which 28 were waited for; matrix products, arithmetic and copies ran while one was open for 1% of the time, Pallas kernels for 33%

profile of v3, /device:TPU:0, one launch (start us, length us, event | category | flops | bytes accessed | tf_op | source)
XLA Modules:
  0.0 380.5 jit_solution(5748610133356788455)
XLA Ops:
  7.3 2.3 pack_near.1
  9.8 2.9 pack_rest.1
  12.7 3.0 collective-permute-start.1
  17.3 2.6 collective-permute-start.9
  25.5 6.8 %collective-permute-done.9.refs_2_ = bf16[128,512]{1,0:T(8,128)(2,1)S(1)} collective-permute-done((bf16[128,512]{1,0:T(8,128)(2,1)S(1)}, bf16[128,512]{1,0:T(8,128)(2,1)S(1)}, u32[]{:S(2)}, u32[]{:S(2)}) %collective-permute-start.9) | collective-permute-done | bytes 131104 | tf_op jit(solution)/shard_map/ppermute | solution.py:945
  34.3 4.0 %collective-permute-done.13.refs_6_ = bf16[128,512]{1,0:T(8,128)(2,1)S(1)} collective-permute-done((bf16[128,512]{1,0:T(8,128)(2,1)S(1)}, bf16[128,512]{1,0:T(8,128)(2,1)S(1)}, u32[]{:S(2)}, u32[]{:S(2)}) %collective-permute-start.13) | collective-permute-done | bytes 131104 | tf_op jit(solution)/shard_map/ppermute | solution.py:948
  47.0 2.5 tokens.1
  52.1 26.4 %all-gather.3.cloned.1.call-done.w_ref.v_ref.refs_11_ = bf16[1024,1536]{1,0:T(8,128)(2,1)} async-done(((bf16[128,1536]{1,0:T(8,128)(2,1)}), bf16[1024,1536]{1,0:T(8,128)(2,1)}) %all-gather.3.cloned.1.call-update) | async-done | bytes 3145744 | tf_op jit(solution)/shard_map/all_gather | solution.py:1031
  86.5 3.4 token_proj.1
  89.9 3.0 token_attend0.1
  93.0 2.9 state_attend0.1
  97.7 7.0 %collective-permute-done.6.refs_2_ = bf16[512,256]{1,0:T(8,128)(2,1)S(1)} collective-permute-done((bf16[512,256]{1,0:T(8,128)(2,1)S(1)}, bf16[512,256]{1,0:T(8,128)(2,1)S(1)}, u32[]{:S(2)}, u32[]{:S(2)}) %collective-permute-start.6) | collective-permute-done | bytes 262176 | tf_op jit(solution)/shard_map/ppermute | solution.py:926
  106.2 5.5 %update0.1 = (f32[512,1024]{1,0:T(8,128)S(1)}, bf16[512,1024]{1,0:T(8,128)(2,1)S(1)}, bf16[512,768]{1,0:T(8,128)(2,1)S(1)}) custom-call(s32[5]{0:T(128)S(1)} %stack.40.s, bf16[512,256]{1,0:T(8,128)(2,1)S(1)} %get-tuple-element.160.refs_0_.refs_8_, bf16[512,256]{1,0:T(8,128)(2,1)S(1)} %collective-permute-done.5.refs_1_, ...), custom_call_target="tpu_custom_call" | custom-call | flops 234881024 | bytes 1024 | tf_op jit(solution)/shard_map/update0/pallas_call | solution.py:51
  112.8 3.7 token_attend1.1
  118.5 2.9 state_attend1.1
  121.5 3.5 collective-permute-done.20.refs_2_
  125.0 3.6 out0.1
  129.9 3.9 %out1.1 = (f32[512,1024]{1,0:T(8,128)S(1)}, bf16[512,1024]{1,0:T(8,128)(2,1)S(1)}) custom-call(s32[5]{0:T(128)S(1)} %stack.40.s, bf16[512,256]{1,0:T(8,128)(2,1)S(1)} %get-tuple-element.170.refs_0_.refs_6_, bf16[512,256]{1,0:T(8,128)(2,1)S(1)} %collective-permute-done.19.refs_1_, bf16[512,256]{1,0:T(8,128)(2,1)S(1)} %collective-permute-done.20.refs_2_, ...), custom_call_target="tpu_custom_call" | custom-call | flops 134217728 | bytes 1024 | tf_op jit(solution)/shard_map/out1/pallas_call | solution.py:51
  136.2 17.3 %all-gather.5.cloned.1.call-done.v_ref.up_ref.refs_8_ = bf16[1024,2048]{1,0:T(8,128)(2,1)} async-done(((bf16[128,2048]{1,0:T(8,128)(2,1)}), bf16[1024,2048]{1,0:T(8,128)(2,1)}) %all-gather.5.cloned.1.call-update) | async-done | bytes 4194320 | tf_op jit(solution)/shard_map/all_gather | solution.py:1053
  157.0 4.2 %dense0.1 = (bf16[512,1024]{1,0:T(8,128)(2,1)S(1)}, bf16[512,1024]{1,0:T(8,128)(2,1)S(1)}, bf16[512,1024]{1,0:T(8,128)(2,1)S(1)}) custom-call(s32[5]{0:T(128)S(1)} %stack.40.s, bf16[512,1024]{1,0:T(8,128)(2,1)S(1)} %copy-done.74, bf16[1024,2048]{1,0:T(8,128)(2,1)S(1)} %copy-done, bf16[1024,1024]{1,0:T(8,128)(2,1)S(1)} %down_turn.1.down_ref), custom_call_target="tpu_custom_call" | custom-call | flops 268435456 | bytes 1024 | tf_op jit(solution)/shard_map/dense0/pallas_call | solution.py:51
  166.4 4.4 %dense1.1 = (bf16[512,1024]{1,0:T(8,128)(2,1)S(1)}, bf16[512,1024]{1,0:T(8,128)(2,1)S(1)}, bf16[512,1024]{1,0:T(8,128)(2,1)S(1)}) custom-call(s32[5]{0:T(128)S(1)} %stack.40.s, bf16[512,1024]{1,0:T(8,128)(2,1)S(1)} %copy-done.72, bf16[1024,2048]{1,0:T(8,128)(2,1)S(1)} %copy-done.1, bf16[1024,1024]{1,0:T(8,128)(2,1)S(1)} %down_turn.1.down_ref), custom_call_target="tpu_custom_call" | custom-call | flops 268435456 | bytes 1024 | tf_op jit(solution)/shard_map/dense1/pallas_call | solution.py:51
  172.0 4.3 %state_back1.1 = (bf16[512,256]{1,0:T(8,128)(2,1)S(1)}, f32[512,256]{1,0:T(8,128)S(1)}, f32[512,256]{1,0:T(8,128)S(1)}, f32[512,256]{1,0:T(8,128)S(1)}, f32[512,256]{1,0:T(8,128)S(1)}) custom-call(s32[5]{0:T(128)S(1)} %stack.40.s, bf16[512,768]{1,0:T(8,128)(2,1)S(1)} %copy-done.14, bf16[1024,768]{1,0:T(8,128)(2,1)S(1)} %get-tuple-element.156.refs_0_.refs_1_, ...), custom_call_target="tpu_custom_call" | custom-call | flops 335544320 | bytes 1024 | tf_op jit(solution)/shard_map/state_back1/pallas_call | solution.py:51
  181.4 4.2 %back0.1 = (bf16[512,1024]{1,0:T(8,128)(2,1)S(1)}, bf16[512,1024]{1,0:T(8,128)(2,1)S(1)}, f32[1,1024]{1,0:T(1,128)S(1)}, bf16[512,1024]{1,0:T(8,128)(2,1)S(1)}) custom-call(s32[5]{0:T(128)S(1)} %stack.40.s, bf16[512,1024]{1,0:T(8,128)(2,1)S(1)} %get-tuple-element.178.refs_0_, bf16[256,1024]{1,0:T(8,128)(2,1)S(1)} %collective-permute-done.23.refs_1_, ...), custom_call_target="tpu_custom_call" | custom-call | flops 268435456 | bytes 1024 | tf_op jit(solution)/shard_map/back0/pallas_call | solution.py:51
  185.9 4.9 %dense_grads0.1.refs_4_ = bf16[1024,2048]{1,0:T(8,128)(2,1)} custom-call(s32[5]{0:T(128)S(1)} %stack.40.s, bf16[512,1024]{1,0:T(8,128)(2,1)S(1)} %copy-done.74, bf16[512,1024]{1,0:T(8,128)(2,1)S(1)} %get-tuple-element.196.refs_1_, bf16[512,1024]{1,0:T(8,128)(2,1)S(1)} %get-tuple-element.195.refs_2_.refs_3_, bf16[512,1024]{1,0:T(8,128)(2,1)S(1)} %get-tuple-element.174.refs_3_), custom_call_target="tpu_custom_call" | custom-call | flops 10737418240 | bytes 1024 | tf_op jit(solution)/shard_map/dense_grads0/pallas_call | solution.py:639
  190.9 3.4 collective-permute-done.26.refs_1_
  196.2 3.1 back1.1
  199.3 5.0 %dense_grads.1 = bf16[1024,2048]{1,0:T(8,128)(2,1)} custom-call(s32[5]{0:T(128)S(1)} %stack.40.s, bf16[512,1024]{1,0:T(8,128)(2,1)S(1)} %copy-done.72, bf16[512,1024]{1,0:T(8,128)(2,1)S(1)} %get-tuple-element.203.refs_1_.ga_ref, bf16[512,1024]{1,0:T(8,128)(2,1)S(1)} %get-tuple-element.204.refs_2_.refs_3_, bf16[512,1024]{1,0:T(8,128)(2,1)S(1)} %get-tuple-element.181.refs_3_, ...), custom_call_target="tpu_custom_call" | custom-call | flops 10737418240 | bytes 1024 | tf_op jit(solution)/shard_map/dense_grads/pallas_call | solution.py:639
  215.2 12.7 %collective-permute-done.29.refs_1_ = bf16[256,1024]{1,0:T(8,128)(2,1)S(1)} collective-permute-done((bf16[256,1024]{1,0:T(8,128)(2,1)S(1)}, bf16[256,1024]{1,0:T(8,128)(2,1)S(1)}, u32[]{:S(2)}, u32[]{:S(2)}) %collective-permute-start.29) | collective-permute-done | bytes 524320 | tf_op jit(solution)/shard_map/ppermute | solution.py:1001
  232.8 4.5 %token_back0.1 = (bf16[512,256]{1,0:T(8,128)(2,1)S(1)}, f32[512,256]{1,0:T(8,128)S(1)}, f32[512,256]{1,0:T(8,128)S(1)}, f32[512,256]{1,0:T(8,128)S(1)}, f32[512,256]{1,0:T(8,128)S(1)}) custom-call(s32[5]{0:T(128)S(1)} %stack.40.s, bf16[1024,768]{1,0:T(8,128)(2,1)S(1)} %get-tuple-element.156.refs_0_.refs_1_, bf16[512,768]{1,0:T(8,128)(2,1)S(1)} %copy-done.17, ...), custom_call_target="tpu_custom_call" | custom-call | flops 335544320 | bytes 1024 | tf_op jit(solution)/shard_map/token_back0/pallas_call | solution.py:51
  238.0 5.3 %collective-permute-done.32.refs_1_ = bf16[256,1024]{1,0:T(8,128)(2,1)S(1)} collective-permute-done((bf16[256,1024]{1,0:T(8,128)(2,1)S(1)}, bf16[256,1024]{1,0:T(8,128)(2,1)S(1)}, u32[]{:S(2)}, u32[]{:S(2)}) %collective-permute-start.32) | collective-permute-done | bytes 524320 | tf_op jit(solution)/shard_map/ppermute | solution.py:1001
  250.1 5.6 %token_back1.1 = (bf16[512,256]{1,0:T(8,128)(2,1)S(1)}, f32[512,256]{1,0:T(8,128)S(1)}, f32[512,256]{1,0:T(8,128)S(1)}, bf16[512,256]{1,0:T(8,128)(2,1)S(1)}, bf...) custom-call(s32[5]{0:T(128)S(1)} %stack.40.s, ...), custom_call_target="tpu_custom_call" | custom-call | flops 503316480 | bytes 1024 | tf_op jit(solution)/shard_map/token_back1/pallas_call | solution.py:51
  258.7 2.6 collective-permute-done.35.b_ref
  267.1 4.7 %update_last.1 = f32[512,1024]{1,0:T(8,128)} custom-call(s32[5]{0:T(128)S(1)} %stack.40.s, bf16[512,256]{1,0:T(8,128)(2,1)S(1)} %copy-done.53, bf16[512,256]{1,0:T(8,128)(2,1)S(1)} %collective-permute-done.37.refs_1_, bf16[512,256]{1,0:T(8,128)(2,1)S(1)} %collective-permute-done.34.refs_2_, bf16[512,256]{1,0:T(8,128)(2,1)S(1)} %collective-permute-done.38.refs_3_, ...), custom_call_target="tpu_custom_call" | custom-call | flops 134217728 | bytes 1024 | tf_op jit(solution)/shard_map/update_last/pallas_call | solution.py:51
  271.7 4.6 %collective-permute-done.36.refs_1_ = bf16[256,1024]{1,0:T(8,128)(2,1)S(1)} collective-permute-done((bf16[256,1024]{1,0:T(8,128)(2,1)S(1)}, bf16[256,1024]{1,0:T(8,128)(2,1)S(1)}, u32[]{:S(2)}, u32[]{:S(2)}) %collective-permute-start.36) | collective-permute-done | bytes 524320 | tf_op jit(solution)/shard_map/ppermute | solution.py:1001
  278.2 2.5 chain_back1.1
  282.1 4.4 %state_back0.1 = (bf16[512,256]{1,0:T(8,128)(2,1)S(1)}, bf16[512,256]{1,0:T(8,128)(2,1)S(1)}, bf16[512,256]{1,0:T(8,128)(2,1)S(1)}, bf16[512,256]{1,0:T(8,128)(2,1)S(1)}, bf16[512,256]{1,0:T(8,128)(2,1)S(1)}) custom-call(s32[5]{0:T(128)S(1)} %stack.40.s, bf16[512,768]{1,0:T(8,128)(2,1)S(1)} %copy-done.17, ...), custom_call_target="tpu_custom_call" | custom-call | flops 335544320 | bytes 1024 | tf_op jit(solution)/shard_map/state_back0/pallas_call | solution.py:51
  286.5 6.7 %late_grads.1 = bf16[1024,1280]{1,0:T(8,128)(2,1)} custom-call(s32[5]{0:T(128)S(1)} %stack.40.s, bf16[512,1024]{1,0:T(8,128)(2,1)S(1)} %copy-done.104, bf16[512,256]{1,0:T(8,128)(2,1)S(1)} %get-tuple-element.258.refs_1_.refs_0_, bf16[512,1024]{1,0:T(8,128)(2,1)S(1)} %copy-done.106, bf16[512,256]{1,0:T(8,128)(2,1)S(1)} %copy-done.86, ...), custom_call_target="tpu_custom_call" | custom-call | flops 38587596800 | bytes 1024 | tf_op jit(solution)/shard_map/late_grads/pallas_call | solution.py:639
  306.6 3.5 rest_grads.1
  310.7 8.4 %collective-permute-done.45.refs_1_ = bf16[256,1024]{1,0:T(8,128)(2,1)S(1)} collective-permute-done((bf16[256,1024]{1,0:T(8,128)(2,1)S(1)}, bf16[256,1024]{1,0:T(8,128)(2,1)S(1)}, u32[]{:S(2)}, u32[]{:S(2)}) %collective-permute-start.45) | collective-permute-done | bytes 524320 | tf_op jit(solution)/shard_map/ppermute | solution.py:1001
  320.9 4.2 %collective-permute-start.43 = (bf16[256,1024]{1,0:T(8,128)(2,1)}, bf16[256,1024]{1,0:T(8,128)(2,1)}, u32[]{:S(2)}, u32[]{:S(2)}) collective-permute-start(bf16[256,1024]{1,0:T(8,128)(2,1)} %get-tuple-element.250), channel_id=1, source_target_pairs={{0,16},{8,24},{1,17},{9,25},{2,18},{10,26},{3,19},{11,27},{4,20},{... | collective-permute-start | bytes 1572872 | tf_op jit(solution)/shard_map/ppermute | solution.py:1001
  328.8 3.2 chain_back0.1
  332.0 3.6 collective-permute-done.47.got_ref
  339.1 2.9 collective-permute-start.52
  347.2 3.2 input_rows.1
  351.7 3.7 collective-permute-done.49
  355.5 3.7 collective-permute-done.53
  360.4 3.5 collective-permute-done.54
  366.4 2.4 collective-permute-done.55
  (381 shorter events, 126.1 us)
Async XLA Ops:
  7.2 71.4 %all-gather.3.cloned.1.call-start = ((), (), s32[]{:S(2)}) async-start(), calls=%async_computation.2 | async-start | bytes 3538944 | tf_op jit(solution)/shard_map/all_gather | solution.py:1031
  9.7 143.7 %all-gather.5.cloned.1.call-start = ((), (), s32[]{:S(2)}) async-start(), calls=%async_computation.3 | async-start | bytes 4718592 | tf_op jit(solution)/shard_map/all_gather | solution.py:1053
  12.7 29.7 %collective-permute-start.1 = (bf16[512,1024]{1,0:T(8,128)(2,1)S(1)}, bf16[512,1024]{1,0:T(8,128)(2,1)}, u32[]{:S(2)}, u32[]{:S(2)}) collective-permute-start(bf16[512,1024]{1,0:T(8,128)(2,1)S(1)} %get-tuple-element.154.refs_0_), channel_id=1, source_target_pairs={{0,16},{8,24},{16,0},{24,8},{1,17},{9,25},{17,1},{25,9},{2,18},{10... | collective-permute-start | bytes 3145736 | tf_op jit(solution)/shard_map/ppermute | solution.py:926
  15.7 8.3 %collective-permute-start.8 = (bf16[128,512]{1,0:T(8,128)(2,1)S(1)}, bf16[128,512]{1,0:T(8,128)(2,1)S(1)}, u32[]{:S(2)}, u32[]{:S(2)}) collective-permute-start(bf16[128,512]{1,0:T(8,128)(2,1)S(1)} %get-tuple-element.162.refs_0_), channel_id=1, source_target_pairs={{0,2},{1,3},{2,4},{3,5},{4,6},{5,7},{6,0},{7,1},{8,10},{9,11},{10,... | collective-permute-start | bytes 393224 | tf_op jit(solution)/shard_map/ppermute | solution.py:945
  17.3 15.1 %collective-permute-start.9 = (bf16[128,512]{1,0:T(8,128)(2,1)S(1)}, bf16[128,512]{1,0:T(8,128)(2,1)S(1)}, u32[]{:S(2)}, u32[]{:S(2)}) collective-permute-start(bf16[128,512]{1,0:T(8,128)(2,1)S(1)} %get-tuple-element.162.refs_0_), channel_id=1, source_target_pairs={{0,4},{1,5},{2,6},{3,7},{4,0},{5,1},{6,2},{7,3},{8,12},{9,13},{10,... | collective-permute-start | bytes 393224 | tf_op jit(solution)/shard_map/ppermute | solution.py:945
  19.8 14.0 %collective-permute-start.10 = (bf16[128,512]{1,0:T(8,128)(2,1)S(1)}, bf16[128,512]{1,0:T(8,128)(2,1)S(1)}, u32[]{:S(2)}, u32[]{:S(2)}) collective-permute-start(bf16[128,512]{1,0:T(8,128)(2,1)S(1)} %get-tuple-element.162.refs_0_), channel_id=1, source_target_pairs={{0,6},{1,7},{2,0},{3,1},{4,2},{5,3},{6,4},{7,5},{8,14},{9,15},{10,... | collective-permute-start | bytes 393224 | tf_op jit(solution)/shard_map/ppermute | solution.py:945
  21.2 13.2 %collective-permute-start.11 = (bf16[128,512]{1,0:T(8,128)(2,1)S(1)}, bf16[128,512]{1,0:T(8,128)(2,1)S(1)}, u32[]{:S(2)}, u32[]{:S(2)}) collective-permute-start(bf16[128,512]{1,0:T(8,128)(2,1)S(1)} %get-tuple-element.162.refs_0_), channel_id=1, source_target_pairs={{0,1},{1,0},{2,3},{3,2},{4,5},{5,4},{6,7},{7,6},{8,9},{9,8},{10,11... | collective-permute-start | bytes 393224 | tf_op jit(solution)/shard_map/ppermute | solution.py:948
  24.0 10.4 %collective-permute-start.12 = (bf16[128,512]{1,0:T(8,128)(2,1)S(1)}, bf16[128,512]{1,0:T(8,128)(2,1)S(1)}, u32[]{:S(2)}, u32[]{:S(2)}) collective-permute-start(bf16[128,512]{1,0:T(8,128)(2,1)S(1)} %collective-permute-done.8.refs_1_), channel_id=1, source_target_pairs={{0,1},{1,0},{2,3},{3,2},{4,5},{5,4},{6,7},{7,6},{8,9},{9,8},{10,11... | collective-permute-start | bytes 393224 | tf_op jit(solution)/shard_map/ppermute | solution.py:948
  32.3 6.1 %collective-permute-start.13 = (bf16[128,512]{1,0:T(8,128)(2,1)S(1)}, bf16[128,512]{1,0:T(8,128)(2,1)S(1)}, u32[]{:S(2)}, u32[]{:S(2)}) collective-permute-start(bf16[128,512]{1,0:T(8,128)(2,1)S(1)} %collective-permute-done.9.refs_2_), channel_id=1, source_target_pairs={{0,1},{1,0},{2,3},{3,2},{4,5},{5,4},{6,7},{7,6},{8,9},{9,8},{10,11... | collective-permute-start | bytes 393224 | tf_op jit(solution)/shard_map/ppermute | solution.py:948
  33.9 5.9 %collective-permute-start.14 = (bf16[128,512]{1,0:T(8,128)(2,1)S(1)}, bf16[128,512]{1,0:T(8,128)(2,1)S(1)}, u32[]{:S(2)}, u32[]{:S(2)}) collective-permute-start(bf16[128,512]{1,0:T(8,128)(2,1)S(1)} %collective-permute-done.10.refs_3_), channel_id=1, source_target_pairs={{0,1},{1,0},{2,3},{3,2},{4,5},{5,4},{6,7},{7,6},{8,9},{9,8},{10,11... | collective-permute-start | bytes 393224 | tf_op jit(solution)/shard_map/ppermute | solution.py:948
  42.4 300.2 %reduce-scatter.3.cloned.1.call-start = ((), (), s32[]{:S(2)}) async-start(), calls=%async_computation.4 | async-start | bytes 4718592 | tf_op jit(solution)/shard_map/reduce_scatter | solution.py:1263
  42.6 4.4 %collective-permute-start.2 = (bf16[512,1024]{1,0:T(8,128)(2,1)}, bf16[512,1024]{1,0:T(8,128)(2,1)}, u32[]{:S(2)}, u32[]{:S(2)}) collective-permute-start(bf16[512,1024]{1,0:T(8,128)(2,1)} %collective-permute-done.1.refs_2_), channel_id=1, source_target_pairs={{0,8},{8,0},{16,24},{24,16},{1,9},{9,1},{17,25},{25,17},{2,10},{10... | collective-permute-start | bytes 3145736 | tf_op jit(solution)/shard_map/ppermute | solution.py:923
  43.2 49.7 %collective-permute-start.16 = (bf16[512,1024]{1,0:T(8,128)(2,1)}, bf16[512,1024]{1,0:T(8,128)(2,1)}, u32[]{:S(2)}, u32[]{:S(2)}) collective-permute-start(bf16[512,1024]{1,0:T(8,128)(2,1)} %mid_turn.1.refs_4_), channel_id=1, source_target_pairs={{0,16},{8,24},{16,0},{24,8},{1,17},{9,25},{17,1},{25,9},{2,18},{10... | collective-permute-start | bytes 3145736 | tf_op jit(solution)/shard_map/ppermute | solution.py:926
  45.3 60.9 %collective-permute-start.15 = (bf16[512,1024]{1,0:T(8,128)(2,1)}, bf16[512,1024]{1,0:T(8,128)(2,1)}, u32[]{:S(2)}, u32[]{:S(2)}) collective-permute-start(bf16[512,1024]{1,0:T(8,128)(2,1)} %mid_turn.1.refs_4_), channel_id=1, source_target_pairs={{0,8},{8,0},{16,24},{24,16},{1,9},{9,1},{17,25},{25,17},{2,10},{10... | collective-permute-start | bytes 3145736 | tf_op jit(solution)/shard_map/ppermute | solution.py:923
  92.9 13.3 %collective-permute-start.17 = (bf16[512,1024]{1,0:T(8,128)(2,1)}, bf16[512,1024]{1,0:T(8,128)(2,1)S(1)}, u32[]{:S(2)}, u32[]{:S(2)}) collective-permute-start(bf16[512,1024]{1,0:T(8,128)(2,1)} %collective-permute-done.16.refs_6_), channel_id=1, source_target_pairs={{0,8},{8,0},{16,24},{24,16},{1,9},{9,1},{17,25},{25,17},{2,10},{10... | collective-permute-start | bytes 3145736 | tf_op jit(solution)/shard_map/ppermute | solution.py:923
  95.9 8.8 %collective-permute-start.6 = (bf16[512,256]{1,0:T(8,128)(2,1)S(1)}, bf16[512,256]{1,0:T(8,128)(2,1)S(1)}, u32[]{:S(2)}, u32[]{:S(2)}) collective-permute-start(bf16[512,256]{1,0:T(8,128)(2,1)S(1)} %get-tuple-element.160.refs_0_.refs_8_), channel_id=1, source_target_pairs={{0,16},{8,24},{16,0},{24,8},{1,17},{9,25},{17,1},{25,9},{2,18},{10... | collective-permute-start | bytes 786440 | tf_op jit(solution)/shard_map/ppermute | solution.py:926
  97.5 8.7 %collective-permute-start.5 = (bf16[512,256]{1,0:T(8,128)(2,1)S(1)}, bf16[512,256]{1,0:T(8,128)(2,1)S(1)}, u32[]{:S(2)}, u32[]{:S(2)}) collective-permute-start(bf16[512,256]{1,0:T(8,128)(2,1)S(1)} %get-tuple-element.160.refs_0_.refs_8_), channel_id=1, source_target_pairs={{0,8},{8,0},{16,24},{24,16},{1,9},{9,1},{17,25},{25,17},{2,10},{10... | collective-permute-start | bytes 786440 | tf_op jit(solution)/shard_map/ppermute | solution.py:923
  104.7 13.9 %collective-permute-start.4 = (bf16[512,256]{1,0:T(8,128)(2,1)S(1)}, bf16[512,256]{1,0:T(8,128)(2,1)S(1)}, u32[]{:S(2)}, u32[]{:S(2)}) collective-permute-start(bf16[512,256]{1,0:T(8,128)(2,1)S(1)} %get-tuple-element.159.refs_0_.refs_4_), channel_id=1, source_target_pairs={{0,16},{8,24},{16,0},{24,8},{1,17},{9,25},{17,1},{25,9},{2,18},{10... | collective-permute-start | bytes 786440 | tf_op jit(solution)/shard_map/ppermute | solution.py:926
  116.5 8.5 %collective-permute-start.20 = (bf16[512,256]{1,0:T(8,128)(2,1)S(1)}, bf16[512,256]{1,0:T(8,128)(2,1)S(1)}, u32[]{:S(2)}, u32[]{:S(2)}) collective-permute-start(bf16[512,256]{1,0:T(8,128)(2,1)S(1)} %get-tuple-element.170.refs_0_.refs_6_), channel_id=1, source_target_pairs={{0,16},{8,24},{16,0},{24,8},{1,17},{9,25},{17,1},{25,9},{2,18},{10... | collective-permute-start | bytes 786440 | tf_op jit(solution)/shard_map/ppermute | solution.py:926
  118.0 6.9 %collective-permute-start.3 = (bf16[512,256]{1,0:T(8,128)(2,1)S(1)}, bf16[512,256]{1,0:T(8,128)(2,1)S(1)}, u32[]{:S(2)}, u32[]{:S(2)}) collective-permute-start(bf16[512,256]{1,0:T(8,128)(2,1)S(1)} %get-tuple-element.159.refs_0_.refs_4_), channel_id=1, source_target_pairs={{0,8},{8,0},{16,24},{24,16},{1,9},{9,1},{17,25},{25,17},{2,10},{10... | collective-permute-start | bytes 786440 | tf_op jit(solution)/shard_map/ppermute | solution.py:923
  118.0 11.8 %collective-permute-start.19 = (bf16[512,256]{1,0:T(8,128)(2,1)S(1)}, bf16[512,256]{1,0:T(8,128)(2,1)S(1)}, u32[]{:S(2)}, u32[]{:S(2)}) collective-permute-start(bf16[512,256]{1,0:T(8,128)(2,1)S(1)} %get-tuple-element.170.refs_0_.refs_6_), channel_id=1, source_target_pairs={{0,8},{8,0},{16,24},{24,16},{1,9},{9,1},{17,25},{25,17},{2,10},{10... | collective-permute-start | bytes 786440 | tf_op jit(solution)/shard_map/ppermute | solution.py:923
  118.5 6.4 %collective-permute-start.18 = (bf16[512,256]{1,0:T(8,128)(2,1)S(1)}, bf16[512,256]{1,0:T(8,128)(2,1)S(1)}, u32[]{:S(2)}, u32[]{:S(2)}) collective-permute-start(bf16[512,256]{1,0:T(8,128)(2,1)S(1)} %collective-permute-done.4.refs_2_), channel_id=1, source_target_pairs={{0,8},{8,0},{16,24},{24,16},{1,9},{9,1},{17,25},{25,17},{2,10},{10... | collective-permute-start | bytes 786440 | tf_op jit(solution)/shard_map/ppermute | solution.py:923
  125.0 4.9 %collective-permute-start.21 = (bf16[512,256]{1,0:T(8,128)(2,1)S(1)}, bf16[512,256]{1,0:T(8,128)(2,1)S(1)}, u32[]{:S(2)}, u32[]{:S(2)}) collective-permute-start(bf16[512,256]{1,0:T(8,128)(2,1)S(1)} %collective-permute-done.20.refs_2_), channel_id=1, source_target_pairs={{0,8},{8,0},{16,24},{24,16},{1,9},{9,1},{17,25},{25,17},{2,10},{10... | collective-permute-start | bytes 786440 | tf_op jit(solution)/shard_map/ppermute | solution.py:923
  164.9 14.0 %collective-permute-start.23 = (bf16[256,1024]{1,0:T(8,128)(2,1)S(1)}, bf16[256,1024]{1,0:T(8,128)(2,1)S(1)}, u32[]{:S(2)}, u32[]{:S(2)}) collective-permute-start(bf16[256,1024]{1,0:T(8,128)(2,1)S(1)} %get-tuple-element.179), channel_id=1, source_target_pairs={{0,16},{8,24},{16,0},{24,8},{1,17},{9,25},{17,1},{25,9},{2,18},{10... | collective-permute-start | bytes 1572872 | tf_op jit(solution)/shard_map/ppermute | solution.py:1001
  170.8 8.4 %collective-permute-start.25 = (bf16[512,1024]{1,0:T(8,128)(2,1)S(1)}, bf16[512,1024]{1,0:T(8,128)(2,1)S(1)}, u32[]{:S(2)}, u32[]{:S(2)}) collective-permute-start(bf16[512,1024]{1,0:T(8,128)(2,1)S(1)} %get-tuple-element.192.a_ref), channel_id=1, source_target_pairs={{0,8},{8,0},{16,24},{24,16},{1,9},{9,1},{17,25},{25,17},{2,10},{10... | collective-permute-start | bytes 3145736 | tf_op jit(solution)/shard_map/ppermute | solution.py:923
  180.1 14.1 %collective-permute-start.26 = (bf16[256,1024]{1,0:T(8,128)(2,1)S(1)}, bf16[256,1024]{1,0:T(8,128)(2,1)S(1)}, u32[]{:S(2)}, u32[]{:S(2)}) collective-permute-start(bf16[256,1024]{1,0:T(8,128)(2,1)S(1)} %get-tuple-element.194), channel_id=1, source_target_pairs={{0,16},{8,24},{16,0},{24,8},{1,17},{9,25},{17,1},{25,9},{2,18},{10... | collective-permute-start | bytes 1572872 | tf_op jit(solution)/shard_map/ppermute | solution.py:1001
  185.6 8.6 %collective-permute-start.28 = (bf16[512,1024]{1,0:T(8,128)(2,1)S(1)}, bf16[512,1024]{1,0:T(8,128)(2,1)S(1)}, u32[]{:S(2)}, u32[]{:S(2)}) collective-permute-start(bf16[512,1024]{1,0:T(8,128)(2,1)S(1)} %get-tuple-element.199.a_ref), channel_id=1, source_target_pairs={{0,8},{8,0},{16,24},{24,16},{1,9},{9,1},{17,25},{25,17},{2,10},{10... | collective-permute-start | bytes 3145736 | tf_op jit(solution)/shard_map/ppermute | solution.py:923
  206.2 164.5 %reduce-scatter.5.cloned.1.call-start = ((), (), s32[]{:S(2)}) async-start(), calls=%async_computation.5 | async-start | bytes 2949120 | tf_op jit(solution)/shard_map/reduce_scatter | solution.py:1319
  213.6 14.4 %collective-permute-start.31 = (bf16[512,1024]{1,0:T(8,128)(2,1)S(1)}, bf16[512,1024]{1,0:T(8,128)(2,1)S(1)}, u32[]{:S(2)}, u32[]{:S(2)}) collective-permute-start(bf16[512,1024]{1,0:T(8,128)(2,1)S(1)} %back_part.1.a_ref), channel_id=1, source_target_pairs={{0,8},{8,0},{16,24},{24,16},{1,9},{9,1},{17,25},{25,17},{2,10},{10... | collective-permute-start | bytes 3145736 | tf_op jit(solution)/shard_map/ppermute | solution.py:923
  213.7 14.2 %collective-permute-start.29 = (bf16[256,1024]{1,0:T(8,128)(2,1)S(1)}, bf16[256,1024]{1,0:T(8,128)(2,1)S(1)}, u32[]{:S(2)}, u32[]{:S(2)}) collective-permute-start(bf16[256,1024]{1,0:T(8,128)(2,1)S(1)} %get-tuple-element.210), channel_id=1, source_target_pairs={{0,16},{8,24},{16,0},{24,8},{1,17},{9,25},{17,1},{25,9},{2,18},{10... | collective-permute-start | bytes 1572872 | tf_op jit(solution)/shard_map/ppermute | solution.py:1001
  228.9 14.4 %collective-permute-start.32 = (bf16[256,1024]{1,0:T(8,128)(2,1)S(1)}, bf16[256,1024]{1,0:T(8,128)(2,1)S(1)}, u32[]{:S(2)}, u32[]{:S(2)}) collective-permute-start(bf16[256,1024]{1,0:T(8,128)(2,1)S(1)} %get-tuple-element.218), channel_id=1, source_target_pairs={{0,16},{8,24},{16,0},{24,8},{1,17},{9,25},{17,1},{25,9},{2,18},{10... | collective-permute-start | bytes 1572872 | tf_op jit(solution)/shard_map/ppermute | solution.py:1001
  248.6 8.3 %collective-permute-start.34 = (bf16[512,256]{1,0:T(8,128)(2,1)S(1)}, bf16[512,256]{1,0:T(8,128)(2,1)S(1)}, u32[]{:S(2)}, u32[]{:S(2)}) collective-permute-start(bf16[512,256]{1,0:T(8,128)(2,1)S(1)} %copy-done.53), channel_id=1, source_target_pairs={{0,16},{8,24},{16,0},{24,8},{1,17},{9,25},{17,1},{25,9},{2,18},{10... | collective-permute-start | bytes 786440 | tf_op jit(solution)/shard_map/ppermute | solution.py:926
  262.3 14.0 %collective-permute-start.36 = (bf16[256,1024]{1,0:T(8,128)(2,1)S(1)}, bf16[256,1024]{1,0:T(8,128)(2,1)S(1)}, u32[]{:S(2)}, u32[]{:S(2)}) collective-permute-start(bf16[256,1024]{1,0:T(8,128)(2,1)S(1)} %get-tuple-element.231), channel_id=1, source_target_pairs={{0,16},{8,24},{16,0},{24,8},{1,17},{9,25},{17,1},{25,9},{2,18},{10... | collective-permute-start | bytes 1572872 | tf_op jit(solution)/shard_map/ppermute | solution.py:1001
  263.8 3.2 collective-permute-start.37
  301.5 17.6 %collective-permute-start.41 = (bf16[512,1024]{1,0:T(8,128)(2,1)S(1)}, bf16[512,1024]{1,0:T(8,128)(2,1)S(1)}, u32[]{:S(2)}, u32[]{:S(2)}) collective-permute-start(bf16[512,1024]{1,0:T(8,128)(2,1)S(1)} %copy-done.31), channel_id=1, source_target_pairs={{0,8},{8,0},{16,24},{24,16},{1,9},{9,1},{17,25},{25,17},{2,10},{10... | collective-permute-start | bytes 3145736 | tf_op jit(solution)/shard_map/ppermute | solution.py:923
  303.7 21.4 %collective-permute-start.40 = (bf16[512,1024]{1,0:T(8,128)(2,1)S(1)}, bf16[512,1024]{1,0:T(8,128)(2,1)S(1)}, u32[]{:S(2)}, u32[]{:S(2)}) collective-permute-start(bf16[512,1024]{1,0:T(8,128)(2,1)S(1)} %first_back0.1.a_ref), channel_id=1, source_target_pairs={{0,8},{8,0},{16,24},{24,16},{1,9},{9,1},{17,25},{25,17},{2,10},{10... | collective-permute-start | bytes 3145736 | tf_op jit(solution)/shard_map/ppermute | solution.py:923
  305.0 14.1 %collective-permute-start.45 = (bf16[256,1024]{1,0:T(8,128)(2,1)S(1)}, bf16[256,1024]{1,0:T(8,128)(2,1)S(1)}, u32[]{:S(2)}, u32[]{:S(2)}) collective-permute-start(bf16[256,1024]{1,0:T(8,128)(2,1)S(1)} %get-tuple-element.265), channel_id=1, source_target_pairs={{0,16},{8,24},{16,0},{24,8},{1,17},{9,25},{17,1},{25,9},{2,18},{10... | collective-permute-start | bytes 1572872 | tf_op jit(solution)/shard_map/ppermute | solution.py:1001
  310.1 25.4 %collective-permute-start.47 = (bf16[512,768]{1,0:T(8,128)(2,1)S(1)}, bf16[512,768]{1,0:T(8,128)(2,1)S(1)}, u32[]{:S(2)}, u32[]{:S(2)}) collective-permute-start(bf16[512,768]{1,0:T(8,128)(2,1)S(1)} %get-tuple-element.274), channel_id=1, source_target_pairs={{0,1},{1,0},{2,3},{3,2},{4,5},{5,4},{6,7},{7,6},{8,9},{9,8},{10,11... | collective-permute-start | bytes 2359304 | tf_op jit(solution)/shard_map/ppermute | solution.py:948
  319.1 9.7 %collective-permute-start.46 = (bf16[256,1024]{1,0:T(8,128)(2,1)S(1)}, bf16[256,1024]{1,0:T(8,128)(2,1)S(1)}, u32[]{:S(2)}, u32[]{:S(2)}) collective-permute-start(bf16[256,1024]{1,0:T(8,128)(2,1)S(1)} %collective-permute-done.45.refs_1_), channel_id=1, source_target_pairs={{0,8},{8,0},{16,24},{24,16},{1,9},{9,1},{17,25},{25,17},{2,10},{10... | collective-permute-start | bytes 1572872 | tf_op jit(solution)/shard_map/ppermute | solution.py:923
  320.9 23.9 %collective-permute-start.43 = (bf16[256,1024]{1,0:T(8,128)(2,1)}, bf16[256,1024]{1,0:T(8,128)(2,1)}, u32[]{:S(2)}, u32[]{:S(2)}) collective-permute-start(bf16[256,1024]{1,0:T(8,128)(2,1)} %get-tuple-element.250), channel_id=1, source_target_pairs={{0,16},{8,24},{1,17},{9,25},{2,18},{10,26},{3,19},{11,27},{4,20},{... | collective-permute-start | bytes 1572872 | tf_op jit(solution)/shard_map/ppermute | solution.py:1001
  326.9 17.9 %collective-permute-start.42 = (bf16[256,1024]{1,0:T(8,128)(2,1)}, bf16[256,1024]{1,0:T(8,128)(2,1)}, u32[]{:S(2)}, u32[]{:S(2)}) collective-permute-start(bf16[256,1024]{1,0:T(8,128)(2,1)} %get-tuple-element.249), channel_id=1, source_target_pairs={{16,0},{24,8},{17,1},{25,9},{18,2},{26,10},{19,3},{27,11},{20,4},{... | collective-permute-start | bytes 1572872 | tf_op jit(solution)/shard_map/ppermute | solution.py:1001
  337.0 18.5 %collective-permute-start.50 = (bf16[128,768]{1,0:T(8,128)(2,1)}, bf16[128,768]{1,0:T(8,128)(2,1)}, u32[]{:S(2)}, u32[]{:S(2)}) collective-permute-start(bf16[128,768]{1,0:T(8,128)(2,1)} %get-tuple-element.277), channel_id=1, source_target_pairs={{0,2},{1,3},{2,4},{3,5},{4,6},{5,7},{6,0},{7,1},{8,10},{9,11},{10,... | collective-permute-start | bytes 589832 | tf_op jit(solution)/shard_map/ppermute | solution.py:945
  338.1 17.3 %collective-permute-start.51 = (bf16[128,768]{1,0:T(8,128)(2,1)}, bf16[128,768]{1,0:T(8,128)(2,1)}, u32[]{:S(2)}, u32[]{:S(2)}) collective-permute-start(bf16[128,768]{1,0:T(8,128)(2,1)} %get-tuple-element.278), channel_id=1, source_target_pairs={{0,4},{1,5},{2,6},{3,7},{4,0},{5,1},{6,2},{7,3},{8,12},{9,13},{10,... | collective-permute-start | bytes 589832 | tf_op jit(solution)/shard_map/ppermute | solution.py:945
  339.1 16.4 %collective-permute-start.52 = (bf16[128,768]{1,0:T(8,128)(2,1)}, bf16[128,768]{1,0:T(8,128)(2,1)}, u32[]{:S(2)}, u32[]{:S(2)}) collective-permute-start(bf16[128,768]{1,0:T(8,128)(2,1)} %get-tuple-element.279), channel_id=1, source_target_pairs={{0,6},{1,7},{2,0},{3,1},{4,2},{5,3},{6,4},{7,5},{8,14},{9,15},{10,... | collective-permute-start | bytes 589832 | tf_op jit(solution)/shard_map/ppermute | solution.py:945
  351.7 3.7 collective-permute-start.49
  355.4 3.8 collective-permute-start.53
  359.2 4.7 %collective-permute-start.54 = (f32[4,1024]{1,0:T(4,128)S(1)}, f32[4,1024]{1,0:T(4,128)S(1)}, u32[]{:S(2)}, u32[]{:S(2)}) collective-permute-start(f32[4,1024]{1,0:T(4,128)S(1)} %add.86), channel_id=1, source_target_pairs={{0,2},{1,3},{2,0},{3,1},{4,6},{5,7},{6,4},{7,5},{8,10},{9,11},{10,... | collective-permute-start | bytes 49160 | tf_op jit(solution)/shard_map/ppermute | solution.py:1018
  364.0 4.8 %collective-permute-start.55 = (f32[4,1024]{1,0:T(4,128)S(1)}, f32[4,1024]{1,0:T(4,128)S(1)}, u32[]{:S(2)}, u32[]{:S(2)}) collective-permute-start(f32[4,1024]{1,0:T(4,128)S(1)} %add.87), channel_id=1, source_target_pairs={{0,4},{1,5},{2,6},{3,7},{4,0},{5,1},{6,2},{7,3},{8,12},{9,13},{10,... | collective-permute-start | bytes 49160 | tf_op jit(solution)/shard_map/ppermute | solution.py:1018
  (126 other events, 697.3 us)
Sparse Core Ops, SparseCore 0:
  10.8 67.7 all-gather.2
  81.3 72.0 all-gather.4
  206.3 86.4 reduce-scatter.2
  296.8 71.9 reduce-scatter.4
